TPU v7x, 32 devices: a whole 2x2x4 slice. The times are simulated.
32 devices in a mesh: grp: 2 (over y), slab: 16 (over z, x, core).
Axes of the slice: x: 2, y: 2, z: 4, core: 2. Of those that a mesh axis runs over, the one named last changes fastest.
Arguments:
- velocity: float32 [16, 128, 512], P('grp', 'slab'), may hold values from -6 to 6
- rate: float32 [16, 128, 512], P('grp', 'slab'), may hold values from 0.02 to 0.16
- forcing: float32 [16, 128, 512], P('grp', 'slab'), may hold values from -3 to 3
- anchor_line: int32 [512], P(('grp', 'slab')), may hold values from 0 to 63
- anchor_z: int32 [512], P(('grp', 'slab')), may hold values from 0 to 384
- assign: int32 [512, 1], P(('grp', 'slab')), may hold values from 0 to 15; in each aligned block of 16 rows (0 to 15, 16 to 31, ...) at most 2 rows name the same one
- spectral: float32 [2048, 64], replicated, may hold values from -0.75 to 0.75
- dense: float32 [68, 64], replicated, may hold values from -4 to 4
- momentum: float32 [2048, 64], P(('grp', 'slab')), may hold values from -0.3125 to 0.3125
Outputs:
- field_out: float32 [16, 128, 512], P('grp', 'slab')
- trainer_loss: float32 [2, 16], P('grp', 'slab')
- spectral_new: float32 [2048, 64], replicated
- dense_new: float32 [68, 64], replicated
- momentum_new: float32 [2048, 64], P(('grp', 'slab'))
Inputs may be any that keep to these rules, and one draw needn't show every extreme that they name: `assign`: within the 16 lines of one device no trainer is named more than 2 times, and in some device's lines one trainer is named exactly 2 times.
All inputs are finite; a program needn't handle non-finite values.
Results may differ from a plain program's by a relative error of at most 0.0001.
Values sent between devices are 32-bit elements; how exact they have to be, the bound alone decides.
No kernel may reach another device: no remote copies, remote signals or barrier semaphores. Data moves between devices by JAX's collectives and lax.ppermute only.
A program may use at most 64 MiB of HBM per device.

v0:
```python
import jax
import jax.numpy as jnp
from jax import lax
from jax.sharding import PartitionSpec as P

STEPS = 2
SUB = 128
MODES = 16


decay_rate = 0.9
learn_rate = 0.5
dense_rate = 3.0


def extended(cells, sides, width):
    for axis, dim in sides:
        count = lax.axis_size(axis)
        ends = count - 1
        head = lax.slice_in_dim(cells, 0, width, axis=dim)
        tail = lax.slice_in_dim(cells, cells.shape[dim] - width, cells.shape[dim], axis=dim)
        cells = jnp.concatenate(
            [
                lax.ppermute(tail, axis, [(i, (i + 1) % count) for i in range(ends)]),
                cells,
                lax.ppermute(head, axis, [((i + 1) % count, i) for i in range(ends)]),
            ],
            axis=dim,
        )
    return cells


def tables():
    counts = jnp.arange(SUB, dtype=jnp.int32)
    waves = jnp.arange(MODES, dtype=jnp.int32)
    phase = counts[:, None] * waves[None, :] % SUB
    angle = phase.astype(jnp.float32) * (2.0 * jnp.pi / SUB)
    weight_k = jnp.where(waves == 0, 1.0, 2.0).astype(jnp.float32) / SUB
    return (jnp.cos(angle), jnp.sin(angle), weight_k)


def line_errors(spectral, dense, inputs, targets, valid):
    highest = lax.Precision.HIGHEST
    width = dense.shape[1]
    mixing = dense[:width]
    lift_gain, lift_bias, layer_bias, projection = (
        dense[width],
        dense[width + 1],
        dense[width + 2],
        dense[width + 3],
    )
    cosine, sine, weight_k = tables()
    hidden = inputs[:, None, :] * lift_gain[None, :, None] + lift_bias[None, :, None]
    real_in = jnp.einsum("bws,sk->bwk", hidden, cosine, precision=highest)
    imag_in = -jnp.einsum("bws,sk->bwk", hidden, sine, precision=highest)
    blocks = spectral.reshape(2, MODES, width, width)
    w_real, w_imag = (blocks[0], blocks[1])
    real_out = jnp.einsum("bwk,kwv->bvk", real_in, w_real, precision=highest) - jnp.einsum(
        "bwk,kwv->bvk", imag_in, w_imag, precision=highest
    )
    imag_out = jnp.einsum("bwk,kwv->bvk", real_in, w_imag, precision=highest) + jnp.einsum(
        "bwk,kwv->bvk", imag_in, w_real, precision=highest
    )
    spatial = jnp.einsum(
        "bvk,sk->bvs", real_out * weight_k, cosine, precision=highest
    ) - jnp.einsum("bvk,sk->bvs", imag_out * weight_k, sine, precision=highest)
    before = (
        spatial
        + jnp.einsum("bws,wv->bvs", hidden, mixing, precision=highest)
        + layer_bias[None, :, None]
    )
    after = jax.nn.gelu(before)
    output = jnp.einsum("bvs,v->bs", after, projection, precision=highest)
    return jnp.sum((output - targets) ** 2, axis=1) * valid


def gradients_of(spectral, dense, inputs, targets, valid, scale):

    def loss_fn(spec, dens):
        errors = line_errors(spec, dens, inputs, targets, valid)
        return (jnp.sum(errors) * scale, errors)

    value, pullback, errors = jax.vjp(loss_fn, spectral, dense, has_aux=True)
    grad_spec, grad_dense = pullback(jnp.ones((), jnp.float32))
    return (grad_spec, grad_dense, errors)


def local(velocity, rate, forcing, anchor_line, anchor_z, assign, spectral, dense, momentum):
    field_now = velocity
    previous = velocity
    change = velocity
    for number in range(STEPS):
        previous = field_now
        padded = extended(field_now, (("grp", 0), ("slab", 1)), 1)
        beside = padded[2:, 1:-1] + padded[:-2, 1:-1] + padded[1:-1, 2:] + padded[1:-1, :-2]
        beside = beside + jnp.roll(field_now, 1, 2) + jnp.roll(field_now, -1, 2)
        change = rate * (beside - 6.0 * field_now) + forcing
        field_now = field_now + change
    cells_x, cells_y, cells_z = velocity.shape
    line_count = anchor_line.shape[0]
    windows = jax.vmap(lambda row, start: lax.dynamic_slice_in_dim(row, start, SUB))
    inputs = windows(
        jnp.take(previous.reshape(cells_x * cells_y, cells_z), anchor_line, axis=0), anchor_z
    )
    targets = windows(
        jnp.take(change.reshape(cells_x * cells_y, cells_z), anchor_line, axis=0), anchor_z
    )
    n_slab = lax.axis_size("slab")
    devices = lax.axis_size("grp") * n_slab
    scale = 1.0 / (devices * line_count * SUB)
    dest = assign[:, 0]
    onehot = (dest[:, None] == jnp.arange(n_slab, dtype=jnp.int32)[None, :]).astype(jnp.int32)
    grad_spec, grad_dense, errors = gradients_of(
        spectral, dense, inputs, targets, jnp.ones((line_count,), jnp.float32), scale
    )
    partial_loss = jnp.dot(errors, onehot.astype(jnp.float32), precision=lax.Precision.HIGHEST) / (
        line_count * SUB
    )
    trainer_loss = lax.psum_scatter(partial_loss, "slab", scatter_dimension=0, tiled=True).reshape(
        1, 1
    )
    grad_rows = lax.psum_scatter(grad_spec, ("grp", "slab"), scatter_dimension=0, tiled=True)
    grad_dense = lax.psum(grad_dense, ("grp", "slab"))
    piece_rows = grad_rows.shape[0]
    position = lax.axis_index(("grp", "slab"))
    own_rows = lax.dynamic_slice_in_dim(spectral, position * piece_rows, piece_rows, 0)
    momentum_new = decay_rate * momentum + grad_rows
    updated_rows = own_rows - learn_rate * momentum_new
    spectral_new = lax.all_gather(updated_rows, ("grp", "slab"), axis=0, tiled=True)
    dense_new = dense - dense_rate * grad_dense
    return (field_now, trainer_loss, spectral_new, dense_new, momentum_new)


def solution(mesh):
    placed = (
        P("grp", "slab", None),
        P("grp", "slab", None),
        P("grp", "slab", None),
        P(("grp", "slab")),
        P(("grp", "slab")),
        P(("grp", "slab"), None),
        P(),
        P(),
        P(("grp", "slab"), None),
    )
    return jax.shard_map(
        local,
        mesh=mesh,
        in_specs=placed,
        out_specs=(P("grp", "slab", None), P("grp", "slab"), P(), P(), P(("grp", "slab"), None)),
        check_vma=False,
    )
```

profile of v0, /device:TPU:0, one launch (start us, length us, event | category | flops | bytes accessed | tf_op | source)
XLA Modules:
  0.0 314.7 jit_solution(17592519083051629129)
XLA Ops:
  8.0 1.3 collective-permute-start
  9.3 4.9 %collective-permute-start.1 = (f32[1,8,512]{2,1,0:T(8,128)S(1)}, f32[1,8,512]{2,1,0:T(8,128)S(1)}, u32[]{:S(2)}, u32[]{:S(2)}) collective-permute-start(f32[1,8,512]{2,1,0:T(8,128)S(1)} %get-tuple-element.86), channel_id=1, source_target_pairs={{0,16},{1,17},{2,18},{3,19},{4,20},{5,21},{6,22},{7,23},{8,24},{9,... | collective-permute-start | bytes 49160 | tf_op jit(solution)/shard_map/ppermute | solution.py:24
  17.7 1.3 collective-permute-start.2
  19.0 3.0 collective-permute-start.3
  24.0 2.3 collective-permute-start.5
  26.2 1.3 collective-permute-start.4
  27.6 4.2 %collective-permute-done.4 = f32[1,8,512]{2,1,0:T(8,128)S(1)} collective-permute-done((f32[1,8,512]{2,1,0:T(8,128)S(1)}, f32[1,8,512]{2,1,0:T(8,128)S(1)}, u32[]{:S(2)}, u32[]{:S(2)}) %collective-permute-start.4) | collective-permute-done | bytes 16416 | tf_op jit(solution)/shard_map/ppermute | solution.py:26
  31.9 1.3 collective-permute-start.6
  33.2 3.3 %collective-permute-start.7 = (f32[10,1,512]{2,1,0:T(1,128)S(1)}, f32[10,1,512]{2,1,0:T(1,128)S(1)}, u32[]{:S(2)}, u32[]{:S(2)}) collective-permute-start(f32[10,1,512]{2,1,0:T(1,128)S(1)} %get-tuple-element.72), channel_id=1, source_target_pairs={{0,1},{1,2},{2,3},{3,4},{4,5},{5,6},{6,7},{7,8},{8,9},{9,10},{10,1... | collective-permute-start | bytes 61448 | tf_op jit(solution)/shard_map/ppermute | solution.py:24
  38.8 32.3 %while.2 = (s32[]{:T(128)}, f32[16,512]{1,0:T(8,128)S(1)}, s32[16,2]{0,1:T(2,128)S(1)}, f32[16,128]{1,0:T(8,128)S(1)}, s32[]{:T(128)}, /*index=5*/s32[]{:T(128)}) while((s32[]{:T(128)}, f32[16,512]{1,0:T(8,128)S(1)}, s32[16,2]{0,1:T(2,128)S(1)}, f32[16,128]{1,0:T(8,128)S(1)}, s32[]{:T(128)}, /*index=5*/s32[]{:T(128)}) %tuple.61), condition=%wide.while_cond, body=%wide.while_body.sunk | while | flops 2 | bytes 2169 | solution.py:101
  39.4 1.3 dynamic-slice.15
  41.5 1.3 dynamic-slice.15
  43.5 1.3 dynamic-slice.15
  45.5 1.3 dynamic-slice.15
  47.5 1.3 dynamic-slice.15
  49.5 1.3 dynamic-slice.15
  51.5 1.3 dynamic-slice.15
  53.6 1.3 dynamic-slice.15
  55.6 1.3 dynamic-slice.15
  57.6 1.3 dynamic-slice.15
  59.6 1.3 dynamic-slice.15
  61.6 1.3 dynamic-slice.15
  63.7 1.3 dynamic-slice.15
  65.7 1.3 dynamic-slice.15
  67.7 1.3 dynamic-slice.15
  69.7 1.3 dynamic-slice.15
  71.1 1.4 convolution_negate_fusion
  72.5 1.4 fusion.38
  74.7 32.1 %while.3 = (s32[]{:T(128)}, f32[16,512]{1,0:T(8,128)S(1)}, s32[16,2]{0,1:T(2,128)S(1)}, f32[16,128]{1,0:T(8,128)S(1)}, s32[]{:T(128)}, /*index=5*/s32[]{:T(128)}) while((s32[]{:T(128)}, f32[16,512]{1,0:T(8,128)S(1)}, s32[16,2]{0,1:T(2,128)S(1)}, f32[16,128]{1,0:T(8,128)S(1)}, s32[]{:T(128)}, /*index=5*/s32[]{:T(128)}) %tuple.69), condition=%wide.while_cond.1, body=%wide.while_body.1.sunk | while | flops 2 | bytes 2169 | solution.py:101
  75.3 1.4 dynamic-slice.17
  77.3 1.4 dynamic-slice.17
  79.3 1.4 dynamic-slice.17
  81.2 1.4 dynamic-slice.17
  83.2 1.4 dynamic-slice.17
  85.2 1.4 dynamic-slice.17
  87.2 1.4 dynamic-slice.17
  89.2 1.4 dynamic-slice.17
  91.2 1.4 dynamic-slice.17
  93.2 1.4 dynamic-slice.17
  95.2 1.4 dynamic-slice.17
  97.2 1.4 dynamic-slice.17
  99.2 1.4 dynamic-slice.17
  101.2 1.4 dynamic-slice.17
  103.2 1.4 dynamic-slice.17
  105.2 1.4 dynamic-slice.17
  109.2 1.0 fusion.72
  110.2 1.0 fusion.35
  112.4 1.3 fusion.6
  113.8 1.4 fusion.186
  116.1 0.9 fusion.78
  117.0 1.0 fusion.82
  118.1 1.0 fusion.84
  121.1 1.0 fusion.1
  122.1 1.2 fusion
  123.4 1.1 pad_add_fusion
  126.2 35.7 %all-reduce.7 = f32[16]{0:T(128)S(1)} all-reduce(f32[16]{0:T(128)S(1)} %fusion.11), channel_id=2, replica_groups=mesh['grp'=2,'slab'=16] {'slab'}, use_global_device_ids=true, to_apply=%region_1.3.clone | all-reduce | flops 16 | bytes 128
  162.0 1.0 convolution_add_fusion.1
  163.0 1.1 fusion.171
  164.4 1.2 dynamic-slice.7
  167.0 37.0 %psum.7 = f32[68,64]{0,1:T(8,128)S(1)} all-reduce(f32[68,64]{0,1:T(8,128)S(1)} %pad_add_fusion.1), channel_id=1, replica_groups=mesh['grp'=2,'slab'=16] {'grp','slab'}, use_global_device_ids=true, to_apply=%region_6.8 | all-reduce | flops 4352 | bytes 34816 | tf_op jit(solution)/shard_map/psum | solution.py:123
  204.6 61.4 %reduce-scatter.2.cloned.1.call-done = f32[64,64]{1,0:T(8,128)} async-done(((f32[2048,64]{1,0:T(8,128)}), f32[64,64]{1,0:T(8,128)}) %reduce-scatter.2.cloned.1.call-update) | async-done | bytes 16400 | tf_op jit(solution)/shard_map/reduce_scatter | solution.py:122
  266.1 1.4 multiply_subtract_fusion.1
  267.5 39.3 %all_gather.3 = f32[2048,64]{1,0:T(8,128)S(1)} all-gather(f32[64,64]{1,0:T(8,128)S(1)} %get-tuple-element.61), channel_id=1, replica_groups=mesh['grp'=2,'slab'=16] {'grp','slab'}, dimensions={0}, use_global_device_ids=true | all-gather | bytes 540672 | tf_op jit(solution)/shard_map/all_gather | solution.py:129
  306.8 1.1 copy.72
  (176 shorter events, 40.4 us)
Async XLA Ops:
  7.2 9.2 %copy-start = (f32[8,8,512]{2,1,0:T(8,128)S(1)}, f32[8,8,512]{2,1,0:T(8,128)}, u32[]{:S(2)}) copy-start(f32[8,8,512]{2,1,0:T(8,128)} %param.11) | copy-start | bytes 393220
  7.2 10.2 %copy-start.2 = (f32[2048,64]{0,1:T(8,128)S(1)}, f32[2048,64]{0,1:T(8,128)}, u32[]{:S(2)}) copy-start(f32[2048,64]{0,1:T(8,128)} %param.17) | copy-start | bytes 1572868
  7.2 258.9 %reduce-scatter.2.cloned.1.call-start = ((), (), s32[]{:S(2)}) async-start(), calls=%async_computation.1 | async-start | bytes 1081344 | tf_op jit(solution)/shard_map/reduce_scatter | solution.py:122
  8.0 9.6 %collective-permute-start = (f32[1,8,512]{2,1,0:T(8,128)S(1)}, f32[1,8,512]{2,1,0:T(8,128)S(1)}, u32[]{:S(2)}, u32[]{:S(2)}) collective-permute-start(f32[1,8,512]{2,1,0:T(8,128)S(1)} %get-tuple-element.85), channel_id=1, source_target_pairs={{16,0},{17,1},{18,2},{19,3},{20,4},{21,5},{22,6},{23,7},{24,8},{25... | collective-permute-start | bytes 49160 | tf_op jit(solution)/shard_map/ppermute | solution.py:26
  9.3 8.3 %collective-permute-start.1 = (f32[1,8,512]{2,1,0:T(8,128)S(1)}, f32[1,8,512]{2,1,0:T(8,128)S(1)}, u32[]{:S(2)}, u32[]{:S(2)}) collective-permute-start(f32[1,8,512]{2,1,0:T(8,128)S(1)} %get-tuple-element.86), channel_id=1, source_target_pairs={{0,16},{1,17},{2,18},{3,19},{4,20},{5,21},{6,22},{7,23},{8,24},{9,... | collective-permute-start | bytes 49160 | tf_op jit(solution)/shard_map/ppermute | solution.py:24
  16.4 0.8 copy-start.1
  16.5 0.7 copy-start.6
  17.7 6.1 %collective-permute-start.2 = (f32[10,1,512]{2,1,0:T(1,128)S(1)}, f32[10,1,512]{2,1,0:T(1,128)S(1)}, u32[]{:S(2)}, u32[]{:S(2)}) collective-permute-start(f32[10,1,512]{2,1,0:T(1,128)S(1)} %get-tuple-element.73), channel_id=1, source_target_pairs={{1,0},{2,1},{3,2},{4,3},{5,4},{6,5},{7,6},{8,7},{9,8},{10,9},{11,1... | collective-permute-start | bytes 61448 | tf_op jit(solution)/shard_map/ppermute | solution.py:26
  19.0 4.8 %collective-permute-start.3 = (f32[10,1,512]{2,1,0:T(1,128)S(1)}, f32[10,1,512]{2,1,0:T(1,128)S(1)}, u32[]{:S(2)}, u32[]{:S(2)}) collective-permute-start(f32[10,1,512]{2,1,0:T(1,128)S(1)} %get-tuple-element.74), channel_id=1, source_target_pairs={{0,1},{1,2},{2,3},{3,4},{4,5},{5,6},{6,7},{7,8},{8,9},{9,10},{10,1... | collective-permute-start | bytes 61448 | tf_op jit(solution)/shard_map/ppermute | solution.py:24
  22.3 1.5 copy-start.3
  22.3 1.5 copy-start.4
  22.5 0.7 copy-start.8
  24.0 3.7 %collective-permute-start.5 = (f32[1,8,512]{2,1,0:T(8,128)S(1)}, f32[1,8,512]{2,1,0:T(8,128)S(1)}, u32[]{:S(2)}, u32[]{:S(2)}) collective-permute-start(f32[1,8,512]{2,1,0:T(8,128)S(1)} %get-tuple-element.75), channel_id=1, source_target_pairs={{0,16},{1,17},{2,18},{3,19},{4,20},{5,21},{6,22},{7,23},{8,24},{9,... | collective-permute-start | bytes 49160 | tf_op jit(solution)/shard_map/ppermute | solution.py:24
  26.2 5.6 %collective-permute-start.4 = (f32[1,8,512]{2,1,0:T(8,128)S(1)}, f32[1,8,512]{2,1,0:T(8,128)S(1)}, u32[]{:S(2)}, u32[]{:S(2)}) collective-permute-start(f32[1,8,512]{2,1,0:T(8,128)S(1)} %get-tuple-element.76), channel_id=1, source_target_pairs={{16,0},{17,1},{18,2},{19,3},{20,4},{21,5},{22,6},{23,7},{24,8},{25... | collective-permute-start | bytes 49160 | tf_op jit(solution)/shard_map/ppermute | solution.py:26
  31.9 5.3 %collective-permute-start.6 = (f32[10,1,512]{2,1,0:T(1,128)S(1)}, f32[10,1,512]{2,1,0:T(1,128)S(1)}, u32[]{:S(2)}, u32[]{:S(2)}) collective-permute-start(f32[10,1,512]{2,1,0:T(1,128)S(1)} %get-tuple-element.71), channel_id=1, source_target_pairs={{1,0},{2,1},{3,2},{4,3},{5,4},{6,5},{7,6},{8,7},{9,8},{10,9},{11,1... | collective-permute-start | bytes 61448 | tf_op jit(solution)/shard_map/ppermute | solution.py:26
  33.2 4.2 %collective-permute-start.7 = (f32[10,1,512]{2,1,0:T(1,128)S(1)}, f32[10,1,512]{2,1,0:T(1,128)S(1)}, u32[]{:S(2)}, u32[]{:S(2)}) collective-permute-start(f32[10,1,512]{2,1,0:T(1,128)S(1)} %get-tuple-element.72), channel_id=1, source_target_pairs={{0,1},{1,2},{2,3},{3,4},{4,5},{5,6},{6,7},{7,8},{8,9},{9,10},{10,1... | collective-permute-start | bytes 61448 | tf_op jit(solution)/shard_map/ppermute | solution.py:24
  124.5 0.7 copy-start.7
  204.0 62.1 %copy-start.5 = (f32[64,64]{1,0:T(8,128)S(1)}, f32[64,64]{1,0:T(8,128)}, u32[]{:S(2)}) copy-start(f32[64,64]{1,0:T(8,128)} %param.19) | copy-start | bytes 49156
Sparse Core Ops, SparseCore 0:
  124.6 141.4 reduce-scatter.1
where the time goes:
time: 316 us; the launch traced here: 315 us
  blocking collectives  112 us (35%)
  local copies, waits for them, and re-layouts  73.2 us (23%)
  waiting for transfers between devices  65.9 us (21%)
  matrix products  23.5 us (7%)
  starting transfers between devices  18.7 us (6%)
  between operations  14.5 us (5%)
  other arithmetic  6.66 us (2%)
    gather x128, local copies, waits for them, and re-layouts  64.1 us
    reduce_scatter x1, waiting for transfers between devices, local(): lax.psum_scatter(grad_spec, ('grp', 'slab'), scatter_dimension=0, tiled=T...  61.4 us
    all_gather x1, blocking collectives, local(): lax.all_gather(updated_rows, ('grp', 'slab'), axis=0, tiled=True)  39.3 us
    psum x1, blocking collectives, local(): grad_dense = lax.psum(grad_dense, ('grp', 'slab'))  37 us
    unnamed x1, blocking collectives  35.7 us
    ppermute x4, starting transfers between devices, extended(): lax.ppermute(tail, axis, [(i, (i + 1) % count) for i in range(ends)])  13.5 us
  transfers between devices with their start and end apart: 9, of which 3 were waited for; matrix products, arithmetic and copies ran while one was open for 4% of the time, Pallas kernels for 0%

commit v1 on v0

v1 whole, which is shorter than its diff:
```python
import functools
import math

import jax
import jax.numpy as jnp
import numpy as np
from jax import lax
from jax.experimental import pallas as pl
from jax.experimental.pallas import tpu as pltpu
from jax.sharding import PartitionSpec as P

STEPS = 2
SUB = 128
MODES = 16
LANES = 128
FEATURES = 2 * MODES + 8

decay_rate = 0.9
learn_rate = 0.5
dense_rate = 3.0

AXES = ("grp", "slab")
HIGHEST = lax.Precision.HIGHEST
NT = (((1,), (1,)), ((), ()))
VMEM = pl.BlockSpec(memory_space=pltpu.VMEM)
SMEM = pl.BlockSpec(memory_space=pltpu.SMEM)


def call(kernel, outs, scratch=(), ins=(), aliases=None, flops=1000000):
    outs = [jax.ShapeDtypeStruct(shape, dtype) for shape, dtype in outs]
    size = sum(math.prod(o.shape) * o.dtype.itemsize for o in outs)
    return pl.pallas_call(
        kernel,
        out_shape=outs,
        in_specs=list(ins),
        out_specs=[VMEM] * len(outs),
        scratch_shapes=list(scratch),
        input_output_aliases=aliases or {},
        compiler_params=pltpu.CompilerParams(vmem_limit_bytes=16 << 20),
        cost_estimate=pl.CostEstimate(flops=flops, bytes_accessed=2 * size, transcendentals=0),
    )


def tables():
    counts = np.arange(SUB)
    waves = np.arange(MODES)
    angle = (waves[:, None] * counts[None, :] % SUB) * (2.0 * np.pi / SUB)
    weight = np.where(waves == 0, 1.0, 2.0)[:, None] / SUB
    cosine, sine = np.cos(angle), np.sin(angle)
    return np.concatenate([cosine, sine, weight * cosine, weight * sine]).astype(np.float32)


def put_plane(ref, row, plane):
    for q in range(plane.shape[1] // LANES):
        ref[row + 8 * q : row + 8 * q + 8, :] = plane[:, q * LANES : (q + 1) * LANES]


def get_plane(ref, row, chunks):
    return jnp.concatenate([ref[row + 8 * q : row + 8 * q + 8, :] for q in range(chunks)], axis=1)


def pack_rows(block):
    half = block.shape[0] // 2
    return jnp.concatenate([block[:half], block[half:]], axis=1)


def edge_kernel(side, with_momentum, v_ref, rate_ref, forcing_ref, momentum_ref, out_ref):
    last = v_ref.shape[0] - 1
    chunks = v_ref.shape[2] // LANES
    high = (lax.axis_index("grp") == 0) if side is None else side
    edge = jnp.where(high, last, 0)
    second = jnp.where(high, last - 1, 1)
    planes = (v_ref[edge], v_ref[second], rate_ref[edge], forcing_ref[edge])
    for number, plane in enumerate(planes):
        put_plane(out_ref, number * 8 * chunks, plane)
    if with_momentum:
        packed = pack_rows(momentum_ref[...])
        start = 4 * 8 * chunks
        out_ref[start : start + packed.shape[0], :] = packed


def grp_halo(two_sided, ref_low, ref_high, layer, chunks):
    rows = 8 * chunks * layer
    if two_sided:
        return get_plane(ref_low, rows, chunks), get_plane(ref_high, rows, chunks)
    plane = get_plane(ref_low, rows, chunks)
    first = lax.axis_index("grp") == 0
    return jnp.where(first, 0.0, plane), jnp.where(first, plane, 0.0)


def side_kernel(two_sided, packed_rows, v_ref, rate_ref, forcing_ref, low_ref, high_ref, own_ref, *outs):
    a_ref, b_ref = outs[:2]
    last = v_ref.shape[1] - 1
    chunks = v_ref.shape[2] // LANES
    even = lax.rem(lax.axis_index("slab"), 2) == 0
    columns = ((v_ref, 0), (v_ref, 1), (rate_ref, 0), (forcing_ref, 0))
    for number, (ref, offset) in enumerate(columns):
        left, right = ref[:, offset, :], ref[:, last - offset, :]
        put_plane(a_ref, number * 8 * chunks, jnp.where(even, right, left))
        put_plane(b_ref, number * 8 * chunks, jnp.where(even, left, right))
    low, high = grp_halo(two_sided, low_ref, high_ref, 0, chunks)
    start = 4 * 8 * chunks
    for number, plane in enumerate((low, high)):
        left, right = plane[0:1], plane[last : last + 1]
        to_a, to_b = jnp.where(even, right, left), jnp.where(even, left, right)
        for q in range(chunks):
            row = start + number * chunks + q
            a_ref[row : row + 1, :] = to_a[:, q * LANES : (q + 1) * LANES]
            b_ref[row : row + 1, :] = to_b[:, q * LANES : (q + 1) * LANES]
    if packed_rows:
        outs[2][0:packed_rows, :] = own_ref[start : start + packed_rows, :]
        outs[2][packed_rows : 2 * packed_rows, :] = low_ref[start : start + packed_rows, :]


def feature_kernel(width, spectral_ref, dense_ref, map_ref, gain_ref, bias_ref, projection_ref, square, rows):
    square[...] = jnp.zeros_like(square)
    square[0 : dense_ref.shape[0], 0:width] = dense_ref[...]
    turned = square[...].T
    gain = jnp.broadcast_to(turned[0:width, width : width + 1], (width, LANES))
    bias = jnp.broadcast_to(turned[0:width, width + 1 : width + 2], (width, LANES))
    gain_ref[...] = gain
    bias_ref[...] = bias
    projection_ref[...] = jnp.broadcast_to(turned[0:width, width + 3 : width + 4], (width, LANES))
    gain, bias = gain[:, :width], bias[:, :width]
    rows[...] = jnp.zeros_like(rows)
    for block in range(2 * MODES):
        weights = spectral_ref[block * width : (block + 1) * width, :]
        rows[block : block + 1, 0:width] = jnp.sum(gain * weights, axis=0, keepdims=True)
    mixing = dense_ref[0:width, :]
    rows[2 * MODES : 2 * MODES + 1, 0:width] = jnp.sum(gain * mixing, axis=0, keepdims=True)
    rows[2 * MODES + 1 : 2 * MODES + 2, 0:width] = (
        jnp.sum(bias * (mixing + spectral_ref[0:width, :]), axis=0, keepdims=True)
        + dense_ref[width + 2 : width + 3, :]
    )
    full = rows[0:FEATURES, :]
    coarse = full.astype(jnp.bfloat16).astype(jnp.float32)
    rows[0:FEATURES, :] = coarse
    rows[FEATURES : 2 * FEATURES, :] = coarse
    rows[2 * FEATURES : 3 * FEATURES, :] = full - coarse
    map_ref[...] = rows[...].T[0:width, :].astype(jnp.bfloat16)


def step_kernel(
    two_sided, width, pay_rows, scale, v_ref, rate_ref, forcing_ref, low_ref, high_ref, a_ref, b_ref,
    line_ref, start_ref, assign_ref, map_ref, projection_ref, table_ref,
    field_ref, pay_ref, previous, change, inputs_ref, targets_ref, feature_ref, slope_ref,
):
    cells_x, cells_y, cells_z = v_ref.shape
    chunks = cells_z // LANES
    even = lax.rem(lax.axis_index("slab"), 2) == 0

    def grp_layer(layer):
        return grp_halo(two_sided, low_ref, high_ref, layer, chunks)

    def slab_layer(layer):
        from_a = get_plane(a_ref, 8 * chunks * layer, chunks)
        from_b = get_plane(b_ref, 8 * chunks * layer, chunks)
        return jnp.where(even, from_b, from_a), jnp.where(even, from_a, from_b)

    def corner(number):
        start = 4 * 8 * chunks + number * chunks
        from_a = jnp.concatenate([a_ref[start + q : start + q + 1, :] for q in range(chunks)], axis=1)
        from_b = jnp.concatenate([b_ref[start + q : start + q + 1, :] for q in range(chunks)], axis=1)
        return jnp.where(even, from_b, from_a), jnp.where(even, from_a, from_b)

    sublane = lax.broadcasted_iota(jnp.int32, (8, cells_z), 0)

    def shifted(plane, before, after):
        up = jnp.where(sublane == 7, after, pltpu.roll(plane, 7, 0))
        down = jnp.where(sublane == 0, before, pltpu.roll(plane, 1, 0))
        return up, down

    def tendency(plane, above, below, up, down, rate, forcing):
        beside = above + below + up + down
        beside = beside + pltpu.roll(plane, 1, 1) + pltpu.roll(plane, cells_z - 1, 1)
        return rate * (beside - 6.0 * plane) + forcing

    low1, high1 = grp_layer(0)
    low2, high2 = grp_layer(1)
    low_rate, high_rate = grp_layer(2)
    low_force, high_force = grp_layer(3)
    left1, right1 = slab_layer(0)
    left2, right2 = slab_layer(1)
    left_rate, right_rate = slab_layer(2)
    left_force, right_force = slab_layer(3)
    low_left, low_right = corner(0)
    high_left, high_right = corner(1)

    planes = [low2, low1] + [v_ref[i] for i in range(cells_x)] + [high1, high2]
    rates = [low_rate] + [rate_ref[i] for i in range(cells_x)] + [high_rate]
    forces = [low_force] + [forcing_ref[i] for i in range(cells_x)] + [high_force]
    lefts = [low_left] + [left1[i : i + 1] for i in range(cells_x)] + [high_left]
    rights = [low_right] + [right1[i : i + 1] for i in range(cells_x)] + [high_right]
    stepped = []
    for i in range(cells_x + 2):
        plane = planes[i + 1]
        up, down = shifted(plane, lefts[i], rights[i])
        stepped.append(plane + tendency(plane, planes[i + 2], planes[i], up, down, rates[i], forces[i]))

    def column_step(near, far, inner, rate, forcing, low, high):
        above, below = shifted(near, low, high)
        return near + tendency(near, above, below, inner, far, rate, forcing)

    left_inner = v_ref[:, 0, :]
    right_inner = v_ref[:, cells_y - 1, :]
    left_new = column_step(left1, left2, left_inner, left_rate, left_force, low_left, high_left)
    right_new = column_step(right1, right2, right_inner, right_rate, right_force, low_right, high_right)
    for i in range(cells_x):
        plane = stepped[i + 1]
        up, down = shifted(plane, left_new[i : i + 1], right_new[i : i + 1])
        moved = tendency(plane, stepped[i + 2], stepped[i], up, down, rate_ref[i], forcing_ref[i])
        field_ref[i] = plane + moved
        previous[8 * i : 8 * i + 8, 0:cells_z] = plane
        change[8 * i : 8 * i + 8, 0:cells_z] = moved
    count = line_ref.shape[0]
    previous[:, cells_z : cells_z + LANES] = jnp.zeros((8 * cells_x, LANES), jnp.float32)
    change[:, cells_z : cells_z + LANES] = jnp.zeros((8 * cells_x, LANES), jnp.float32)
    for t in range(count):
        line, start = line_ref[t], start_ref[t]
        base = pl.multiple_of((start // LANES) * LANES, LANES)
        turn = lax.rem(2 * LANES - lax.rem(start, LANES), 2 * LANES)
        row = previous[pl.ds(line, 1), pl.ds(base, 2 * LANES)]
        inputs_ref[t : t + 1, :] = pltpu.roll(row, turn, 1)[:, :SUB]
        row = change[pl.ds(line, 1), pl.ds(base, 2 * LANES)]
        targets_ref[t : t + 1, :] = pltpu.roll(row, turn, 1)[:, :SUB]

    table = table_ref[...]
    cos_w, sin_w = table[2 * MODES : 3 * MODES], table[3 * MODES :]
    inputs = inputs_ref[...]
    waves = lax.dot_general(
        table[: 2 * MODES], inputs, NT, precision=HIGHEST, preferred_element_type=jnp.float32
    )
    tail = lax.broadcasted_iota(jnp.int32, (8, SUB), 0)
    projection = projection_ref[...]
    channel_map = map_ref[...]
    held = jnp.zeros((width, SUB), jnp.float32)
    lane = lax.broadcasted_iota(jnp.int32, (1, LANES), 1)
    losses = jnp.zeros((1, LANES), jnp.float32)
    root = math.sqrt(2.0 / math.pi)
    for t in range(count):
        real, imag = waves[:MODES, t : t + 1], waves[MODES:, t : t + 1]
        line = inputs_ref[t : t + 1, :]
        rest = jnp.where(tail == 0, line, jnp.where(tail == 1, 1.0, 0.0))
        feature = jnp.concatenate([real * cos_w + imag * sin_w, imag * cos_w - real * sin_w, rest], axis=0)
        coarse = feature.astype(jnp.bfloat16).astype(jnp.float32)
        fine = feature - coarse
        zeros = jnp.zeros((LANES - 3 * FEATURES, SUB), jnp.float32)
        stack = jnp.concatenate([coarse, fine, coarse, zeros], axis=0).astype(jnp.bfloat16)
        feature_ref[:, t * SUB : (t + 1) * SUB] = stack
        before = jnp.dot(channel_map, stack, preferred_element_type=jnp.float32)
        square = before * before
        bend = jnp.tanh(root * (before + 0.044715 * (before * square)))
        half = 0.5 * (1.0 + bend)
        after = before * half
        slope = half + (0.5 * root) * before * (1.0 - bend * bend) * (1.0 + (3 * 0.044715) * square)
        output = jnp.sum(after * projection, axis=0, keepdims=True)
        differ = output - targets_ref[t : t + 1, :]
        error = jnp.sum(differ * differ, axis=1, keepdims=True)
        losses = losses + jnp.where(lane == assign_ref[t], error, 0.0)
        pull = (2.0 * scale) * differ
        held = held + after * pull
        slope = slope * projection * pull
        coarse = slope.astype(jnp.bfloat16).astype(jnp.float32)
        slope_ref[0:width, t * SUB : (t + 1) * SUB] = coarse.astype(jnp.bfloat16)
        slope_ref[width : 2 * width, t * SUB : (t + 1) * SUB] = (slope - coarse).astype(jnp.bfloat16)
    pairs = lax.dot_general(
        feature_ref[...], slope_ref[...], NT, preferred_element_type=jnp.float32
    )
    total = pairs[0:FEATURES, 0:width] + pairs[FEATURES : 2 * FEATURES, 0:width] + pairs[0:FEATURES, width:]
    pay_ref[...] = jnp.zeros_like(pay_ref)
    pay_ref[0:MODES, :] = jnp.concatenate([total[0:MODES], total[MODES : 2 * MODES]], axis=1)
    row = 2 * MODES
    pay_ref[MODES : MODES + 1, :] = jnp.concatenate([total[row : row + 1], total[row + 1 : row + 2]], axis=1)
    ones = jnp.ones((8, SUB), jnp.float32)
    summed = lax.dot_general(ones, held, NT, precision=HIGHEST, preferred_element_type=jnp.float32)
    pay_ref[MODES + 1 : MODES + 2, 0:width] = summed[0:1]
    pay_ref[pl.ds(MODES + 2 + lax.axis_index("grp"), 1), :] = losses


def base_kernel(masks, width, spectral_ref, mine_ref, other_ref, out_ref):
    here = lax.axis_index("grp") * lax.axis_size("slab") + lax.axis_index("slab")
    rows = width // 2
    held = mine_ref.shape[0] // rows
    for number in range(2 * held):
        source = here
        for bit, mask in enumerate(masks):
            if number >> bit & 1:
                source = source ^ mask
        ref, place = (mine_ref, number) if number < held else (other_ref, number - held)
        for part in range(2):
            start = pl.multiple_of(source * width + part * rows, rows)
            moved = ref[place * rows : (place + 1) * rows, part * width : (part + 1) * width]
            out_ref[pl.ds(start, rows), :] = spectral_ref[pl.ds(start, rows), :] - (learn_rate * decay_rate) * moved


def update_kernel(
    width, lines, pay_ref, spectral_ref, base_ref, dense_ref, momentum_ref, gain_ref, bias_ref,
    spectral_out, dense_out, momentum_out, loss_out, row_ref,
):
    first, second = lax.axis_index("grp"), lax.axis_index("slab")
    here = first * lax.axis_size("slab") + second
    gain, bias = gain_ref[:, 0:width], bias_ref[:, 0:width]
    row_ref[0:MODES, :] = pay_ref[0:MODES, 0:width]
    row_ref[MODES : 2 * MODES, :] = pay_ref[0:MODES, width : 2 * width]
    slopes = pay_ref[MODES : MODES + 2, :]
    by_input, by_one = slopes[0:1, 0:width], slopes[0:1, width : 2 * width]
    offset = bias * by_one
    gathered = dense_ref[0:width, :] * by_input
    for block in range(2 * MODES):
        span = slice(block * width, (block + 1) * width)
        row = row_ref[block : block + 1, :]
        gradient = gain * row
        if block == 0:
            gradient = gradient + offset
        spectral_out[span, :] = base_ref[span, :] - learn_rate * gradient
        gathered = gathered + spectral_ref[span, :] * row
    constant = (dense_ref[0:width, :] + spectral_ref[0:width, :]) * by_one
    ones = jnp.ones((8, width), jnp.float32)
    gain_row = lax.dot_general(ones, gathered, NT, precision=HIGHEST, preferred_element_type=jnp.float32)
    bias_row = lax.dot_general(ones, constant, NT, precision=HIGHEST, preferred_element_type=jnp.float32)
    dense_out[0:width, :] = dense_ref[0:width, :] - dense_rate * (gain * by_input + offset)
    changes = (gain_row[0:1], bias_row[0:1], by_one, slopes[1:2, 0:width])
    for number, gradient in enumerate(changes):
        at = slice(width + number, width + number + 1)
        dense_out[at, :] = dense_ref[at, :] - dense_rate * gradient
    piece = momentum_ref.shape[0]
    block = here * piece // width
    inside = 0 if piece == width else pl.multiple_of(lax.rem(here * piece, width), piece)
    at = pl.ds(inside, piece)
    gradient = gain_ref[at, 0:width] * row_ref[pl.ds(block, 1), :]
    gradient = gradient + jnp.where(block == 0, bias_ref[at, 0:width] * by_one, 0.0)
    momentum_out[...] = decay_rate * momentum_ref[...] + gradient
    sums = pay_ref[pl.ds(MODES + 2 + first, 1), :]
    lane = lax.broadcasted_iota(jnp.int32, (1, LANES), 1)
    own = jnp.sum(jnp.where(lane == second, sums, 0.0), axis=1, keepdims=True)
    loss_out[...] = own * (1.0 / (lines * SUB))


def hop_masks(n_grp, n_slab):
    masks, bit = [], 0
    while 1 << bit < n_slab:
        masks.append(3 << (bit - 1) if bit > 2 and bit % 2 else 1 << bit)
        bit += 1
    bit = 1
    while bit < n_grp:
        masks.append(bit * n_slab)
        bit *= 2
    return masks


def swap(array, mask, count):
    return lax.ppermute(array, AXES, [(i, i ^ mask) for i in range(count)])


def local(velocity, rate, forcing, anchor_line, anchor_z, assign, spectral, dense, momentum):
    n_grp, n_slab = lax.axis_size("grp"), lax.axis_size("slab")
    devices = n_grp * n_slab
    width = dense.shape[1]
    lines = anchor_line.shape[0]
    cells_x, cells_y, cells_z = velocity.shape
    chunks = cells_z // LANES
    halo_rows = 4 * 8 * chunks
    piece = momentum.shape[0]
    packed = piece // 2
    f32 = jnp.float32
    joined = n_grp == 2 and piece == width and devices & (devices - 1) == 0
    two_sided = n_grp != 2
    table = jnp.asarray(tables())

    def edge(side):
        rows = halo_rows + (packed if joined else 0)
        return call(
            functools.partial(edge_kernel, side, joined), [((rows, LANES), f32)], ins=[VMEM] * 4
        )(velocity, rate, forcing, momentum)[0]

    if two_sided:
        low = lax.ppermute(edge(True), "grp", [(i, i + 1) for i in range(n_grp - 1)])
        high = lax.ppermute(edge(False), "grp", [(i + 1, i) for i in range(n_grp - 1)])
        own = low
    else:
        own = edge(None)
        low = high = lax.ppermute(own, "grp", [(0, 1), (1, 0)])
    message = (halo_rows + 2 * chunks, LANES)
    outs = [(message, f32), (message, f32)] + ([((2 * packed, LANES), f32)] if joined else [])
    to_a, to_b, *gathered = call(
        functools.partial(side_kernel, two_sided, packed if joined else 0), outs, ins=[VMEM] * 6
    )(velocity, rate, forcing, low, high, own)
    pairs = [(i, i ^ 1) for i in range(n_slab)]
    odd = [(i, i + 1) for i in range(1, n_slab - 1, 2)]
    from_b = lax.ppermute(to_b, "slab", odd + [(j, i) for i, j in odd])
    from_a = lax.ppermute(to_a, "slab", pairs)

    channel_map, gain, bias, projection = call(
        functools.partial(feature_kernel, width),
        [((width, LANES), jnp.bfloat16)] + [((width, LANES), f32)] * 3,
        scratch=[pltpu.VMEM((LANES, LANES), f32), pltpu.VMEM((LANES, LANES), f32)],
        ins=[VMEM] * 2,
    )(spectral, dense)
    pay_rows = -(-(MODES + 2 + n_grp) // 8) * 8
    scale = 1.0 / (devices * lines * SUB)
    field_now, payload = call(
        functools.partial(step_kernel, two_sided, width, pay_rows, scale),
        [(velocity.shape, f32), ((pay_rows, LANES), f32)],
        scratch=[
            pltpu.VMEM((8 * cells_x, cells_z + LANES), f32),
            pltpu.VMEM((8 * cells_x, cells_z + LANES), f32),
            pltpu.VMEM((lines, SUB), f32),
            pltpu.VMEM((lines, SUB), f32),
            pltpu.VMEM((LANES, lines * SUB), jnp.bfloat16),
            pltpu.VMEM((2 * width, lines * SUB), jnp.bfloat16),
        ],
        ins=[VMEM] * 7 + [SMEM] * 3 + [VMEM] * 3,
    )(velocity, rate, forcing, low, high, from_a, from_b,
      anchor_line, anchor_z, assign.reshape(-1), channel_map, projection, table)

    masks = hop_masks(n_grp, n_slab)
    if joined:
        mine = gathered[0]
        order = [n_slab] + [m for m in masks if m not in (1, n_slab)] + [1]
        for mask in order[1:-1]:
            mine = jnp.concatenate([mine, swap(mine, mask, devices)], axis=0)
        other = swap(mine, order[-1], devices)
        base = call(
            functools.partial(base_kernel, order, width), [(spectral.shape, f32)], ins=[VMEM] * 3
        )(spectral, mine, other)[0]
    else:
        whole = lax.all_gather(momentum, AXES, axis=0, tiled=True)
        base = spectral - (learn_rate * decay_rate) * whole
    if devices & (devices - 1) == 0:
        for mask in masks:
            payload = payload + swap(payload, mask, devices)
    else:
        payload = lax.psum(payload, AXES)
    spectral_new, dense_new, momentum_new, trainer_loss = call(
        functools.partial(update_kernel, width, lines),
        [(spectral.shape, f32), (dense.shape, f32), (momentum.shape, f32), ((1, 1), f32)],
        scratch=[pltpu.VMEM((2 * MODES, width), f32)],
        ins=[VMEM] * 7,
    )(payload, spectral, base, dense, momentum, gain, bias)
    return (field_now, trainer_loss, spectral_new, dense_new, momentum_new)


def solution(mesh):
    placed = (
        P("grp", "slab", None),
        P("grp", "slab", None),
        P("grp", "slab", None),
        P(("grp", "slab")),
        P(("grp", "slab")),
        P(("grp", "slab"), None),
        P(),
        P(),
        P(("grp", "slab"), None),
    )
    return jax.shard_map(
        local,
        mesh=mesh,
        in_specs=placed,
        out_specs=(P("grp", "slab", None), P("grp", "slab"), P(), P(), P(("grp", "slab"), None)),
        check_vma=False,
    )
```

time: 316 us -> 56.9 us (0.18)
  blocking collectives: 112 us -> 0 us
  local copies, waits for them, and re-layouts: 73.2 us -> 7.01 us
  waiting for transfers between devices: 65.9 us -> 17.7 us
  matrix products: 23.5 us -> 0 us
  between operations: 14.5 us -> 0.81 us
  starting transfers between devices: 18.7 us -> 27.2 us
  other arithmetic: 6.66 us -> 0.03 us
  Pallas kernels: 0 us -> 3.82 us
    gather x130 -> x0, local copies, waits for them, and re-layouts: 65.2 us -> none
    reduce_scatter x1 -> x0, waiting for transfers between devices: 61.4 us -> none  [local(): lax.psum_scatter(grad_spec, ('grp', 'slab'), scatter_dimension=0, tiled=T...]
    all_gather x1 -> x0, blocking collectives: 39.3 us -> none  [local(): lax.all_gather(updated_rows, ('grp', 'slab'), axis=0, tiled=True)]
    psum x1 -> x0, blocking collectives: 37 us -> none  [local(): grad_dense = lax.psum(grad_dense, ('grp', 'slab'))]
    unnamed x1 -> x0, blocking collectives: 35.7 us -> none
    dot_general x26 -> x0, matrix products: 23.5 us -> none  [the longest x3 2.76 us: line_errors(): jnp.einsum('bwk,kwv->bvk', real_in, w_real, precision=highest)]
    ppermute x8 -> x12, waiting for transfers between devices: 4.4 us -> 17.7 us  [the longest x9 15.2 us: swap(): return lax.ppermute(array, AXES, [(i, i ^ mask) for i in range(count)])]
    ppermute x8 -> x12, starting transfers between devices: 18.7 us -> 27.2 us  [the longest x9 23 us: swap(): return lax.ppermute(array, AXES, [(i, i ^ mask) for i in range(count)])]
  transfers between devices with their start and end apart: 9 -> 12, of which waited for: 3 -> 9; matrix products, arithmetic and copies ran while one was open for 4% -> 1% of each run, Pallas kernels for 0% -> 5%
where the time goes in v1:
time: 56.9 us; the launch traced here: 56.5 us
  starting transfers between devices  27.2 us (48%)
  waiting for transfers between devices  17.7 us (31%)
  local copies, waits for them, and re-layouts  7.01 us (12%)
  Pallas kernels  3.82 us (7%)
  between operations  0.81 us (1%)
    ppermute x9, starting transfers between devices, swap(): return lax.ppermute(array, AXES, [(i, i ^ mask) for i in range(count)])  23 us
    ppermute x9, waiting for transfers between devices, swap(): return lax.ppermute(array, AXES, [(i, i ^ mask) for i in range(count)])  15.2 us
    unnamed x35, local copies, waits for them, and re-layouts  7 us
    ppermute x1, starting transfers between devices, local(): low = high = lax.ppermute(own, 'grp', [(0, 1), (1, 0)])  3 us
    ppermute x1, waiting for transfers between devices, local(): low = high = lax.ppermute(own, 'grp', [(0, 1), (1, 0)])  2.44 us
    pallas_call x1, Pallas kernels, local(): call(functools.partial(step_kernel, two_sided, width, pay_rows, scale), [...  2.26 us
  transfers between devices with their start and end apart: 12, of which 9 were waited for; matrix products, arithmetic and copies ran while one was open for 1% of the time, Pallas kernels for 5%

profile of v1, /device:TPU:0, one launch (start us, length us, event | category | flops | bytes accessed | tf_op | source)
XLA Modules:
  0.0 56.5 jit_solution(3277693021748281663)
XLA Ops:
  0.6 0.0 copy-start
  0.6 0.9 %copy-done = f32[8,8,512]{2,1,0:T(8,128)S(1)} copy-done((f32[8,8,512]{2,1,0:T(8,128)S(1)}, f32[8,8,512]{2,1,0:T(8,128)}, u32[]{:S(2)}) %copy-start) | copy-done | bytes 131096
  1.5 0.0 copy-start.2
  1.5 0.9 %copy-done.2 = f32[8,8,512]{2,1,0:T(8,128)S(1)} copy-done((f32[8,8,512]{2,1,0:T(8,128)S(1)}, f32[8,8,512]{2,1,0:T(8,128)}, u32[]{:S(2)}) %copy-start.2) | copy-done | bytes 131096
  2.4 0.0 copy-start.4
  2.4 0.9 %copy-done.4 = f32[8,8,512]{2,1,0:T(8,128)S(1)} copy-done((f32[8,8,512]{2,1,0:T(8,128)S(1)}, f32[8,8,512]{2,1,0:T(8,128)}, u32[]{:S(2)}) %copy-start.4) | copy-done | bytes 131096
  3.3 0.0 copy-start.6
  3.3 0.8 %copy-done.6 = f32[64,64]{1,0:T(8,128)S(1)} copy-done((f32[64,64]{1,0:T(8,128)S(1)}, f32[64,64]{1,0:T(8,128)}, u32[]{:S(2)}) %copy-start.6) | copy-done | bytes 16408
  4.1 0.1 shard_map.137.own_ref
  4.2 3.0 %collective-permute-start = (f32[160,128]{1,0:T(8,128)S(1)}, f32[160,128]{1,0:T(8,128)S(1)}, u32[]{:S(2)}, u32[]{:S(2)}) collective-permute-start(f32[160,128]{1,0:T(8,128)S(1)} %shard_map.137.own_ref), channel_id=1, source_target_pairs={{0,16},{16,0},{1,17},{17,1},{2,18},{18,2},{3,19},{19,3},{4,20},{20... | collective-permute-start | bytes 245768 | tf_op jit(solution)/shard_map/ppermute | solution.py:382
  7.2 2.4 %collective-permute-done.low_ref.high_ref = f32[160,128]{1,0:T(8,128)S(1)} collective-permute-done((f32[160,128]{1,0:T(8,128)S(1)}, f32[160,128]{1,0:T(8,128)S(1)}, u32[]{:S(2)}, u32[]{:S(2)}) %collective-permute-start) | collective-permute-done | bytes 81952 | tf_op jit(solution)/shard_map/ppermute | solution.py:382
  9.6 0.1 shard_map.138
  9.7 0.0 copy-start.12
  9.7 2.0 %collective-permute-start.8 = (f32[64,128]{1,0:T(8,128)S(1)}, f32[64,128]{1,0:T(8,128)S(1)}, u32[]{:S(2)}, u32[]{:S(2)}) collective-permute-start(f32[64,128]{1,0:T(8,128)S(1)} %get-tuple-element.24), channel_id=1, source_target_pairs={{0,2},{1,3},{2,0},{3,1},{4,6},{5,7},{6,4},{7,5},{8,10},{9,11},{10,... | collective-permute-start | bytes 98312 | tf_op jit(solution)/shard_map/ppermute | solution.py:352
  11.7 1.9 %collective-permute-done.8 = f32[64,128]{1,0:T(8,128)S(1)} collective-permute-done((f32[64,128]{1,0:T(8,128)S(1)}, f32[64,128]{1,0:T(8,128)S(1)}, u32[]{:S(2)}, u32[]{:S(2)}) %collective-permute-start.8) | collective-permute-done | bytes 32800 | tf_op jit(solution)/shard_map/ppermute | solution.py:352
  13.7 2.1 %collective-permute-start.9 = (f32[128,128]{1,0:T(8,128)S(1)}, f32[128,128]{1,0:T(8,128)S(1)}, u32[]{:S(2)}, u32[]{:S(2)}) collective-permute-start(f32[128,128]{1,0:T(8,128)S(1)} %pad_maximum_fusion.1), channel_id=1, source_target_pairs={{0,4},{1,5},{2,6},{3,7},{4,0},{5,1},{6,2},{7,3},{8,12},{9,13},{10,... | collective-permute-start | bytes 196616 | tf_op jit(solution)/shard_map/ppermute | solution.py:352
  15.7 2.2 %collective-permute-done.9 = f32[128,128]{1,0:T(8,128)S(1)} collective-permute-done((f32[128,128]{1,0:T(8,128)S(1)}, f32[128,128]{1,0:T(8,128)S(1)}, u32[]{:S(2)}, u32[]{:S(2)}) %collective-permute-start.9) | collective-permute-done | bytes 65568 | tf_op jit(solution)/shard_map/ppermute | solution.py:352
  18.0 4.1 %collective-permute-start.10 = (f32[256,128]{1,0:T(8,128)S(1)}, f32[256,128]{1,0:T(8,128)S(1)}, u32[]{:S(2)}, u32[]{:S(2)}) collective-permute-start(f32[256,128]{1,0:T(8,128)S(1)} %pad_maximum_fusion), channel_id=1, source_target_pairs={{0,12},{1,13},{2,14},{3,15},{4,8},{5,9},{6,10},{7,11},{8,4},{9,5},... | collective-permute-start | bytes 393224 | tf_op jit(solution)/shard_map/ppermute | solution.py:352
  22.1 0.0 copy-start.13
  22.1 3.0 %collective-permute-done.10 = f32[256,128]{1,0:T(8,128)S(1)} collective-permute-done((f32[256,128]{1,0:T(8,128)S(1)}, f32[256,128]{1,0:T(8,128)S(1)}, u32[]{:S(2)}, u32[]{:S(2)}) %collective-permute-start.10) | collective-permute-done | bytes 131104 | tf_op jit(solution)/shard_map/ppermute | solution.py:352
  25.2 0.1 collective-permute-start.11
  25.2 0.5 collective-permute-start.1
  25.7 0.7 %collective-permute-start.2 = (f32[136,128]{1,0:T(8,128)S(1)}, f32[136,128]{1,0:T(8,128)S(1)}, u32[]{:S(2)}, u32[]{:S(2)}) collective-permute-start(f32[136,128]{1,0:T(8,128)S(1)} %get-tuple-element.19), channel_id=1, source_target_pairs={{1,2},{3,4},{5,6},{7,8},{9,10},{11,12},{13,14},{2,1},{4,3},{6,5},{... | collective-permute-start | bytes 208904 | tf_op jit(solution)/shard_map/ppermute | solution.py:390
  26.4 0.0 copy-done.13
  26.4 0.1 copy.16.dense_ref
  26.5 0.0 copy-done.12
  26.5 0.3 copy.15.spectral_ref
  26.9 0.0 copy-start.1
  26.9 0.0 copy-start.3
  26.9 0.0 copy-start.5
  26.9 0.0 copy-start.8
  26.9 0.4 shard_map.139
  27.3 0.0 collective-permute-done.1.a_ref
  27.3 0.0 collective-permute-done.2.b_ref
  27.3 0.0 copy-start.9
  27.3 0.0 copy-start.10
  27.3 0.0 copy-start.11
  27.3 0.4 copy-done.1
  27.8 0.1 copy-done.3
  27.8 0.1 copy-done.5
  27.9 0.0 copy-done.8
  27.9 0.1 copy-done.9
  28.0 0.0 copy-done.10
  28.0 0.0 copy-done.11
  28.0 2.3 %shard_map.140 = (f32[8,8,512]{2,1,0:T(8,128)}, f32[24,128]{1,0:T(8,128)S(1)}) custom-call(f32[8,8,512]{2,1,0:T(8,128)S(1)} %copy-done.1, f32[8,8,512]{2,1,0:T(8,128)S(1)} %copy-done.3, f32[8,8,512]{2,1,0:T(8,128)S(1)} %copy-done.5, f32[160,128]{1,0:T(8,128)S(1)} %collective-permute-done.low_ref.high_ref, ...), custom_call_target="tpu_custom_call" | custom-call | flops 1000000 | bytes 286720 | tf_op jit(solution)/shard_map/pallas_call | solution.py:401
  30.3 4.1 %collective-permute-start.3 = (f32[24,128]{1,0:T(8,128)S(1)}, f32[24,128]{1,0:T(8,128)S(1)}, u32[]{:S(2)}, u32[]{:S(2)}) collective-permute-start(f32[24,128]{1,0:T(8,128)S(1)} %get-tuple-element.23), channel_id=1, source_target_pairs={{0,1},{1,0},{2,3},{3,2},{4,5},{5,4},{6,7},{7,6},{8,9},{9,8},{10,11... | collective-permute-start | bytes 36872 | tf_op jit(solution)/shard_map/ppermute | solution.py:352
  34.4 0.8 %collective-permute-done.3 = f32[24,128]{1,0:T(8,128)S(1)} collective-permute-done((f32[24,128]{1,0:T(8,128)S(1)}, f32[24,128]{1,0:T(8,128)S(1)}, u32[]{:S(2)}, u32[]{:S(2)}) %collective-permute-start.3) | collective-permute-done | bytes 12320 | tf_op jit(solution)/shard_map/ppermute | solution.py:352
  35.2 2.6 %collective-permute-start.4 = (f32[24,128]{1,0:T(8,128)S(1)}, f32[24,128]{1,0:T(8,128)S(1)}, u32[]{:S(2)}, u32[]{:S(2)}) collective-permute-start(f32[24,128]{1,0:T(8,128)S(1)} %add.15), channel_id=1, source_target_pairs={{0,2},{1,3},{2,0},{3,1},{4,6},{5,7},{6,4},{7,5},{8,10},{9,11},{10,... | collective-permute-start | bytes 36872 | tf_op jit(solution)/shard_map/ppermute | solution.py:352
  37.8 1.7 %collective-permute-done.4 = f32[24,128]{1,0:T(8,128)S(1)} collective-permute-done((f32[24,128]{1,0:T(8,128)S(1)}, f32[24,128]{1,0:T(8,128)S(1)}, u32[]{:S(2)}, u32[]{:S(2)}) %collective-permute-start.4) | collective-permute-done | bytes 12320 | tf_op jit(solution)/shard_map/ppermute | solution.py:352
  39.5 2.2 %collective-permute-start.5 = (f32[24,128]{1,0:T(8,128)S(1)}, f32[24,128]{1,0:T(8,128)S(1)}, u32[]{:S(2)}, u32[]{:S(2)}) collective-permute-start(f32[24,128]{1,0:T(8,128)S(1)} %add.16), channel_id=1, source_target_pairs={{0,4},{1,5},{2,6},{3,7},{4,0},{5,1},{6,2},{7,3},{8,12},{9,13},{10,... | collective-permute-start | bytes 36872 | tf_op jit(solution)/shard_map/ppermute | solution.py:352
  41.7 1.7 %collective-permute-done.5 = f32[24,128]{1,0:T(8,128)S(1)} collective-permute-done((f32[24,128]{1,0:T(8,128)S(1)}, f32[24,128]{1,0:T(8,128)S(1)}, u32[]{:S(2)}, u32[]{:S(2)}) %collective-permute-start.5) | collective-permute-done | bytes 12320 | tf_op jit(solution)/shard_map/ppermute | solution.py:352
  43.4 4.3 %collective-permute-start.6 = (f32[24,128]{1,0:T(8,128)S(1)}, f32[24,128]{1,0:T(8,128)S(1)}, u32[]{:S(2)}, u32[]{:S(2)}) collective-permute-start(f32[24,128]{1,0:T(8,128)S(1)} %add.17), channel_id=1, source_target_pairs={{0,12},{1,13},{2,14},{3,15},{4,8},{5,9},{6,10},{7,11},{8,4},{9,5},... | collective-permute-start | bytes 36872 | tf_op jit(solution)/shard_map/ppermute | solution.py:352
  47.7 1.7 %collective-permute-done.6 = f32[24,128]{1,0:T(8,128)S(1)} collective-permute-done((f32[24,128]{1,0:T(8,128)S(1)}, f32[24,128]{1,0:T(8,128)S(1)}, u32[]{:S(2)}, u32[]{:S(2)}) %collective-permute-start.6) | collective-permute-done | bytes 12320 | tf_op jit(solution)/shard_map/ppermute | solution.py:352
  49.4 1.5 %collective-permute-start.7 = (f32[24,128]{1,0:T(8,128)S(1)}, f32[24,128]{1,0:T(8,128)S(1)}, u32[]{:S(2)}, u32[]{:S(2)}) collective-permute-start(f32[24,128]{1,0:T(8,128)S(1)} %add.18), channel_id=1, source_target_pairs={{0,16},{1,17},{2,18},{3,19},{4,20},{5,21},{6,22},{7,23},{8,24},{9,... | collective-permute-start | bytes 36872 | tf_op jit(solution)/shard_map/ppermute | solution.py:352
  50.9 2.2 %collective-permute-done.7 = f32[24,128]{1,0:T(8,128)S(1)} collective-permute-done((f32[24,128]{1,0:T(8,128)S(1)}, f32[24,128]{1,0:T(8,128)S(1)}, u32[]{:S(2)}, u32[]{:S(2)}) %collective-permute-start.7) | collective-permute-done | bytes 12320 | tf_op jit(solution)/shard_map/ppermute | solution.py:352
  53.1 0.0 copy-start.7
  53.1 0.0 collective-permute-done.11.other_ref
  53.1 0.2 shard_map.141.base_ref
  53.3 0.5 copy-done.7
  53.8 0.9 %shard_map.142 = (f32[2048,64]{1,0:T(8,128)S(1)}, f32[68,64]{1,0:T(8,128)S(1)}, f32[64,64]{1,0:T(8,128)}, f32[1,1]{1,0:T(1,128)}) custom-call(f32[24,128]{1,0:T(8,128)S(1)} %add.19.pay_ref, f32[2048,64]{1,0:T(8,128)S(1)} %copy.15.spectral_ref, f32[2048,64]{1,0:T(8,128)S(1)} %shard_map.141.base_ref, f32[68,64]{1,0:T(8,128)S(1)} %copy.16.dense_ref, ...), custom_call_target="tpu_custom_call" | custom-call | flops 1000000 | bytes 1116168 | tf_op jit(solution)/shard_map/pallas_call | solution.py:434
  54.7 1.1 %copy.20 = f32[2048,64]{0,1:T(8,128)} copy(f32[2048,64]{1,0:T(8,128)S(1)} %get-tuple-element.33) | data formatting | bytes 1048576
  55.8 0.7 %copy.21 = f32[68,64]{0,1:T(8,128)} copy(f32[68,64]{1,0:T(8,128)S(1)} %get-tuple-element.34) | data formatting | bytes 34816
  (11 shorter events, 0.1 us)
Async XLA Ops:
  0.6 0.9 %copy-start = (f32[8,8,512]{2,1,0:T(8,128)S(1)}, f32[8,8,512]{2,1,0:T(8,128)}, u32[]{:S(2)}) copy-start(f32[8,8,512]{2,1,0:T(8,128)} %v_ref.5) | copy-start | bytes 393220
  1.5 0.9 %copy-start.2 = (f32[8,8,512]{2,1,0:T(8,128)S(1)}, f32[8,8,512]{2,1,0:T(8,128)}, u32[]{:S(2)}) copy-start(f32[8,8,512]{2,1,0:T(8,128)} %rate_ref.5) | copy-start | bytes 393220
  2.4 0.9 %copy-start.4 = (f32[8,8,512]{2,1,0:T(8,128)S(1)}, f32[8,8,512]{2,1,0:T(8,128)}, u32[]{:S(2)}) copy-start(f32[8,8,512]{2,1,0:T(8,128)} %forcing_ref.5) | copy-start | bytes 393220
  3.3 0.8 %copy-start.6 = (f32[64,64]{1,0:T(8,128)S(1)}, f32[64,64]{1,0:T(8,128)}, u32[]{:S(2)}) copy-start(f32[64,64]{1,0:T(8,128)} %momentum_ref.3) | copy-start | bytes 49156
  4.2 5.4 %collective-permute-start = (f32[160,128]{1,0:T(8,128)S(1)}, f32[160,128]{1,0:T(8,128)S(1)}, u32[]{:S(2)}, u32[]{:S(2)}) collective-permute-start(f32[160,128]{1,0:T(8,128)S(1)} %shard_map.137.own_ref), channel_id=1, source_target_pairs={{0,16},{16,0},{1,17},{17,1},{2,18},{18,2},{3,19},{19,3},{4,20},{20... | collective-permute-start | bytes 245768 | tf_op jit(solution)/shard_map/ppermute | solution.py:382
  9.7 16.8 %copy-start.12 = (f32[2048,64]{0,1:T(8,128)S(1)}, f32[2048,64]{0,1:T(8,128)}, u32[]{:S(2)}) copy-start(f32[2048,64]{0,1:T(8,128)} %param.16) | copy-start | bytes 1572868
  9.7 4.0 %collective-permute-start.8 = (f32[64,128]{1,0:T(8,128)S(1)}, f32[64,128]{1,0:T(8,128)S(1)}, u32[]{:S(2)}, u32[]{:S(2)}) collective-permute-start(f32[64,128]{1,0:T(8,128)S(1)} %get-tuple-element.24), channel_id=1, source_target_pairs={{0,2},{1,3},{2,0},{3,1},{4,6},{5,7},{6,4},{7,5},{8,10},{9,11},{10,... | collective-permute-start | bytes 98312 | tf_op jit(solution)/shard_map/ppermute | solution.py:352
  13.7 4.3 %collective-permute-start.9 = (f32[128,128]{1,0:T(8,128)S(1)}, f32[128,128]{1,0:T(8,128)S(1)}, u32[]{:S(2)}, u32[]{:S(2)}) collective-permute-start(f32[128,128]{1,0:T(8,128)S(1)} %pad_maximum_fusion.1), channel_id=1, source_target_pairs={{0,4},{1,5},{2,6},{3,7},{4,0},{5,1},{6,2},{7,3},{8,12},{9,13},{10,... | collective-permute-start | bytes 196616 | tf_op jit(solution)/shard_map/ppermute | solution.py:352
  18.0 7.2 %collective-permute-start.10 = (f32[256,128]{1,0:T(8,128)S(1)}, f32[256,128]{1,0:T(8,128)S(1)}, u32[]{:S(2)}, u32[]{:S(2)}) collective-permute-start(f32[256,128]{1,0:T(8,128)S(1)} %pad_maximum_fusion), channel_id=1, source_target_pairs={{0,12},{1,13},{2,14},{3,15},{4,8},{5,9},{6,10},{7,11},{8,4},{9,5},... | collective-permute-start | bytes 393224 | tf_op jit(solution)/shard_map/ppermute | solution.py:352
  22.1 4.3 %copy-start.13 = (f32[68,64]{0,1:T(8,128)S(1)}, f32[68,64]{0,1:T(8,128)}, u32[]{:S(2)}) copy-start(f32[68,64]{0,1:T(8,128)} %param.17) | copy-start | bytes 52228
  25.2 27.9 %collective-permute-start.11 = (f32[512,128]{1,0:T(8,128)S(1)}, f32[512,128]{1,0:T(8,128)S(1)}, u32[]{:S(2)}, u32[]{:S(2)}) collective-permute-start(f32[512,128]{1,0:T(8,128)S(1)} %constant_dynamic-update-slice_fusion.mine_ref), channel_id=1, source_target_pairs={{0,1},{1,0},{2,3},{3,2},{4,5},{5,4},{6,7},{7,6},{8,9},{9,8},{10,11... | collective-permute-start | bytes 786440 | tf_op jit(solution)/shard_map/ppermute | solution.py:352
  25.2 2.0 %collective-permute-start.1 = (f32[136,128]{1,0:T(8,128)S(1)}, f32[136,128]{1,0:T(8,128)S(1)}, u32[]{:S(2)}, u32[]{:S(2)}) collective-permute-start(f32[136,128]{1,0:T(8,128)S(1)} %get-tuple-element.18), channel_id=1, source_target_pairs={{0,1},{1,0},{2,3},{3,2},{4,5},{5,4},{6,7},{7,6},{8,9},{9,8},{10,11... | collective-permute-start | bytes 208904 | tf_op jit(solution)/shard_map/ppermute | solution.py:391
  25.7 1.5 %collective-permute-start.2 = (f32[136,128]{1,0:T(8,128)S(1)}, f32[136,128]{1,0:T(8,128)S(1)}, u32[]{:S(2)}, u32[]{:S(2)}) collective-permute-start(f32[136,128]{1,0:T(8,128)S(1)} %get-tuple-element.19), channel_id=1, source_target_pairs={{1,2},{3,4},{5,6},{7,8},{9,10},{11,12},{13,14},{2,1},{4,3},{6,5},{... | collective-permute-start | bytes 208904 | tf_op jit(solution)/shard_map/ppermute | solution.py:390
  26.9 0.9 %copy-start.1 = (f32[8,8,512]{2,1,0:T(8,128)S(1)}, f32[8,8,512]{2,1,0:T(8,128)}, u32[]{:S(2)}) copy-start(f32[8,8,512]{2,1,0:T(8,128)} %v_ref.5) | copy-start | bytes 393220
  26.9 1.0 %copy-start.3 = (f32[8,8,512]{2,1,0:T(8,128)S(1)}, f32[8,8,512]{2,1,0:T(8,128)}, u32[]{:S(2)}) copy-start(f32[8,8,512]{2,1,0:T(8,128)} %rate_ref.5) | copy-start | bytes 393220
  26.9 1.0 %copy-start.5 = (f32[8,8,512]{2,1,0:T(8,128)S(1)}, f32[8,8,512]{2,1,0:T(8,128)}, u32[]{:S(2)}) copy-start(f32[8,8,512]{2,1,0:T(8,128)} %forcing_ref.5) | copy-start | bytes 393220
  26.9 1.0 %copy-start.8 = (f32[64,128]{1,0:T(8,128)S(1)}, f32[64,128]{1,0:T(8,128)}, u32[]{:S(2)}) copy-start(f32[64,128]{1,0:T(8,128)} %constant.2.clone.table_ref) | copy-start | bytes 98308
  27.3 0.7 %copy-start.9 = (s32[16]{0:T(128)S(1)}, s32[16]{0:T(128)}, u32[]{:S(2)}) copy-start(s32[16]{0:T(128)} %line_ref.1) | copy-start | bytes 196
  27.3 0.7 %copy-start.10 = (s32[16]{0:T(128)S(1)}, s32[16]{0:T(128)}, u32[]{:S(2)}) copy-start(s32[16]{0:T(128)} %start_ref.1) | copy-start | bytes 196
  27.3 0.7 %copy-start.11 = (s32[16,1]{0,1:T(1,128)S(1)}, s32[16,1]{0,1:T(1,128)}, u32[]{:S(2)}) copy-start(s32[16,1]{0,1:T(1,128)} %param.15) | copy-start | bytes 196
  30.3 4.9 %collective-permute-start.3 = (f32[24,128]{1,0:T(8,128)S(1)}, f32[24,128]{1,0:T(8,128)S(1)}, u32[]{:S(2)}, u32[]{:S(2)}) collective-permute-start(f32[24,128]{1,0:T(8,128)S(1)} %get-tuple-element.23), channel_id=1, source_target_pairs={{0,1},{1,0},{2,3},{3,2},{4,5},{5,4},{6,7},{7,6},{8,9},{9,8},{10,11... | collective-permute-start | bytes 36872 | tf_op jit(solution)/shard_map/ppermute | solution.py:352
  35.2 4.3 %collective-permute-start.4 = (f32[24,128]{1,0:T(8,128)S(1)}, f32[24,128]{1,0:T(8,128)S(1)}, u32[]{:S(2)}, u32[]{:S(2)}) collective-permute-start(f32[24,128]{1,0:T(8,128)S(1)} %add.15), channel_id=1, source_target_pairs={{0,2},{1,3},{2,0},{3,1},{4,6},{5,7},{6,4},{7,5},{8,10},{9,11},{10,... | collective-permute-start | bytes 36872 | tf_op jit(solution)/shard_map/ppermute | solution.py:352
  39.5 3.9 %collective-permute-start.5 = (f32[24,128]{1,0:T(8,128)S(1)}, f32[24,128]{1,0:T(8,128)S(1)}, u32[]{:S(2)}, u32[]{:S(2)}) collective-permute-start(f32[24,128]{1,0:T(8,128)S(1)} %add.16), channel_id=1, source_target_pairs={{0,4},{1,5},{2,6},{3,7},{4,0},{5,1},{6,2},{7,3},{8,12},{9,13},{10,... | collective-permute-start | bytes 36872 | tf_op jit(solution)/shard_map/ppermute | solution.py:352
  43.4 6.0 %collective-permute-start.6 = (f32[24,128]{1,0:T(8,128)S(1)}, f32[24,128]{1,0:T(8,128)S(1)}, u32[]{:S(2)}, u32[]{:S(2)}) collective-permute-start(f32[24,128]{1,0:T(8,128)S(1)} %add.17), channel_id=1, source_target_pairs={{0,12},{1,13},{2,14},{3,15},{4,8},{5,9},{6,10},{7,11},{8,4},{9,5},... | collective-permute-start | bytes 36872 | tf_op jit(solution)/shard_map/ppermute | solution.py:352
  49.4 3.7 %collective-permute-start.7 = (f32[24,128]{1,0:T(8,128)S(1)}, f32[24,128]{1,0:T(8,128)S(1)}, u32[]{:S(2)}, u32[]{:S(2)}) collective-permute-start(f32[24,128]{1,0:T(8,128)S(1)} %add.18), channel_id=1, source_target_pairs={{0,16},{1,17},{2,18},{3,19},{4,20},{5,21},{6,22},{7,23},{8,24},{9,... | collective-permute-start | bytes 36872 | tf_op jit(solution)/shard_map/ppermute | solution.py:352
  53.1 0.8 %copy-start.7 = (f32[64,64]{1,0:T(8,128)S(1)}, f32[64,64]{1,0:T(8,128)}, u32[]{:S(2)}) copy-start(f32[64,64]{1,0:T(8,128)} %momentum_ref.3) | copy-start | bytes 49156

commit v2 on v1

--- a/solution.py
+++ b/solution.py
@@ -9,7 +9,7 @@
 from jax.experimental.pallas import tpu as pltpu
 from jax.sharding import PartitionSpec as P
 
-STEPS = 2
+
 SUB = 128
 MODES = 16
 LANES = 128
@@ -23,19 +23,18 @@
 HIGHEST = lax.Precision.HIGHEST
 NT = (((1,), (1,)), ((), ()))
 VMEM = pl.BlockSpec(memory_space=pltpu.VMEM)
-SMEM = pl.BlockSpec(memory_space=pltpu.SMEM)
-
-
-def call(kernel, outs, scratch=(), ins=(), aliases=None, flops=1000000):
+HBM = pl.BlockSpec(memory_space=pltpu.HBM)
+
+
+def call(kernel, outs, scratch=(), ins=(), places=None, flops=1000000):
     outs = [jax.ShapeDtypeStruct(shape, dtype) for shape, dtype in outs]
     size = sum(math.prod(o.shape) * o.dtype.itemsize for o in outs)
     return pl.pallas_call(
         kernel,
         out_shape=outs,
         in_specs=list(ins),
-        out_specs=[VMEM] * len(outs),
+        out_specs=places or [VMEM] * len(outs),
         scratch_shapes=list(scratch),
-        input_output_aliases=aliases or {},
         compiler_params=pltpu.CompilerParams(vmem_limit_bytes=16 << 20),
         cost_estimate=pl.CostEstimate(flops=flops, bytes_accessed=2 * size, transcendentals=0),
     )
@@ -64,19 +63,34 @@
     return jnp.concatenate([block[:half], block[half:]], axis=1)
 
 
-def edge_kernel(side, with_momentum, v_ref, rate_ref, forcing_ref, momentum_ref, out_ref):
+def edge_kernel(
+    with_momentum, v_hbm, rate_hbm, forcing_hbm, momentum_hbm, v_ref, rate_ref, forcing_ref, momentum_ref, *rest
+):
+    out_refs, sems = rest[:-1], rest[-1]
+    moves = [
+        pltpu.make_async_copy(source, target, sems.at[number])
+        for number, (source, target) in enumerate(
+            ((momentum_hbm, momentum_ref), (v_hbm, v_ref), (rate_hbm, rate_ref), (forcing_hbm, forcing_ref))
+        )
+    ]
+    for move in moves:
+        move.start()
     last = v_ref.shape[0] - 1
     chunks = v_ref.shape[2] // LANES
-    high = (lax.axis_index("grp") == 0) if side is None else side
-    edge = jnp.where(high, last, 0)
-    second = jnp.where(high, last - 1, 1)
-    planes = (v_ref[edge], v_ref[second], rate_ref[edge], forcing_ref[edge])
-    for number, plane in enumerate(planes):
-        put_plane(out_ref, number * 8 * chunks, plane)
+    moves[0].wait()
     if with_momentum:
-        packed = pack_rows(momentum_ref[...])
+        packed = pack_rows(momentum_ref[...].T)
         start = 4 * 8 * chunks
-        out_ref[start : start + packed.shape[0], :] = packed
+        out_refs[0][start : start + packed.shape[0], :] = packed
+    for move in moves[1:]:
+        move.wait()
+    sides = [lax.axis_index("grp") == 0] if len(out_refs) == 1 else [True, False]
+    for out_ref, high in zip(out_refs, sides):
+        edge = jnp.where(high, last, 0)
+        second = jnp.where(high, last - 1, 1)
+        planes = (v_ref[edge], v_ref[second], rate_ref[edge], forcing_ref[edge])
+        for number, plane in enumerate(planes):
+            put_plane(out_ref, number * 8 * chunks, plane)
 
 
 def grp_halo(two_sided, ref_low, ref_high, layer, chunks):
@@ -112,39 +126,61 @@
         outs[2][packed_rows : 2 * packed_rows, :] = low_ref[start : start + packed_rows, :]
 
 
-def feature_kernel(width, spectral_ref, dense_ref, map_ref, gain_ref, bias_ref, projection_ref, square, rows):
-    square[...] = jnp.zeros_like(square)
-    square[0 : dense_ref.shape[0], 0:width] = dense_ref[...]
-    turned = square[...].T
-    gain = jnp.broadcast_to(turned[0:width, width : width + 1], (width, LANES))
-    bias = jnp.broadcast_to(turned[0:width, width + 1 : width + 2], (width, LANES))
-    gain_ref[...] = gain
-    bias_ref[...] = bias
-    projection_ref[...] = jnp.broadcast_to(turned[0:width, width + 3 : width + 4], (width, LANES))
-    gain, bias = gain[:, :width], bias[:, :width]
-    rows[...] = jnp.zeros_like(rows)
-    for block in range(2 * MODES):
-        weights = spectral_ref[block * width : (block + 1) * width, :]
-        rows[block : block + 1, 0:width] = jnp.sum(gain * weights, axis=0, keepdims=True)
-    mixing = dense_ref[0:width, :]
-    rows[2 * MODES : 2 * MODES + 1, 0:width] = jnp.sum(gain * mixing, axis=0, keepdims=True)
-    rows[2 * MODES + 1 : 2 * MODES + 2, 0:width] = (
-        jnp.sum(bias * (mixing + spectral_ref[0:width, :]), axis=0, keepdims=True)
-        + dense_ref[width + 2 : width + 3, :]
-    )
-    full = rows[0:FEATURES, :]
+def as_row(column):
+    size = column.shape[0]
+    square = (size, size)
+    same = lax.broadcasted_iota(jnp.int32, square, 0) == lax.broadcasted_iota(jnp.int32, square, 1)
+    return jnp.sum(jnp.where(same, column, 0.0), axis=0, keepdims=True)
+
+
+def as_column(row):
+    size = row.shape[1]
+    square = (size, size)
+    same = lax.broadcasted_iota(jnp.int32, square, 0) == lax.broadcasted_iota(jnp.int32, square, 1)
+    return jnp.sum(jnp.where(same, row, 0.0), axis=1, keepdims=True)
+
+
+def feature_kernel(width, spectral_ref, dense_ref, map_ref, projection_ref, row_ref):
+    gain = as_row(dense_ref[:, width : width + 1])
+    bias = as_row(dense_ref[:, width + 1 : width + 2])
+    projection_ref[...] = jnp.broadcast_to(dense_ref[:, width + 3 : width + 4], (width, LANES))
+    row_ref[...] = jnp.zeros_like(row_ref)
+    row_ref[0:1, :] = jnp.concatenate([gain, gain], axis=1)
+    row_ref[1:2, :] = jnp.concatenate([bias, bias], axis=1)
+    gains = row_ref[0:1, :]
+    lane = lax.broadcasted_iota(jnp.int32, (width, LANES), 1)
+    low = lane < width
+    full = jnp.zeros((width, LANES), jnp.float32)
+    for pair in range(MODES):
+        product = spectral_ref[:, pair * LANES : (pair + 1) * LANES] * gains
+        first = jnp.sum(jnp.where(low, product, 0.0), axis=1, keepdims=True)
+        second = jnp.sum(jnp.where(low, 0.0, product), axis=1, keepdims=True)
+        full = jnp.where(lane == 2 * pair, first, jnp.where(lane == 2 * pair + 1, second, full))
+    mixing = dense_ref[:, 0:width]
+    by_input = jnp.sum(gain * mixing, axis=1, keepdims=True)
+    by_one = jnp.sum(bias * (mixing + spectral_ref[:, 0:width]), axis=1, keepdims=True)
+    by_one = by_one + dense_ref[:, width + 2 : width + 3]
+    full = jnp.where(lane == 2 * MODES, by_input, jnp.where(lane == 2 * MODES + 1, by_one, full))
     coarse = full.astype(jnp.bfloat16).astype(jnp.float32)
-    rows[0:FEATURES, :] = coarse
-    rows[FEATURES : 2 * FEATURES, :] = coarse
-    rows[2 * FEATURES : 3 * FEATURES, :] = full - coarse
-    map_ref[...] = rows[...].T[0:width, :].astype(jnp.bfloat16)
+    fine = full - coarse
+    joined = coarse + pltpu.roll(coarse, FEATURES, 1) + pltpu.roll(fine, 2 * FEATURES, 1)
+    map_ref[...] = joined.astype(jnp.bfloat16)
 
 
 def step_kernel(
-    two_sided, width, pay_rows, scale, v_ref, rate_ref, forcing_ref, low_ref, high_ref, a_ref, b_ref,
-    line_ref, start_ref, assign_ref, map_ref, projection_ref, table_ref,
-    field_ref, pay_ref, previous, change, inputs_ref, targets_ref, feature_ref, slope_ref,
+    two_sided, width, scale, v_ref, rate_ref, forcing_ref, low_ref, high_ref, a_ref, b_ref,
+    line_hbm, start_hbm, assign_hbm, map_ref, projection_ref, table_ref,
+    previous, change, pay_ref, line_ref, start_ref, assign_ref, sems,
+    inputs_ref, targets_ref, feature_ref, slope_ref,
 ):
+    moves = [
+        pltpu.make_async_copy(source, target, sems.at[number])
+        for number, (source, target) in enumerate(
+            ((line_hbm, line_ref), (start_hbm, start_ref), (assign_hbm, assign_ref))
+        )
+    ]
+    for move in moves:
+        move.start()
     cells_x, cells_y, cells_z = v_ref.shape
     chunks = cells_z // LANES
     even = lax.rem(lax.axis_index("slab"), 2) == 0
@@ -209,12 +245,13 @@
         plane = stepped[i + 1]
         up, down = shifted(plane, left_new[i : i + 1], right_new[i : i + 1])
         moved = tendency(plane, stepped[i + 2], stepped[i], up, down, rate_ref[i], forcing_ref[i])
-        field_ref[i] = plane + moved
         previous[8 * i : 8 * i + 8, 0:cells_z] = plane
         change[8 * i : 8 * i + 8, 0:cells_z] = moved
     count = line_ref.shape[0]
     previous[:, cells_z : cells_z + LANES] = jnp.zeros((8 * cells_x, LANES), jnp.float32)
     change[:, cells_z : cells_z + LANES] = jnp.zeros((8 * cells_x, LANES), jnp.float32)
+    for move in moves:
+        move.wait()
     for t in range(count):
         line, start = line_ref[t], start_ref[t]
         base = pl.multiple_of((start // LANES) * LANES, LANES)
@@ -277,63 +314,98 @@
     pay_ref[pl.ds(MODES + 2 + lax.axis_index("grp"), 1), :] = losses
 
 
+def field_kernel(previous, change, _, out_ref):
+    cells_x, _, cells_z = out_ref.shape
+    for i in range(cells_x):
+        at = slice(8 * i, 8 * i + 8)
+        out_ref[i] = previous[at, 0:cells_z] + change[at, 0:cells_z]
+
+
 def base_kernel(masks, width, spectral_ref, mine_ref, other_ref, out_ref):
     here = lax.axis_index("grp") * lax.axis_size("slab") + lax.axis_index("slab")
+    even = lax.rem(here, 2) == 0
     rows = width // 2
-    held = mine_ref.shape[0] // rows
-    for number in range(2 * held):
+    low = lax.broadcasted_iota(jnp.int32, (rows, LANES), 1) < width
+    for number in range(mine_ref.shape[0] // rows):
         source = here
         for bit, mask in enumerate(masks):
             if number >> bit & 1:
                 source = source ^ mask
-        ref, place = (mine_ref, number) if number < held else (other_ref, number - held)
-        for part in range(2):
-            start = pl.multiple_of(source * width + part * rows, rows)
-            moved = ref[place * rows : (place + 1) * rows, part * width : (part + 1) * width]
-            out_ref[pl.ds(start, rows), :] = spectral_ref[pl.ds(start, rows), :] - (learn_rate * decay_rate) * moved
+        columns = pl.ds(pl.multiple_of((source // 2) * LANES, LANES), LANES)
+        mine = mine_ref[number * rows : (number + 1) * rows, :]
+        other = other_ref[number * rows : (number + 1) * rows, :]
+        first, second = jnp.where(even, mine, other), jnp.where(even, other, mine)
+        top = jnp.where(low, first, pltpu.roll(second, width, 1))
+        bottom = jnp.where(low, pltpu.roll(first, width, 1), second)
+        factor = learn_rate * decay_rate
+        out_ref[0:rows, columns] = spectral_ref[0:rows, columns] - factor * top
+        out_ref[rows : 2 * rows, columns] = spectral_ref[rows : 2 * rows, columns] - factor * bottom
 
 
 def update_kernel(
-    width, lines, pay_ref, spectral_ref, base_ref, dense_ref, momentum_ref, gain_ref, bias_ref,
-    spectral_out, dense_out, momentum_out, loss_out, row_ref,
+    width, lines, groups, pay_ref, spectral_ref, base_ref, dense_ref, momentum_ref, row_ref,
+    spectral_hbm, dense_out, momentum_out, loss_out, square, result, sems,
 ):
     first, second = lax.axis_index("grp"), lax.axis_index("slab")
     here = first * lax.axis_size("slab") + second
-    gain, bias = gain_ref[:, 0:width], bias_ref[:, 0:width]
-    row_ref[0:MODES, :] = pay_ref[0:MODES, 0:width]
-    row_ref[MODES : 2 * MODES, :] = pay_ref[0:MODES, width : 2 * width]
+    square[...] = jnp.zeros_like(square)
+    square[0:MODES, 0:width] = pay_ref[0:MODES, 0:width]
+    square[MODES : 2 * MODES, 0:width] = pay_ref[0:MODES, width : 2 * width]
     slopes = pay_ref[MODES : MODES + 2, :]
-    by_input, by_one = slopes[0:1, 0:width], slopes[0:1, width : 2 * width]
-    offset = bias * by_one
-    gathered = dense_ref[0:width, :] * by_input
-    for block in range(2 * MODES):
-        span = slice(block * width, (block + 1) * width)
-        row = row_ref[block : block + 1, :]
-        gradient = gain * row
-        if block == 0:
-            gradient = gradient + offset
-        spectral_out[span, :] = base_ref[span, :] - learn_rate * gradient
-        gathered = gathered + spectral_ref[span, :] * row
-    constant = (dense_ref[0:width, :] + spectral_ref[0:width, :]) * by_one
-    ones = jnp.ones((8, width), jnp.float32)
-    gain_row = lax.dot_general(ones, gathered, NT, precision=HIGHEST, preferred_element_type=jnp.float32)
-    bias_row = lax.dot_general(ones, constant, NT, precision=HIGHEST, preferred_element_type=jnp.float32)
-    dense_out[0:width, :] = dense_ref[0:width, :] - dense_rate * (gain * by_input + offset)
-    changes = (gain_row[0:1], bias_row[0:1], by_one, slopes[1:2, 0:width])
-    for number, gradient in enumerate(changes):
-        at = slice(width + number, width + number + 1)
-        dense_out[at, :] = dense_ref[at, :] - dense_rate * gradient
+    square[2 * MODES : 2 * MODES + 1, 0:width] = slopes[0:1, 0:width]
+    square[2 * MODES + 1 : 2 * MODES + 2, 0:width] = slopes[0:1, width : 2 * width]
+    square[2 * MODES + 2 : 2 * MODES + 3, 0:width] = slopes[1:2, 0:width]
+    turned = square[...].T[0:width, :]
+    gains, biases = row_ref[0:1, :], row_ref[1:2, :]
+    by_input = turned[:, 2 * MODES : 2 * MODES + 1]
+    by_one = turned[:, 2 * MODES + 1 : 2 * MODES + 2]
+    by_output = turned[:, 2 * MODES + 2 : 2 * MODES + 3]
+    lane = lax.broadcasted_iota(jnp.int32, (width, LANES), 1)
+    low = lane < width
+    gathered = jnp.zeros((width, LANES), jnp.float32)
+    copies = []
+    for pair in range(MODES):
+        span = slice(pair * LANES, (pair + 1) * LANES)
+        column = jnp.where(low, turned[:, 2 * pair : 2 * pair + 1], turned[:, 2 * pair + 1 : 2 * pair + 2])
+        gradient = gains * column
+        if pair == 0:
+            gradient = gradient + jnp.where(low, biases * by_one, 0.0)
+        result[:, span] = base_ref[:, span] - learn_rate * gradient
+        gathered = gathered + spectral_ref[:, span] * column
+        if (pair + 1) % (MODES // groups) == 0:
+            number = len(copies)
+            part = pl.ds(number * (MODES // groups) * LANES, (MODES // groups) * LANES)
+            copies.append(pltpu.make_async_copy(result.at[:, part], spectral_hbm.at[:, part], sems.at[number]))
+            copies[-1].start()
+    mixing = dense_ref[:, 0:width]
+    gain_row = jnp.sum(gathered, axis=0, keepdims=True)
+    gain_row = gain_row[:, 0:width] + gain_row[:, width:] + jnp.sum(mixing * by_input, axis=0, keepdims=True)
+    bias_row = jnp.sum((mixing + spectral_ref[:, 0:width]) * by_one, axis=0, keepdims=True)
+    dense_out[:, 0:width] = mixing - dense_rate * (gains[:, 0:width] * by_input + biases[:, 0:width] * by_one)
+    tail = dense_ref[:, width : width + 4]
+    lane4 = lax.broadcasted_iota(jnp.int32, (width, 4), 1)
+    change = jnp.where(
+        lane4 == 0, as_column(gain_row), jnp.where(
+            lane4 == 1, as_column(bias_row), jnp.where(lane4 == 2, by_one, by_output)))
+    dense_out[:, width : width + 4] = tail - dense_rate * change
     piece = momentum_ref.shape[0]
     block = here * piece // width
-    inside = 0 if piece == width else pl.multiple_of(lax.rem(here * piece, width), piece)
-    at = pl.ds(inside, piece)
-    gradient = gain_ref[at, 0:width] * row_ref[pl.ds(block, 1), :]
-    gradient = gradient + jnp.where(block == 0, bias_ref[at, 0:width] * by_one, 0.0)
+    inside = here * piece - block * width
+    square[0 : width, :] = jnp.where(low, dense_ref[:, width : width + 1], dense_ref[:, width + 1 : width + 2])
+    at = pl.ds(0 if piece == width else pl.multiple_of(inside, piece), piece)
+    half = block // MODES
+    mode = block - half * MODES
+    row = pay_ref[pl.ds(mode, 1), :]
+    row = jnp.where(half == 0, row[:, 0:width], row[:, width : 2 * width])
+    gradient = square[at, 0:1] * row
+    gradient = gradient + jnp.where(block == 0, square[at, width : width + 1] * slopes[0:1, width : 2 * width], 0.0)
     momentum_out[...] = decay_rate * momentum_ref[...] + gradient
     sums = pay_ref[pl.ds(MODES + 2 + first, 1), :]
     lane = lax.broadcasted_iota(jnp.int32, (1, LANES), 1)
     own = jnp.sum(jnp.where(lane == second, sums, 0.0), axis=1, keepdims=True)
     loss_out[...] = own * (1.0 / (lines * SUB))
+    for copy in copies:
+        copy.wait()
 
 
 def hop_masks(n_grp, n_slab):
@@ -348,6 +420,10 @@
     return masks
 
 
+def in_hbm(array):
+    return pltpu.with_memory_space_constraint(array, pltpu.HBM)
+
+
 def swap(array, mask, count):
     return lax.ppermute(array, AXES, [(i, i ^ mask) for i in range(count)])
 
@@ -357,7 +433,7 @@
     devices = n_grp * n_slab
     width = dense.shape[1]
     lines = anchor_line.shape[0]
-    cells_x, cells_y, cells_z = velocity.shape
+    cells_x, _, cells_z = velocity.shape
     chunks = cells_z // LANES
     halo_rows = 4 * 8 * chunks
     piece = momentum.shape[0]
@@ -366,78 +442,85 @@
     joined = n_grp == 2 and piece == width and devices & (devices - 1) == 0
     two_sided = n_grp != 2
     table = jnp.asarray(tables())
-
-    def edge(side):
-        rows = halo_rows + (packed if joined else 0)
-        return call(
-            functools.partial(edge_kernel, side, joined), [((rows, LANES), f32)], ins=[VMEM] * 4
-        )(velocity, rate, forcing, momentum)[0]
-
+    spectral, dense = spectral.T, dense.T
+
+    edge_rows = halo_rows + (packed if joined else 0)
+    velocity, rate, forcing, near_momentum, *edges = call(
+        functools.partial(edge_kernel, joined),
+        [(velocity.shape, f32)] * 3 + [(momentum.shape, f32)]
+        + [((edge_rows, LANES), f32)] * (2 if two_sided else 1),
+        scratch=[pltpu.SemaphoreType.DMA((4,))],
+        ins=[HBM] * 4,
+    )(*(in_hbm(array) for array in (velocity, rate, forcing, momentum)))
     if two_sided:
-        low = lax.ppermute(edge(True), "grp", [(i, i + 1) for i in range(n_grp - 1)])
-        high = lax.ppermute(edge(False), "grp", [(i + 1, i) for i in range(n_grp - 1)])
-        own = low
+        low = lax.ppermute(edges[0], "grp", [(i, i + 1) for i in range(n_grp - 1)])
+        high = lax.ppermute(edges[1], "grp", [(i + 1, i) for i in range(n_grp - 1)])
     else:
-        own = edge(None)
-        low = high = lax.ppermute(own, "grp", [(0, 1), (1, 0)])
+        low = high = lax.ppermute(edges[0], "grp", [(0, 1), (1, 0)])
     message = (halo_rows + 2 * chunks, LANES)
     outs = [(message, f32), (message, f32)] + ([((2 * packed, LANES), f32)] if joined else [])
     to_a, to_b, *gathered = call(
         functools.partial(side_kernel, two_sided, packed if joined else 0), outs, ins=[VMEM] * 6
-    )(velocity, rate, forcing, low, high, own)
+    )(velocity, rate, forcing, low, high, edges[0])
     pairs = [(i, i ^ 1) for i in range(n_slab)]
     odd = [(i, i + 1) for i in range(1, n_slab - 1, 2)]
     from_b = lax.ppermute(to_b, "slab", odd + [(j, i) for i, j in odd])
     from_a = lax.ppermute(to_a, "slab", pairs)
-
-    channel_map, gain, bias, projection = call(
+    channel_map, projection, rows = call(
         functools.partial(feature_kernel, width),
-        [((width, LANES), jnp.bfloat16)] + [((width, LANES), f32)] * 3,
-        scratch=[pltpu.VMEM((LANES, LANES), f32), pltpu.VMEM((LANES, LANES), f32)],
+        [((width, LANES), jnp.bfloat16), ((width, LANES), f32), ((8, LANES), f32)],
         ins=[VMEM] * 2,
     )(spectral, dense)
     pay_rows = -(-(MODES + 2 + n_grp) // 8) * 8
     scale = 1.0 / (devices * lines * SUB)
-    field_now, payload = call(
-        functools.partial(step_kernel, two_sided, width, pay_rows, scale),
-        [(velocity.shape, f32), ((pay_rows, LANES), f32)],
-        scratch=[
-            pltpu.VMEM((8 * cells_x, cells_z + LANES), f32),
-            pltpu.VMEM((8 * cells_x, cells_z + LANES), f32),
+    window = ((8 * cells_x, cells_z + LANES), f32)
+    previous, change, payload = call(
+        functools.partial(step_kernel, two_sided, width, scale),
+        [window, window, ((pay_rows, LANES), f32)],
+        scratch=[pltpu.SMEM((lines,), jnp.int32)] * 3 + [
+            pltpu.SemaphoreType.DMA((3,)),
             pltpu.VMEM((lines, SUB), f32),
             pltpu.VMEM((lines, SUB), f32),
             pltpu.VMEM((LANES, lines * SUB), jnp.bfloat16),
             pltpu.VMEM((2 * width, lines * SUB), jnp.bfloat16),
         ],
-        ins=[VMEM] * 7 + [SMEM] * 3 + [VMEM] * 3,
+        ins=[VMEM] * 7 + [HBM] * 3 + [VMEM] * 3,
     )(velocity, rate, forcing, low, high, from_a, from_b,
-      anchor_line, anchor_z, assign.reshape(-1), channel_map, projection, table)
+      in_hbm(anchor_line), in_hbm(anchor_z), in_hbm(assign.reshape(-1)), channel_map, projection, table)
 
     masks = hop_masks(n_grp, n_slab)
     if joined:
         mine = gathered[0]
         order = [n_slab] + [m for m in masks if m not in (1, n_slab)] + [1]
         for mask in order[1:-1]:
-            mine = jnp.concatenate([mine, swap(mine, mask, devices)], axis=0)
+            other = swap(mine, mask, devices)
+            mine = jnp.concatenate([mine, other], axis=0)
         other = swap(mine, order[-1], devices)
         base = call(
-            functools.partial(base_kernel, order, width), [(spectral.shape, f32)], ins=[VMEM] * 3
+            functools.partial(base_kernel, order[:-1], width), [(spectral.shape, f32)], ins=[VMEM] * 3
         )(spectral, mine, other)[0]
+        masks = [1, n_slab] + [m for m in masks if m not in (1, n_slab)]
     else:
         whole = lax.all_gather(momentum, AXES, axis=0, tiled=True)
-        base = spectral - (learn_rate * decay_rate) * whole
+        base = spectral - (learn_rate * decay_rate) * whole.T
+    anchor = payload
     if devices & (devices - 1) == 0:
-        for mask in masks:
+        for number, mask in enumerate(masks):
             payload = payload + swap(payload, mask, devices)
+            if number == 0:
+                anchor = payload
     else:
         payload = lax.psum(payload, AXES)
+    field_now = call(field_kernel, [(velocity.shape, f32)], ins=[VMEM, VMEM, HBM])(previous, change, anchor)[0]
+    groups = 4
     spectral_new, dense_new, momentum_new, trainer_loss = call(
-        functools.partial(update_kernel, width, lines),
+        functools.partial(update_kernel, width, lines, groups),
         [(spectral.shape, f32), (dense.shape, f32), (momentum.shape, f32), ((1, 1), f32)],
-        scratch=[pltpu.VMEM((2 * MODES, width), f32)],
-        ins=[VMEM] * 7,
-    )(payload, spectral, base, dense, momentum, gain, bias)
-    return (field_now, trainer_loss, spectral_new, dense_new, momentum_new)
+        scratch=[pltpu.VMEM((LANES, LANES), f32), pltpu.VMEM(spectral.shape, f32), pltpu.SemaphoreType.DMA((groups,))],
+        ins=[VMEM] * 6,
+        places=[HBM, VMEM, VMEM, VMEM],
+    )(payload, spectral, base, dense, near_momentum, rows)
+    return (field_now, trainer_loss, spectral_new.T, dense_new.T, momentum_new)
 
 
 def solution(mesh):
@@ -452,6 +535,7 @@
         P(),
         P(("grp", "slab"), None),
     )
+
     return jax.shard_map(
         local,
         mesh=mesh,

time: 56.9 us -> 52.4 us (0.921)
  local copies, waits for them, and re-layouts: 7.01 us -> 0.12 us
  Pallas kernels: 3.82 us -> 6.79 us
  waiting for transfers between devices: 17.7 us -> 16.8 us
    unnamed x35 -> x9, local copies, waits for them, and re-layouts: 7 us -> 0.11 us
    pallas_call x4 -> x5, Pallas kernels: 3.42 us -> 6.11 us  [the longest x1 2.26 us: local(): call(functools.partial(step_kernel, two_sided, width, scale), [window, wi...]
    ppermute x9, waiting for transfers between devices: 15.2 us -> 14.4 us  [swap(): return lax.ppermute(array, AXES, [(i, i ^ mask) for i in range(count)])]
  transfers between devices with their start and end apart: 12 -> 12, of which waited for: 9 -> 9; matrix products, arithmetic and copies ran while one was open for 1% -> 0% of each run, Pallas kernels for 5% -> 7%
where the time goes in v2:
time: 52.4 us; the launch traced here: 52.2 us
  starting transfers between devices  27.7 us (53%)
  waiting for transfers between devices  16.8 us (32%)
  Pallas kernels  6.79 us (13%)
  between operations  0.76 us (1%)
    ppermute x9, starting transfers between devices, swap(): return lax.ppermute(array, AXES, [(i, i ^ mask) for i in range(count)])  23.4 us
    ppermute x9, waiting for transfers between devices, swap(): return lax.ppermute(array, AXES, [(i, i ^ mask) for i in range(count)])  14.4 us
    ppermute x1, starting transfers between devices, local(): low = high = lax.ppermute(edges[0], 'grp', [(0, 1), (1, 0)])  3.06 us
    ppermute x1, waiting for transfers between devices, local(): low = high = lax.ppermute(edges[0], 'grp', [(0, 1), (1, 0)])  2.44 us
    pallas_call x1, Pallas kernels, local(): call(functools.partial(step_kernel, two_sided, width, scale), [window, wi...  2.26 us
    pallas_call x1, Pallas kernels, local(): call(functools.partial(update_kernel, width, lines, groups), [(spectral.s...  1.86 us
    pallas_call x1, Pallas kernels, local(): call(functools.partial(edge_kernel, joined), [(velocity.shape, f32)] * 3...  1.09 us
  transfers between devices with their start and end apart: 12, of which 9 were waited for; matrix products, arithmetic and copies ran while one was open for 0% of the time, Pallas kernels for 7%

profile of v2, /device:TPU:0, one launch (start us, length us, event | category | flops | bytes accessed | tf_op | source)
XLA Modules:
  0.0 52.2 jit_solution(16347796908454670348)
XLA Ops:
  0.6 1.1 %shard_map.137 = (f32[8,8,512]{2,1,0:T(8,128)S(1)}, f32[8,8,512]{2,1,0:T(8,128)S(1)}, f32[8,8,512]{2,1,0:T(8,128)S(1)}, f32[64,64]{1,0:T(8,128)S(1)}, f32[160,128]{1,0:T(8,128)S(1)}) custom-call(f32[8,8,512]{2,1,0:T(8,128)} %v_hbm.1, f32[8,8,512]{2,1,0:T(8,128)} %rate_hbm.1, f32[8,8,512]{2,1,0:T(8,128)} %forcing_hbm.1, f32[64,64]{1,0:T(8,128)} %momentum_hbm.1), custom_call_target="tpu_custom_call" | custom-call | flops 1000000 | bytes 983040 | tf_op jit(solution)/shard_map/pallas_call | solution.py:448
  1.7 3.1 %collective-permute-start = (f32[160,128]{1,0:T(8,128)S(1)}, f32[160,128]{1,0:T(8,128)S(1)}, u32[]{:S(2)}, u32[]{:S(2)}) collective-permute-start(f32[160,128]{1,0:T(8,128)S(1)} %get-tuple-element.26.own_ref), channel_id=1, source_target_pairs={{0,16},{16,0},{1,17},{17,1},{2,18},{18,2},{3,19},{19,3},{4,20},{20... | collective-permute-start | bytes 245768 | tf_op jit(solution)/shard_map/ppermute | solution.py:459
  4.8 2.4 %collective-permute-done.low_ref.high_ref = f32[160,128]{1,0:T(8,128)S(1)} collective-permute-done((f32[160,128]{1,0:T(8,128)S(1)}, f32[160,128]{1,0:T(8,128)S(1)}, u32[]{:S(2)}, u32[]{:S(2)}) %collective-permute-start) | collective-permute-done | bytes 81952 | tf_op jit(solution)/shard_map/ppermute | solution.py:459
  7.2 0.1 shard_map.138
  7.3 0.0 copy-start
  7.3 2.0 %collective-permute-start.8 = (f32[64,128]{1,0:T(8,128)S(1)}, f32[64,128]{1,0:T(8,128)S(1)}, u32[]{:S(2)}, u32[]{:S(2)}) collective-permute-start(f32[64,128]{1,0:T(8,128)S(1)} %get-tuple-element.34), channel_id=1, source_target_pairs={{0,2},{1,3},{2,0},{3,1},{4,6},{5,7},{6,4},{7,5},{8,10},{9,11},{10,... | collective-permute-start | bytes 98312 | tf_op jit(solution)/shard_map/ppermute | solution.py:428
  9.3 1.9 %collective-permute-done.8 = f32[64,128]{1,0:T(8,128)S(1)} collective-permute-done((f32[64,128]{1,0:T(8,128)S(1)}, f32[64,128]{1,0:T(8,128)S(1)}, u32[]{:S(2)}, u32[]{:S(2)}) %collective-permute-start.8) | collective-permute-done | bytes 32800 | tf_op jit(solution)/shard_map/ppermute | solution.py:428
  11.3 2.1 %collective-permute-start.9 = (f32[128,128]{1,0:T(8,128)S(1)}, f32[128,128]{1,0:T(8,128)S(1)}, u32[]{:S(2)}, u32[]{:S(2)}) collective-permute-start(f32[128,128]{1,0:T(8,128)S(1)} %pad_maximum_fusion.1), channel_id=1, source_target_pairs={{0,4},{1,5},{2,6},{3,7},{4,0},{5,1},{6,2},{7,3},{8,12},{9,13},{10,... | collective-permute-start | bytes 196616 | tf_op jit(solution)/shard_map/ppermute | solution.py:428
  13.3 2.2 %collective-permute-done.9 = f32[128,128]{1,0:T(8,128)S(1)} collective-permute-done((f32[128,128]{1,0:T(8,128)S(1)}, f32[128,128]{1,0:T(8,128)S(1)}, u32[]{:S(2)}, u32[]{:S(2)}) %collective-permute-start.9) | collective-permute-done | bytes 65568 | tf_op jit(solution)/shard_map/ppermute | solution.py:428
  15.6 4.1 %collective-permute-start.10 = (f32[256,128]{1,0:T(8,128)S(1)}, f32[256,128]{1,0:T(8,128)S(1)}, u32[]{:S(2)}, u32[]{:S(2)}) collective-permute-start(f32[256,128]{1,0:T(8,128)S(1)} %pad_maximum_fusion), channel_id=1, source_target_pairs={{0,12},{1,13},{2,14},{3,15},{4,8},{5,9},{6,10},{7,11},{8,4},{9,5},... | collective-permute-start | bytes 393224 | tf_op jit(solution)/shard_map/ppermute | solution.py:428
  19.7 0.0 copy-start.1
  19.7 3.0 %collective-permute-done.10 = f32[256,128]{1,0:T(8,128)S(1)} collective-permute-done((f32[256,128]{1,0:T(8,128)S(1)}, f32[256,128]{1,0:T(8,128)S(1)}, u32[]{:S(2)}, u32[]{:S(2)}) %collective-permute-start.10) | collective-permute-done | bytes 131104 | tf_op jit(solution)/shard_map/ppermute | solution.py:428
  22.8 0.1 collective-permute-start.11
  22.9 0.5 collective-permute-start.1
  23.4 0.7 %collective-permute-start.2 = (f32[136,128]{1,0:T(8,128)S(1)}, f32[136,128]{1,0:T(8,128)S(1)}, u32[]{:S(2)}, u32[]{:S(2)}) collective-permute-start(f32[136,128]{1,0:T(8,128)S(1)} %get-tuple-element.28), channel_id=1, source_target_pairs={{1,2},{3,4},{5,6},{7,8},{9,10},{11,12},{13,14},{2,1},{4,3},{6,5},{... | collective-permute-start | bytes 208904 | tf_op jit(solution)/shard_map/ppermute | solution.py:467
  24.0 0.0 copy-done
  24.0 0.0 copy-done.1
  24.0 0.0 copy-start.2
  24.0 0.6 %shard_map.139 = (bf16[64,128]{1,0:T(8,128)(2,1)S(1)}, f32[64,128]{1,0:T(8,128)S(1)}, f32[8,128]{1,0:T(8,128)S(1)}) custom-call(f32[64,2048]{1,0:T(8,128)S(1)} %bitcast.5, f32[64,68]{1,0:T(8,128)S(1)} %bitcast.8), custom_call_target="tpu_custom_call" | custom-call | flops 1000000 | bytes 106496 | tf_op jit(solution)/shard_map/pallas_call | solution.py:469
  24.7 0.0 collective-permute-done.1.a_ref
  24.7 0.0 collective-permute-done.2.b_ref
  24.7 0.1 copy-done.2
  24.8 2.3 %shard_map.140 = (f32[64,640]{1,0:T(8,128)S(1)}, f32[64,640]{1,0:T(8,128)S(1)}, f32[24,128]{1,0:T(8,128)S(1)}) custom-call(f32[8,8,512]{2,1,0:T(8,128)S(1)} %get-tuple-element.23.v_ref, f32[8,8,512]{2,1,0:T(8,128)S(1)} %get-tuple-element.24.rate_ref, f32[8,8,512]{2,1,0:T(8,128)S(1)} %get-tuple-element.25.forcing_ref, ...), custom_call_target="tpu_custom_call" | custom-call | flops 1000000 | bytes 679936 | tf_op jit(solution)/shard_map/pallas_call | solution.py:477
  27.1 4.3 %collective-permute-start.3 = (f32[24,128]{1,0:T(8,128)S(1)}, f32[24,128]{1,0:T(8,128)S(1)}, u32[]{:S(2)}, u32[]{:S(2)}) collective-permute-start(f32[24,128]{1,0:T(8,128)S(1)} %get-tuple-element.33), channel_id=1, source_target_pairs={{0,1},{1,0},{2,3},{3,2},{4,5},{5,4},{6,7},{7,6},{8,9},{9,8},{10,11... | collective-permute-start | bytes 36872 | tf_op jit(solution)/shard_map/ppermute | solution.py:428
  31.4 0.8 %collective-permute-done.3 = f32[24,128]{1,0:T(8,128)S(1)} collective-permute-done((f32[24,128]{1,0:T(8,128)S(1)}, f32[24,128]{1,0:T(8,128)S(1)}, u32[]{:S(2)}, u32[]{:S(2)}) %collective-permute-start.3) | collective-permute-done | bytes 12320 | tf_op jit(solution)/shard_map/ppermute | solution.py:428
  32.2 1.7 %collective-permute-start.4 = (f32[24,128]{1,0:T(8,128)S(1)}, f32[24,128]{1,0:T(8,128)S(1)}, u32[]{:S(2)}, u32[]{:S(2)}) collective-permute-start(f32[24,128]{1,0:T(8,128)S(1)} %add.15._), channel_id=1, source_target_pairs={{0,16},{1,17},{2,18},{3,19},{4,20},{5,21},{6,22},{7,23},{8,24},{9,... | collective-permute-start | bytes 36872 | tf_op jit(solution)/shard_map/ppermute | solution.py:428
  34.0 2.0 %collective-permute-done.4 = f32[24,128]{1,0:T(8,128)S(1)} collective-permute-done((f32[24,128]{1,0:T(8,128)S(1)}, f32[24,128]{1,0:T(8,128)S(1)}, u32[]{:S(2)}, u32[]{:S(2)}) %collective-permute-start.4) | collective-permute-done | bytes 12320 | tf_op jit(solution)/shard_map/ppermute | solution.py:428
  35.9 2.6 %collective-permute-start.5 = (f32[24,128]{1,0:T(8,128)S(1)}, f32[24,128]{1,0:T(8,128)S(1)}, u32[]{:S(2)}, u32[]{:S(2)}) collective-permute-start(f32[24,128]{1,0:T(8,128)S(1)} %add.16), channel_id=1, source_target_pairs={{0,2},{1,3},{2,0},{3,1},{4,6},{5,7},{6,4},{7,5},{8,10},{9,11},{10,... | collective-permute-start | bytes 36872 | tf_op jit(solution)/shard_map/ppermute | solution.py:428
  38.5 1.7 %collective-permute-done.5 = f32[24,128]{1,0:T(8,128)S(1)} collective-permute-done((f32[24,128]{1,0:T(8,128)S(1)}, f32[24,128]{1,0:T(8,128)S(1)}, u32[]{:S(2)}, u32[]{:S(2)}) %collective-permute-start.5) | collective-permute-done | bytes 12320 | tf_op jit(solution)/shard_map/ppermute | solution.py:428
  40.2 2.2 %collective-permute-start.6 = (f32[24,128]{1,0:T(8,128)S(1)}, f32[24,128]{1,0:T(8,128)S(1)}, u32[]{:S(2)}, u32[]{:S(2)}) collective-permute-start(f32[24,128]{1,0:T(8,128)S(1)} %add.17), channel_id=1, source_target_pairs={{0,4},{1,5},{2,6},{3,7},{4,0},{5,1},{6,2},{7,3},{8,12},{9,13},{10,... | collective-permute-start | bytes 36872 | tf_op jit(solution)/shard_map/ppermute | solution.py:428
  42.4 1.7 %collective-permute-done.6 = f32[24,128]{1,0:T(8,128)S(1)} collective-permute-done((f32[24,128]{1,0:T(8,128)S(1)}, f32[24,128]{1,0:T(8,128)S(1)}, u32[]{:S(2)}, u32[]{:S(2)}) %collective-permute-start.6) | collective-permute-done | bytes 12320 | tf_op jit(solution)/shard_map/ppermute | solution.py:428
  44.1 4.3 %collective-permute-start.7 = (f32[24,128]{1,0:T(8,128)S(1)}, f32[24,128]{1,0:T(8,128)S(1)}, u32[]{:S(2)}, u32[]{:S(2)}) collective-permute-start(f32[24,128]{1,0:T(8,128)S(1)} %add.18), channel_id=1, source_target_pairs={{0,12},{1,13},{2,14},{3,15},{4,8},{5,9},{6,10},{7,11},{8,4},{9,5},... | collective-permute-start | bytes 36872 | tf_op jit(solution)/shard_map/ppermute | solution.py:428
  48.4 0.7 %shard_map.141 = f32[8,8,512]{2,1,0:T(8,128)} custom-call(f32[64,640]{1,0:T(8,128)S(1)} %get-tuple-element.31.previous, f32[64,640]{1,0:T(8,128)S(1)} %get-tuple-element.32.change, f32[24,128]{1,0:T(8,128)S(1)} %add.15._), custom_call_target="tpu_custom_call" | custom-call | flops 1000000 | bytes 262144 | tf_op jit(solution)/shard_map/pallas_call | solution.py:514
  49.1 1.0 %collective-permute-done.7 = f32[24,128]{1,0:T(8,128)S(1)} collective-permute-done((f32[24,128]{1,0:T(8,128)S(1)}, f32[24,128]{1,0:T(8,128)S(1)}, u32[]{:S(2)}, u32[]{:S(2)}) %collective-permute-start.7) | collective-permute-done | bytes 12320 | tf_op jit(solution)/shard_map/ppermute | solution.py:428
  50.1 0.0 collective-permute-done.11.other_ref
  50.1 0.2 shard_map.142.base_ref
  50.3 1.9 %shard_map.143 = (f32[64,2048]{1,0:T(8,128)}, f32[64,68]{1,0:T(8,128)}, f32[64,64]{1,0:T(8,128)}, f32[1,1]{1,0:T(1,128)}) custom-call(f32[24,128]{1,0:T(8,128)S(1)} %add.19.pay_ref, f32[64,2048]{1,0:T(8,128)S(1)} %bitcast.7, f32[64,2048]{1,0:T(8,128)S(1)} %shard_map.142.base_ref, f32[64,68]{1,0:T(8,128)S(1)} %bitcast.9, ...), custom_call_target="tpu_custom_call" | custom-call | flops 1000000 | bytes 1116168 | tf_op jit(solution)/shard_map/pallas_call | solution.py:516
  (11 shorter events, 0.1 us)
Async XLA Ops:
  1.7 5.5 %collective-permute-start = (f32[160,128]{1,0:T(8,128)S(1)}, f32[160,128]{1,0:T(8,128)S(1)}, u32[]{:S(2)}, u32[]{:S(2)}) collective-permute-start(f32[160,128]{1,0:T(8,128)S(1)} %get-tuple-element.26.own_ref), channel_id=1, source_target_pairs={{0,16},{16,0},{1,17},{17,1},{2,18},{18,2},{3,19},{19,3},{4,20},{20... | collective-permute-start | bytes 245768 | tf_op jit(solution)/shard_map/ppermute | solution.py:459
  7.3 16.7 %copy-start = (f32[2048,64]{0,1:T(8,128)S(1)}, f32[2048,64]{0,1:T(8,128)}, u32[]{:S(2)}) copy-start(f32[2048,64]{0,1:T(8,128)} %param.16) | copy-start | bytes 1572868
  7.3 4.0 %collective-permute-start.8 = (f32[64,128]{1,0:T(8,128)S(1)}, f32[64,128]{1,0:T(8,128)S(1)}, u32[]{:S(2)}, u32[]{:S(2)}) collective-permute-start(f32[64,128]{1,0:T(8,128)S(1)} %get-tuple-element.34), channel_id=1, source_target_pairs={{0,2},{1,3},{2,0},{3,1},{4,6},{5,7},{6,4},{7,5},{8,10},{9,11},{10,... | collective-permute-start | bytes 98312 | tf_op jit(solution)/shard_map/ppermute | solution.py:428
  11.3 4.3 %collective-permute-start.9 = (f32[128,128]{1,0:T(8,128)S(1)}, f32[128,128]{1,0:T(8,128)S(1)}, u32[]{:S(2)}, u32[]{:S(2)}) collective-permute-start(f32[128,128]{1,0:T(8,128)S(1)} %pad_maximum_fusion.1), channel_id=1, source_target_pairs={{0,4},{1,5},{2,6},{3,7},{4,0},{5,1},{6,2},{7,3},{8,12},{9,13},{10,... | collective-permute-start | bytes 196616 | tf_op jit(solution)/shard_map/ppermute | solution.py:428
  15.6 7.2 %collective-permute-start.10 = (f32[256,128]{1,0:T(8,128)S(1)}, f32[256,128]{1,0:T(8,128)S(1)}, u32[]{:S(2)}, u32[]{:S(2)}) collective-permute-start(f32[256,128]{1,0:T(8,128)S(1)} %pad_maximum_fusion), channel_id=1, source_target_pairs={{0,12},{1,13},{2,14},{3,15},{4,8},{5,9},{6,10},{7,11},{8,4},{9,5},... | collective-permute-start | bytes 393224 | tf_op jit(solution)/shard_map/ppermute | solution.py:428
  19.7 4.3 %copy-start.1 = (f32[68,64]{0,1:T(8,128)S(1)}, f32[68,64]{0,1:T(8,128)}, u32[]{:S(2)}) copy-start(f32[68,64]{0,1:T(8,128)} %param.17) | copy-start | bytes 52228
  22.8 27.3 %collective-permute-start.11 = (f32[512,128]{1,0:T(8,128)S(1)}, f32[512,128]{1,0:T(8,128)S(1)}, u32[]{:S(2)}, u32[]{:S(2)}) collective-permute-start(f32[512,128]{1,0:T(8,128)S(1)} %constant_dynamic-update-slice_fusion.mine_ref), channel_id=1, source_target_pairs={{0,1},{1,0},{2,3},{3,2},{4,5},{5,4},{6,7},{7,6},{8,9},{9,8},{10,11... | collective-permute-start | bytes 786440 | tf_op jit(solution)/shard_map/ppermute | solution.py:428
  22.9 1.8 %collective-permute-start.1 = (f32[136,128]{1,0:T(8,128)S(1)}, f32[136,128]{1,0:T(8,128)S(1)}, u32[]{:S(2)}, u32[]{:S(2)}) collective-permute-start(f32[136,128]{1,0:T(8,128)S(1)} %get-tuple-element.27), channel_id=1, source_target_pairs={{0,1},{1,0},{2,3},{3,2},{4,5},{5,4},{6,7},{7,6},{8,9},{9,8},{10,11... | collective-permute-start | bytes 208904 | tf_op jit(solution)/shard_map/ppermute | solution.py:468
  23.4 1.4 %collective-permute-start.2 = (f32[136,128]{1,0:T(8,128)S(1)}, f32[136,128]{1,0:T(8,128)S(1)}, u32[]{:S(2)}, u32[]{:S(2)}) collective-permute-start(f32[136,128]{1,0:T(8,128)S(1)} %get-tuple-element.28), channel_id=1, source_target_pairs={{1,2},{3,4},{5,6},{7,8},{9,10},{11,12},{13,14},{2,1},{4,3},{6,5},{... | collective-permute-start | bytes 208904 | tf_op jit(solution)/shard_map/ppermute | solution.py:467
  24.0 0.8 %copy-start.2 = (f32[64,128]{1,0:T(8,128)S(1)}, f32[64,128]{1,0:T(8,128)}, u32[]{:S(2)}) copy-start(f32[64,128]{1,0:T(8,128)} %constant.2.clone.table_ref) | copy-start | bytes 98308
  27.1 5.2 %collective-permute-start.3 = (f32[24,128]{1,0:T(8,128)S(1)}, f32[24,128]{1,0:T(8,128)S(1)}, u32[]{:S(2)}, u32[]{:S(2)}) collective-permute-start(f32[24,128]{1,0:T(8,128)S(1)} %get-tuple-element.33), channel_id=1, source_target_pairs={{0,1},{1,0},{2,3},{3,2},{4,5},{5,4},{6,7},{7,6},{8,9},{9,8},{10,11... | collective-permute-start | bytes 36872 | tf_op jit(solution)/shard_map/ppermute | solution.py:428
  32.2 3.7 %collective-permute-start.4 = (f32[24,128]{1,0:T(8,128)S(1)}, f32[24,128]{1,0:T(8,128)S(1)}, u32[]{:S(2)}, u32[]{:S(2)}) collective-permute-start(f32[24,128]{1,0:T(8,128)S(1)} %add.15._), channel_id=1, source_target_pairs={{0,16},{1,17},{2,18},{3,19},{4,20},{5,21},{6,22},{7,23},{8,24},{9,... | collective-permute-start | bytes 36872 | tf_op jit(solution)/shard_map/ppermute | solution.py:428
  35.9 4.3 %collective-permute-start.5 = (f32[24,128]{1,0:T(8,128)S(1)}, f32[24,128]{1,0:T(8,128)S(1)}, u32[]{:S(2)}, u32[]{:S(2)}) collective-permute-start(f32[24,128]{1,0:T(8,128)S(1)} %add.16), channel_id=1, source_target_pairs={{0,2},{1,3},{2,0},{3,1},{4,6},{5,7},{6,4},{7,5},{8,10},{9,11},{10,... | collective-permute-start | bytes 36872 | tf_op jit(solution)/shard_map/ppermute | solution.py:428
  40.2 3.9 %collective-permute-start.6 = (f32[24,128]{1,0:T(8,128)S(1)}, f32[24,128]{1,0:T(8,128)S(1)}, u32[]{:S(2)}, u32[]{:S(2)}) collective-permute-start(f32[24,128]{1,0:T(8,128)S(1)} %add.17), channel_id=1, source_target_pairs={{0,4},{1,5},{2,6},{3,7},{4,0},{5,1},{6,2},{7,3},{8,12},{9,13},{10,... | collective-permute-start | bytes 36872 | tf_op jit(solution)/shard_map/ppermute | solution.py:428
  44.1 6.0 %collective-permute-start.7 = (f32[24,128]{1,0:T(8,128)S(1)}, f32[24,128]{1,0:T(8,128)S(1)}, u32[]{:S(2)}, u32[]{:S(2)}) collective-permute-start(f32[24,128]{1,0:T(8,128)S(1)} %add.18), channel_id=1, source_target_pairs={{0,12},{1,13},{2,14},{3,15},{4,8},{5,9},{6,10},{7,11},{8,4},{9,5},... | collective-permute-start | bytes 36872 | tf_op jit(solution)/shard_map/ppermute | solution.py:428

commit v3 on v2

--- a/solution.py
+++ b/solution.py
@@ -63,34 +63,63 @@
     return jnp.concatenate([block[:half], block[half:]], axis=1)
 
 
-def edge_kernel(
-    with_momentum, v_hbm, rate_hbm, forcing_hbm, momentum_hbm, v_ref, rate_ref, forcing_ref, momentum_ref, *rest
-):
-    out_refs, sems = rest[:-1], rest[-1]
-    moves = [
-        pltpu.make_async_copy(source, target, sems.at[number])
-        for number, (source, target) in enumerate(
-            ((momentum_hbm, momentum_ref), (v_hbm, v_ref), (rate_hbm, rate_ref), (forcing_hbm, forcing_ref))
-        )
-    ]
+LAYERS = 3
+
+
+def beside_in_z(plane):
+    size = plane.shape[1]
+    return pltpu.roll(plane, 1, 1) + pltpu.roll(plane, size - 1, 1)
+
+
+def shifted(plane, before, after):
+    sublane = lax.broadcasted_iota(jnp.int32, plane.shape, 0)
+    last = plane.shape[0] - 1
+    up = jnp.where(sublane == last, after, pltpu.roll(plane, last, 0))
+    down = jnp.where(sublane == 0, before, pltpu.roll(plane, 1, 0))
+    return up, down
+
+
+def edge_kernel(with_momentum, sides, v_hbm, rate_hbm, forcing_hbm, momentum_hbm, *rest):
+    momentum_ref, planes, momentum_scratch, sems = rest[sides], *rest[-3:]
+    last = v_hbm.shape[0] - 1
+    chunks = v_hbm.shape[2] // LANES
+    moves = []
+
+    def move(source, target):
+        moves.append(pltpu.make_async_copy(source, target, sems.at[len(moves)]))
+        moves[-1].start()
+
+    highs = [lax.axis_index("grp") == 0] if sides == 1 else [True, False]
+    move(momentum_hbm, momentum_scratch)
+    for number, high in enumerate(highs):
+        edge = jnp.where(high, last, 0)
+        second = jnp.where(high, last - 1, 1)
+        for layer, (ref, at) in enumerate(((v_hbm, edge), (v_hbm, second), (rate_hbm, edge), (forcing_hbm, edge))):
+            move(ref.at[at], planes.at[4 * number + layer])
+    moves[0].wait()
+    block = momentum_scratch[...]
+    momentum_ref[...] = block
+    if with_momentum:
+        packed = pack_rows(block.T)
+        start = LAYERS * 8 * chunks
+        rest[0][start : start + packed.shape[0], :] = packed
+    for item in moves[1:]:
+        item.wait()
+    for number in range(sides):
+        edge, second, rate, forcing = (planes[4 * number + layer] for layer in range(4))
+        up, down = shifted(edge, 0.0, 0.0)
+        partial = edge + (rate * (second + up + down + beside_in_z(edge) - 6.0 * edge) + forcing)
+        for layer, plane in enumerate((edge, rate, partial)):
+            put_plane(rest[number], layer * 8 * chunks, plane)
+
+
+def stage_kernel(v_hbm, rate_hbm, forcing_hbm, v_ref, rate_ref, forcing_ref, sems):
+    pairs = ((v_hbm, v_ref), (rate_hbm, rate_ref), (forcing_hbm, forcing_ref))
+    moves = [pltpu.make_async_copy(*pair, sems.at[number]) for number, pair in enumerate(pairs)]
     for move in moves:
         move.start()
-    last = v_ref.shape[0] - 1
-    chunks = v_ref.shape[2] // LANES
-    moves[0].wait()
-    if with_momentum:
-        packed = pack_rows(momentum_ref[...].T)
-        start = 4 * 8 * chunks
-        out_refs[0][start : start + packed.shape[0], :] = packed
-    for move in moves[1:]:
+    for move in moves:
         move.wait()
-    sides = [lax.axis_index("grp") == 0] if len(out_refs) == 1 else [True, False]
-    for out_ref, high in zip(out_refs, sides):
-        edge = jnp.where(high, last, 0)
-        second = jnp.where(high, last - 1, 1)
-        planes = (v_ref[edge], v_ref[second], rate_ref[edge], forcing_ref[edge])
-        for number, plane in enumerate(planes):
-            put_plane(out_ref, number * 8 * chunks, plane)
 
 
 def grp_halo(two_sided, ref_low, ref_high, layer, chunks):
@@ -107,20 +136,24 @@
     last = v_ref.shape[1] - 1
     chunks = v_ref.shape[2] // LANES
     even = lax.rem(lax.axis_index("slab"), 2) == 0
-    columns = ((v_ref, 0), (v_ref, 1), (rate_ref, 0), (forcing_ref, 0))
-    for number, (ref, offset) in enumerate(columns):
-        left, right = ref[:, offset, :], ref[:, last - offset, :]
-        put_plane(a_ref, number * 8 * chunks, jnp.where(even, right, left))
-        put_plane(b_ref, number * 8 * chunks, jnp.where(even, left, right))
     low, high = grp_halo(two_sided, low_ref, high_ref, 0, chunks)
-    start = 4 * 8 * chunks
-    for number, plane in enumerate((low, high)):
-        left, right = plane[0:1], plane[last : last + 1]
-        to_a, to_b = jnp.where(even, right, left), jnp.where(even, left, right)
-        for q in range(chunks):
-            row = start + number * chunks + q
-            a_ref[row : row + 1, :] = to_a[:, q * LANES : (q + 1) * LANES]
-            b_ref[row : row + 1, :] = to_b[:, q * LANES : (q + 1) * LANES]
+    messages = []
+    for at, inside in ((0, 1), (last, last - 1)):
+        edge, second, rate = v_ref[:, at, :], v_ref[:, inside, :], rate_ref[:, at, :]
+        below, above = low[at : at + 1], high[at : at + 1]
+        up, down = shifted(edge, below, above)
+        beside = up + down + second + beside_in_z(edge)
+        partial = edge + (rate * (beside - 6.0 * edge) + forcing_ref[:, at, :])
+        messages.append((edge, rate, partial, below, above))
+    start = LAYERS * 8 * chunks
+    for number, (left, right) in enumerate(zip(*messages)):
+        for ref, plane in ((a_ref, jnp.where(even, right, left)), (b_ref, jnp.where(even, left, right))):
+            if number < LAYERS:
+                put_plane(ref, number * 8 * chunks, plane)
+                continue
+            for q in range(chunks):
+                row = start + (number - LAYERS) * chunks + q
+                ref[row : row + 1, :] = plane[:, q * LANES : (q + 1) * LANES]
     if packed_rows:
         outs[2][0:packed_rows, :] = own_ref[start : start + packed_rows, :]
         outs[2][packed_rows : 2 * packed_rows, :] = low_ref[start : start + packed_rows, :]
@@ -183,64 +216,50 @@
         move.start()
     cells_x, cells_y, cells_z = v_ref.shape
     chunks = cells_z // LANES
-    even = lax.rem(lax.axis_index("slab"), 2) == 0
+    slab = lax.axis_index("slab")
+    even = lax.rem(slab, 2) == 0
+    inner = jnp.logical_and(slab > 0, slab < lax.axis_size("slab") - 1)
 
     def grp_layer(layer):
         return grp_halo(two_sided, low_ref, high_ref, layer, chunks)
 
     def slab_layer(layer):
         from_a = get_plane(a_ref, 8 * chunks * layer, chunks)
-        from_b = get_plane(b_ref, 8 * chunks * layer, chunks)
+        from_b = jnp.where(inner, get_plane(b_ref, 8 * chunks * layer, chunks), 0.0)
         return jnp.where(even, from_b, from_a), jnp.where(even, from_a, from_b)
 
     def corner(number):
-        start = 4 * 8 * chunks + number * chunks
+        start = LAYERS * 8 * chunks + number * chunks
         from_a = jnp.concatenate([a_ref[start + q : start + q + 1, :] for q in range(chunks)], axis=1)
         from_b = jnp.concatenate([b_ref[start + q : start + q + 1, :] for q in range(chunks)], axis=1)
+        from_b = jnp.where(inner, from_b, 0.0)
         return jnp.where(even, from_b, from_a), jnp.where(even, from_a, from_b)
 
-    sublane = lax.broadcasted_iota(jnp.int32, (8, cells_z), 0)
-
-    def shifted(plane, before, after):
-        up = jnp.where(sublane == 7, after, pltpu.roll(plane, 7, 0))
-        down = jnp.where(sublane == 0, before, pltpu.roll(plane, 1, 0))
-        return up, down
-
     def tendency(plane, above, below, up, down, rate, forcing):
-        beside = above + below + up + down
-        beside = beside + pltpu.roll(plane, 1, 1) + pltpu.roll(plane, cells_z - 1, 1)
+        beside = above + below + up + down + beside_in_z(plane)
         return rate * (beside - 6.0 * plane) + forcing
 
-    low1, high1 = grp_layer(0)
-    low2, high2 = grp_layer(1)
-    low_rate, high_rate = grp_layer(2)
-    low_force, high_force = grp_layer(3)
-    left1, right1 = slab_layer(0)
-    left2, right2 = slab_layer(1)
-    left_rate, right_rate = slab_layer(2)
-    left_force, right_force = slab_layer(3)
-    low_left, low_right = corner(0)
-    high_left, high_right = corner(1)
-
-    planes = [low2, low1] + [v_ref[i] for i in range(cells_x)] + [high1, high2]
-    rates = [low_rate] + [rate_ref[i] for i in range(cells_x)] + [high_rate]
-    forces = [low_force] + [forcing_ref[i] for i in range(cells_x)] + [high_force]
-    lefts = [low_left] + [left1[i : i + 1] for i in range(cells_x)] + [high_left]
-    rights = [low_right] + [right1[i : i + 1] for i in range(cells_x)] + [high_right]
-    stepped = []
-    for i in range(cells_x + 2):
+    low, high = grp_layer(0)
+    low_rate, high_rate = grp_layer(1)
+    low_part, high_part = grp_layer(2)
+    left, right = slab_layer(0)
+    left_rate, right_rate = slab_layer(1)
+    left_part, right_part = slab_layer(2)
+    sublane = lax.broadcasted_iota(jnp.int32, (cells_y, cells_z), 0)
+
+    def halo_step(part, rate, inner, corners):
+        at_ends = jnp.where(sublane == 0, corners[0], jnp.where(sublane == cells_y - 1, corners[1], 0.0))
+        return part + rate * (inner + at_ends)
+
+    planes = [low] + [v_ref[i] for i in range(cells_x)] + [high]
+    stepped = [halo_step(low_part, low_rate, planes[1], corner(0))]
+    for i in range(cells_x):
         plane = planes[i + 1]
-        up, down = shifted(plane, lefts[i], rights[i])
-        stepped.append(plane + tendency(plane, planes[i + 2], planes[i], up, down, rates[i], forces[i]))
-
-    def column_step(near, far, inner, rate, forcing, low, high):
-        above, below = shifted(near, low, high)
-        return near + tendency(near, above, below, inner, far, rate, forcing)
-
-    left_inner = v_ref[:, 0, :]
-    right_inner = v_ref[:, cells_y - 1, :]
-    left_new = column_step(left1, left2, left_inner, left_rate, left_force, low_left, high_left)
-    right_new = column_step(right1, right2, right_inner, right_rate, right_force, low_right, high_right)
+        up, down = shifted(plane, left[i : i + 1], right[i : i + 1])
+        stepped.append(plane + tendency(plane, planes[i + 2], planes[i], up, down, rate_ref[i], forcing_ref[i]))
+    stepped.append(halo_step(high_part, high_rate, planes[cells_x], corner(1)))
+    left_new = left_part + left_rate * v_ref[:, 0, :]
+    right_new = right_part + right_rate * v_ref[:, cells_y - 1, :]
     for i in range(cells_x):
         plane = stepped[i + 1]
         up, down = shifted(plane, left_new[i : i + 1], right_new[i : i + 1])
@@ -323,7 +342,6 @@
 
 def base_kernel(masks, width, spectral_ref, mine_ref, other_ref, out_ref):
     here = lax.axis_index("grp") * lax.axis_size("slab") + lax.axis_index("slab")
-    even = lax.rem(here, 2) == 0
     rows = width // 2
     low = lax.broadcasted_iota(jnp.int32, (rows, LANES), 1) < width
     for number in range(mine_ref.shape[0] // rows):
@@ -331,6 +349,7 @@
         for bit, mask in enumerate(masks):
             if number >> bit & 1:
                 source = source ^ mask
+        even = lax.rem(source, 2) == 0
         columns = pl.ds(pl.multiple_of((source // 2) * LANES, LANES), LANES)
         mine = mine_ref[number * rows : (number + 1) * rows, :]
         other = other_ref[number * rows : (number + 1) * rows, :]
@@ -344,7 +363,7 @@
 
 def update_kernel(
     width, lines, groups, pay_ref, spectral_ref, base_ref, dense_ref, momentum_ref, row_ref,
-    spectral_hbm, dense_out, momentum_out, loss_out, square, result, sems,
+    spectral_hbm, dense_hbm, momentum_hbm, loss_hbm, square, result, dense_out, momentum_out, loss_out, sems,
 ):
     first, second = lax.axis_index("grp"), lax.axis_index("slab")
     here = first * lax.axis_size("slab") + second
@@ -362,32 +381,12 @@
     by_output = turned[:, 2 * MODES + 2 : 2 * MODES + 3]
     lane = lax.broadcasted_iota(jnp.int32, (width, LANES), 1)
     low = lane < width
-    gathered = jnp.zeros((width, LANES), jnp.float32)
     copies = []
-    for pair in range(MODES):
-        span = slice(pair * LANES, (pair + 1) * LANES)
-        column = jnp.where(low, turned[:, 2 * pair : 2 * pair + 1], turned[:, 2 * pair + 1 : 2 * pair + 2])
-        gradient = gains * column
-        if pair == 0:
-            gradient = gradient + jnp.where(low, biases * by_one, 0.0)
-        result[:, span] = base_ref[:, span] - learn_rate * gradient
-        gathered = gathered + spectral_ref[:, span] * column
-        if (pair + 1) % (MODES // groups) == 0:
-            number = len(copies)
-            part = pl.ds(number * (MODES // groups) * LANES, (MODES // groups) * LANES)
-            copies.append(pltpu.make_async_copy(result.at[:, part], spectral_hbm.at[:, part], sems.at[number]))
-            copies[-1].start()
-    mixing = dense_ref[:, 0:width]
-    gain_row = jnp.sum(gathered, axis=0, keepdims=True)
-    gain_row = gain_row[:, 0:width] + gain_row[:, width:] + jnp.sum(mixing * by_input, axis=0, keepdims=True)
-    bias_row = jnp.sum((mixing + spectral_ref[:, 0:width]) * by_one, axis=0, keepdims=True)
-    dense_out[:, 0:width] = mixing - dense_rate * (gains[:, 0:width] * by_input + biases[:, 0:width] * by_one)
-    tail = dense_ref[:, width : width + 4]
-    lane4 = lax.broadcasted_iota(jnp.int32, (width, 4), 1)
-    change = jnp.where(
-        lane4 == 0, as_column(gain_row), jnp.where(
-            lane4 == 1, as_column(bias_row), jnp.where(lane4 == 2, by_one, by_output)))
-    dense_out[:, width : width + 4] = tail - dense_rate * change
+
+    def send(source, target):
+        copies.append(pltpu.make_async_copy(source, target, sems.at[len(copies)]))
+        copies[-1].start()
+
     piece = momentum_ref.shape[0]
     block = here * piece // width
     inside = here * piece - block * width
@@ -400,24 +399,45 @@
     gradient = square[at, 0:1] * row
     gradient = gradient + jnp.where(block == 0, square[at, width : width + 1] * slopes[0:1, width : 2 * width], 0.0)
     momentum_out[...] = decay_rate * momentum_ref[...] + gradient
+    send(momentum_out, momentum_hbm)
     sums = pay_ref[pl.ds(MODES + 2 + first, 1), :]
-    lane = lax.broadcasted_iota(jnp.int32, (1, LANES), 1)
-    own = jnp.sum(jnp.where(lane == second, sums, 0.0), axis=1, keepdims=True)
+    lane1 = lax.broadcasted_iota(jnp.int32, (1, LANES), 1)
+    own = jnp.sum(jnp.where(lane1 == second, sums, 0.0), axis=1, keepdims=True)
     loss_out[...] = own * (1.0 / (lines * SUB))
+    send(loss_out, loss_hbm)
+    gathered = jnp.zeros((width, LANES), jnp.float32)
+    for pair in range(MODES):
+        span = slice(pair * LANES, (pair + 1) * LANES)
+        column = jnp.where(low, turned[:, 2 * pair : 2 * pair + 1], turned[:, 2 * pair + 1 : 2 * pair + 2])
+        gradient = gains * column
+        if pair == 0:
+            gradient = gradient + jnp.where(low, biases * by_one, 0.0)
+        result[:, span] = base_ref[:, span] - learn_rate * gradient
+        gathered = gathered + spectral_ref[:, span] * column
+        if (pair + 1) % (MODES // groups) == 0:
+            many = (MODES // groups) * LANES
+            part = pl.ds((pair + 1) * LANES - many, many)
+            send(result.at[:, part], spectral_hbm.at[:, part])
+    mixing = dense_ref[:, 0:width]
+    gain_row = jnp.sum(gathered, axis=0, keepdims=True)
+    gain_row = gain_row[:, 0:width] + gain_row[:, width:] + jnp.sum(mixing * by_input, axis=0, keepdims=True)
+    bias_row = jnp.sum((mixing + spectral_ref[:, 0:width]) * by_one, axis=0, keepdims=True)
+    dense_out[:, 0:width] = mixing - dense_rate * (gains[:, 0:width] * by_input + biases[:, 0:width] * by_one)
+    tail = dense_ref[:, width : width + 4]
+    lane4 = lax.broadcasted_iota(jnp.int32, (width, 4), 1)
+    change = jnp.where(
+        lane4 == 0, as_column(gain_row), jnp.where(
+            lane4 == 1, as_column(bias_row), jnp.where(lane4 == 2, by_one, by_output)))
+    dense_out[:, width : width + 4] = tail - dense_rate * change
+    send(dense_out, dense_hbm)
     for copy in copies:
         copy.wait()
 
 
 def hop_masks(n_grp, n_slab):
-    masks, bit = [], 0
-    while 1 << bit < n_slab:
-        masks.append(3 << (bit - 1) if bit > 2 and bit % 2 else 1 << bit)
-        bit += 1
-    bit = 1
-    while bit < n_grp:
-        masks.append(bit * n_slab)
-        bit *= 2
-    return masks
+    slab_bits = [1 << bit for bit in range(n_slab.bit_length() - 1)]
+    grp_bits = [n_slab << bit for bit in range(n_grp.bit_length() - 1)]
+    return [1] + [mask + 1 for mask in grp_bits + slab_bits[1:2] + slab_bits[:1:-1]]
 
 
 def in_hbm(array):
@@ -433,9 +453,9 @@
     devices = n_grp * n_slab
     width = dense.shape[1]
     lines = anchor_line.shape[0]
-    cells_x, _, cells_z = velocity.shape
+    cells_x, cells_y, cells_z = velocity.shape
     chunks = cells_z // LANES
-    halo_rows = 4 * 8 * chunks
+    halo_rows = LAYERS * 8 * chunks
     piece = momentum.shape[0]
     packed = piece // 2
     f32 = jnp.float32
@@ -444,14 +464,22 @@
     table = jnp.asarray(tables())
     spectral, dense = spectral.T, dense.T
 
+    sides = 2 if two_sided else 1
     edge_rows = halo_rows + (packed if joined else 0)
-    velocity, rate, forcing, near_momentum, *edges = call(
-        functools.partial(edge_kernel, joined),
-        [(velocity.shape, f32)] * 3 + [(momentum.shape, f32)]
-        + [((edge_rows, LANES), f32)] * (2 if two_sided else 1),
-        scratch=[pltpu.SemaphoreType.DMA((4,))],
+    blocks = [in_hbm(array) for array in (velocity, rate, forcing)]
+    *edges, near_momentum = call(
+        functools.partial(edge_kernel, joined, sides),
+        [((edge_rows, LANES), f32)] * sides + [(momentum.shape, f32)],
+        scratch=[
+            pltpu.VMEM((4 * sides, cells_y, cells_z), f32),
+            pltpu.VMEM(momentum.shape, f32),
+            pltpu.SemaphoreType.DMA((1 + 4 * sides,)),
+        ],
         ins=[HBM] * 4,
-    )(*(in_hbm(array) for array in (velocity, rate, forcing, momentum)))
+    )(*blocks, in_hbm(momentum))
+    velocity, rate, forcing = call(
+        stage_kernel, [(velocity.shape, f32)] * 3, scratch=[pltpu.SemaphoreType.DMA((3,))], ins=[HBM] * 3
+    )(*blocks)
     if two_sided:
         low = lax.ppermute(edges[0], "grp", [(i, i + 1) for i in range(n_grp - 1)])
         high = lax.ppermute(edges[1], "grp", [(i + 1, i) for i in range(n_grp - 1)])
@@ -463,7 +491,7 @@
         functools.partial(side_kernel, two_sided, packed if joined else 0), outs, ins=[VMEM] * 6
     )(velocity, rate, forcing, low, high, edges[0])
     pairs = [(i, i ^ 1) for i in range(n_slab)]
-    odd = [(i, i + 1) for i in range(1, n_slab - 1, 2)]
+    odd = [(i, (i + 1) % n_slab) for i in range(1, n_slab, 2)]
     from_b = lax.ppermute(to_b, "slab", odd + [(j, i) for i, j in odd])
     from_a = lax.ppermute(to_a, "slab", pairs)
     channel_map, projection, rows = call(
@@ -491,7 +519,7 @@
     masks = hop_masks(n_grp, n_slab)
     if joined:
         mine = gathered[0]
-        order = [n_slab] + [m for m in masks if m not in (1, n_slab)] + [1]
+        order = [n_slab] + masks[3:] + masks[2:3] + [1]
         for mask in order[1:-1]:
             other = swap(mine, mask, devices)
             mine = jnp.concatenate([mine, other], axis=0)
@@ -499,7 +527,6 @@
         base = call(
             functools.partial(base_kernel, order[:-1], width), [(spectral.shape, f32)], ins=[VMEM] * 3
         )(spectral, mine, other)[0]
-        masks = [1, n_slab] + [m for m in masks if m not in (1, n_slab)]
     else:
         whole = lax.all_gather(momentum, AXES, axis=0, tiled=True)
         base = spectral - (learn_rate * decay_rate) * whole.T
@@ -516,9 +543,12 @@
     spectral_new, dense_new, momentum_new, trainer_loss = call(
         functools.partial(update_kernel, width, lines, groups),
         [(spectral.shape, f32), (dense.shape, f32), (momentum.shape, f32), ((1, 1), f32)],
-        scratch=[pltpu.VMEM((LANES, LANES), f32), pltpu.VMEM(spectral.shape, f32), pltpu.SemaphoreType.DMA((groups,))],
+        scratch=[
+            pltpu.VMEM((LANES, LANES), f32), pltpu.VMEM(spectral.shape, f32), pltpu.VMEM(dense.shape, f32),
+            pltpu.VMEM(momentum.shape, f32), pltpu.VMEM((1, 1), f32), pltpu.SemaphoreType.DMA((groups + 3,)),
+        ],
         ins=[VMEM] * 6,
-        places=[HBM, VMEM, VMEM, VMEM],
+        places=[HBM] * 4,
     )(payload, spectral, base, dense, near_momentum, rows)
     return (field_now, trainer_loss, spectral_new.T, dense_new.T, momentum_new)
 

time: 52.4 us -> 47.2 us (0.901)
  starting transfers between devices: 27.7 us -> 16 us
  waiting for transfers between devices: 16.8 us -> 22.5 us
  Pallas kernels: 6.79 us -> 7.68 us
    ppermute x9, starting transfers between devices: 23.4 us -> 8.71 us  [swap(): return lax.ppermute(array, AXES, [(i, i ^ mask) for i in range(count)])]
    ppermute x9, waiting for transfers between devices: 14.4 us -> 19.7 us  [swap(): return lax.ppermute(array, AXES, [(i, i ^ mask) for i in range(count)])]
    ppermute x1, starting transfers between devices: 0.65 us -> 4.02 us  [local(): from_b = lax.ppermute(to_b, 'slab', odd + [(j, i) for i, j in odd])]
    ppermute x1, waiting for transfers between devices: 0.01 us -> 1.58 us  [local(): from_b = lax.ppermute(to_b, 'slab', odd + [(j, i) for i, j in odd])]
    ppermute x1, waiting for transfers between devices: 2.44 us -> 1.18 us  [local(): low = high = lax.ppermute(edges[0], 'grp', [(0, 1), (1, 0)])]
    pallas_call x1 -> x2, Pallas kernels: 1.09 us -> 2.1 us  [the longest x1 1.05 us: local(): call(stage_kernel, [(velocity.shape, f32)] * 3, scratch=[pltpu.SemaphoreT...]
  transfers between devices with their start and end apart: 12 -> 12, of which waited for: 9 -> 10; matrix products, arithmetic and copies ran while one was open for 0% -> 0% of each run, Pallas kernels for 7% -> 10%
where the time goes in v3:
time: 47.2 us; the launch traced here: 47 us
  waiting for transfers between devices  22.5 us (48%)
  starting transfers between devices  16 us (34%)
  Pallas kernels  7.68 us (16%)
  between operations  0.73 us (2%)
    ppermute x9, waiting for transfers between devices, swap(): return lax.ppermute(array, AXES, [(i, i ^ mask) for i in range(count)])  19.7 us
    ppermute x9, starting transfers between devices, swap(): return lax.ppermute(array, AXES, [(i, i ^ mask) for i in range(count)])  8.71 us
    ppermute x1, starting transfers between devices, local(): from_b = lax.ppermute(to_b, 'slab', odd + [(j, i) for i, j in odd])  4.02 us
    ppermute x1, starting transfers between devices, local(): low = high = lax.ppermute(edges[0], 'grp', [(0, 1), (1, 0)])  3.06 us
    pallas_call x1, Pallas kernels, local(): call(functools.partial(step_kernel, two_sided, width, scale), [window, wi...  2.41 us
    ppermute x1, waiting for transfers between devices, local(): from_b = lax.ppermute(to_b, 'slab', odd + [(j, i) for i, j in odd])  1.58 us
    pallas_call x1, Pallas kernels, local(): call(functools.partial(update_kernel, width, lines, groups), [(spectral.s...  1.54 us
    ppermute x1, waiting for transfers between devices, local(): low = high = lax.ppermute(edges[0], 'grp', [(0, 1), (1, 0)])  1.18 us
  transfers between devices with their start and end apart: 12, of which 10 were waited for; matrix products, arithmetic and copies ran while one was open for 0% of the time, Pallas kernels for 10%

profile of v3, /device:TPU:0, one launch (start us, length us, event | category | flops | bytes accessed | tf_op | source)
XLA Modules:
  0.0 47.0 jit_solution(13687922620391577843)
XLA Ops:
  0.6 1.0 %shard_map.138 = (f32[128,128]{1,0:T(8,128)S(1)}, f32[64,64]{1,0:T(8,128)S(1)}) custom-call(f32[8,8,512]{2,1,0:T(8,128)} %v_hbm.3, f32[8,8,512]{2,1,0:T(8,128)} %rate_hbm.3, f32[8,8,512]{2,1,0:T(8,128)} %forcing_hbm.3, f32[64,64]{1,0:T(8,128)} %momentum_hbm.1), custom_call_target="tpu_custom_call" | custom-call | flops 1000000 | bytes 163840 | tf_op jit(solution)/shard_map/pallas_call | solution.py:470
  1.7 3.1 %collective-permute-start = (f32[128,128]{1,0:T(8,128)S(1)}, f32[128,128]{1,0:T(8,128)S(1)}, u32[]{:S(2)}, u32[]{:S(2)}) collective-permute-start(f32[128,128]{1,0:T(8,128)S(1)} %get-tuple-element.26.own_ref), channel_id=1, source_target_pairs={{0,16},{16,0},{1,17},{17,1},{2,18},{18,2},{3,19},{19,3},{4,20},{20... | collective-permute-start | bytes 196616 | tf_op jit(solution)/shard_map/ppermute | solution.py:487
  4.7 1.1 %shard_map.137 = (f32[8,8,512]{2,1,0:T(8,128)S(1)}, f32[8,8,512]{2,1,0:T(8,128)S(1)}, f32[8,8,512]{2,1,0:T(8,128)S(1)}) custom-call(f32[8,8,512]{2,1,0:T(8,128)} %v_hbm.3, f32[8,8,512]{2,1,0:T(8,128)} %rate_hbm.3, f32[8,8,512]{2,1,0:T(8,128)} %forcing_hbm.3), custom_call_target="tpu_custom_call" | custom-call | flops 1000000 | bytes 786432 | tf_op jit(solution)/shard_map/pallas_call | solution.py:480
  5.8 1.2 %collective-permute-done.low_ref.high_ref = f32[128,128]{1,0:T(8,128)S(1)} collective-permute-done((f32[128,128]{1,0:T(8,128)S(1)}, f32[128,128]{1,0:T(8,128)S(1)}, u32[]{:S(2)}, u32[]{:S(2)}) %collective-permute-start) | collective-permute-done | bytes 65568 | tf_op jit(solution)/shard_map/ppermute | solution.py:487
  7.0 0.1 shard_map.139
  7.1 0.0 copy-start
  7.1 1.4 %collective-permute-start.8 = (f32[64,128]{1,0:T(8,128)S(1)}, f32[64,128]{1,0:T(8,128)S(1)}, u32[]{:S(2)}, u32[]{:S(2)}) collective-permute-start(f32[64,128]{1,0:T(8,128)S(1)} %get-tuple-element.34), channel_id=1, source_target_pairs={{0,9},{1,8},{2,11},{3,10},{4,13},{5,12},{6,15},{7,14},{8,1},{9,0},... | collective-permute-start | bytes 98312 | tf_op jit(solution)/shard_map/ppermute | solution.py:448
  8.6 2.9 %collective-permute-done.8 = f32[64,128]{1,0:T(8,128)S(1)} collective-permute-done((f32[64,128]{1,0:T(8,128)S(1)}, f32[64,128]{1,0:T(8,128)S(1)}, u32[]{:S(2)}, u32[]{:S(2)}) %collective-permute-start.8) | collective-permute-done | bytes 32800 | tf_op jit(solution)/shard_map/ppermute | solution.py:448
  11.4 1.9 %collective-permute-start.9 = (f32[128,128]{1,0:T(8,128)S(1)}, f32[128,128]{1,0:T(8,128)S(1)}, u32[]{:S(2)}, u32[]{:S(2)}) collective-permute-start(f32[128,128]{1,0:T(8,128)S(1)} %pad_maximum_fusion.1), channel_id=1, source_target_pairs={{0,5},{1,4},{2,7},{3,6},{4,1},{5,0},{6,3},{7,2},{8,13},{9,12},{10,... | collective-permute-start | bytes 196616 | tf_op jit(solution)/shard_map/ppermute | solution.py:448
  13.3 2.2 %collective-permute-done.9 = f32[128,128]{1,0:T(8,128)S(1)} collective-permute-done((f32[128,128]{1,0:T(8,128)S(1)}, f32[128,128]{1,0:T(8,128)S(1)}, u32[]{:S(2)}, u32[]{:S(2)}) %collective-permute-start.9) | collective-permute-done | bytes 65568 | tf_op jit(solution)/shard_map/ppermute | solution.py:448
  15.5 1.9 %collective-permute-start.10 = (f32[256,128]{1,0:T(8,128)S(1)}, f32[256,128]{1,0:T(8,128)S(1)}, u32[]{:S(2)}, u32[]{:S(2)}) collective-permute-start(f32[256,128]{1,0:T(8,128)S(1)} %pad_maximum_fusion), channel_id=1, source_target_pairs={{0,3},{1,2},{2,1},{3,0},{4,7},{5,6},{6,5},{7,4},{8,11},{9,10},{10,... | collective-permute-start | bytes 393224 | tf_op jit(solution)/shard_map/ppermute | solution.py:448
  17.4 0.0 copy-start.1
  17.4 3.6 %collective-permute-done.10 = f32[256,128]{1,0:T(8,128)S(1)} collective-permute-done((f32[256,128]{1,0:T(8,128)S(1)}, f32[256,128]{1,0:T(8,128)S(1)}, u32[]{:S(2)}, u32[]{:S(2)}) %collective-permute-start.10) | collective-permute-done | bytes 131104 | tf_op jit(solution)/shard_map/ppermute | solution.py:448
  21.0 0.3 collective-permute-start.11
  21.4 0.2 collective-permute-start.1
  21.6 4.0 %collective-permute-start.2 = (f32[104,128]{1,0:T(8,128)S(1)}, f32[104,128]{1,0:T(8,128)S(1)}, u32[]{:S(2)}, u32[]{:S(2)}) collective-permute-start(f32[104,128]{1,0:T(8,128)S(1)} %get-tuple-element.28), channel_id=1, source_target_pairs={{1,2},{3,4},{5,6},{7,8},{9,10},{11,12},{13,14},{15,0},{2,1},{4,3},... | collective-permute-start | bytes 159752 | tf_op jit(solution)/shard_map/ppermute | solution.py:495
  25.6 0.0 copy-done
  25.6 0.0 copy-done.1
  25.6 0.0 copy-start.2
  25.6 0.6 %shard_map.140 = (bf16[64,128]{1,0:T(8,128)(2,1)S(1)}, f32[64,128]{1,0:T(8,128)S(1)}, f32[8,128]{1,0:T(8,128)S(1)}) custom-call(f32[64,2048]{1,0:T(8,128)S(1)} %bitcast.5, f32[64,68]{1,0:T(8,128)S(1)} %bitcast.8), custom_call_target="tpu_custom_call" | custom-call | flops 1000000 | bytes 106496 | tf_op jit(solution)/shard_map/pallas_call | solution.py:497
  26.3 0.0 collective-permute-done.1.a_ref
  26.3 1.6 %collective-permute-done.2.b_ref = f32[104,128]{1,0:T(8,128)S(1)} collective-permute-done((f32[104,128]{1,0:T(8,128)S(1)}, f32[104,128]{1,0:T(8,128)S(1)}, u32[]{:S(2)}, u32[]{:S(2)}) %collective-permute-start.2) | collective-permute-done | bytes 53280 | tf_op jit(solution)/shard_map/ppermute | solution.py:495
  27.9 0.0 copy-done.2
  27.9 2.4 %shard_map.141 = (f32[64,640]{1,0:T(8,128)S(1)}, f32[64,640]{1,0:T(8,128)S(1)}, f32[24,128]{1,0:T(8,128)S(1)}) custom-call(f32[8,8,512]{2,1,0:T(8,128)S(1)} %get-tuple-element.23.v_ref, f32[8,8,512]{2,1,0:T(8,128)S(1)} %get-tuple-element.24.rate_ref, f32[8,8,512]{2,1,0:T(8,128)S(1)} %get-tuple-element.25.forcing_ref, ...), custom_call_target="tpu_custom_call" | custom-call | flops 1000000 | bytes 679936 | tf_op jit(solution)/shard_map/pallas_call | solution.py:505
  30.3 0.1 collective-permute-start.3
  30.4 1.2 %collective-permute-done.3 = f32[24,128]{1,0:T(8,128)S(1)} collective-permute-done((f32[24,128]{1,0:T(8,128)S(1)}, f32[24,128]{1,0:T(8,128)S(1)}, u32[]{:S(2)}, u32[]{:S(2)}) %collective-permute-start.3) | collective-permute-done | bytes 12320 | tf_op jit(solution)/shard_map/ppermute | solution.py:448
  31.5 2.0 %collective-permute-start.4 = (f32[24,128]{1,0:T(8,128)S(1)}, f32[24,128]{1,0:T(8,128)S(1)}, u32[]{:S(2)}, u32[]{:S(2)}) collective-permute-start(f32[24,128]{1,0:T(8,128)S(1)} %add.15._), channel_id=1, source_target_pairs={{0,17},{1,16},{2,19},{3,18},{4,21},{5,20},{6,23},{7,22},{8,25},{9,... | collective-permute-start | bytes 36872 | tf_op jit(solution)/shard_map/ppermute | solution.py:448
  33.5 1.4 %collective-permute-done.4 = f32[24,128]{1,0:T(8,128)S(1)} collective-permute-done((f32[24,128]{1,0:T(8,128)S(1)}, f32[24,128]{1,0:T(8,128)S(1)}, u32[]{:S(2)}, u32[]{:S(2)}) %collective-permute-start.4) | collective-permute-done | bytes 12320 | tf_op jit(solution)/shard_map/ppermute | solution.py:448
  34.9 0.0 collective-permute-start.5
  34.9 3.1 %collective-permute-done.5 = f32[24,128]{1,0:T(8,128)S(1)} collective-permute-done((f32[24,128]{1,0:T(8,128)S(1)}, f32[24,128]{1,0:T(8,128)S(1)}, u32[]{:S(2)}, u32[]{:S(2)}) %collective-permute-start.5) | collective-permute-done | bytes 12320 | tf_op jit(solution)/shard_map/ppermute | solution.py:448
  38.0 0.8 %collective-permute-start.6 = (f32[24,128]{1,0:T(8,128)S(1)}, f32[24,128]{1,0:T(8,128)S(1)}, u32[]{:S(2)}, u32[]{:S(2)}) collective-permute-start(f32[24,128]{1,0:T(8,128)S(1)} %add.17), channel_id=1, source_target_pairs={{0,9},{1,8},{2,11},{3,10},{4,13},{5,12},{6,15},{7,14},{8,1},{9,0},... | collective-permute-start | bytes 36872 | tf_op jit(solution)/shard_map/ppermute | solution.py:448
  38.9 3.2 %collective-permute-done.6 = f32[24,128]{1,0:T(8,128)S(1)} collective-permute-done((f32[24,128]{1,0:T(8,128)S(1)}, f32[24,128]{1,0:T(8,128)S(1)}, u32[]{:S(2)}, u32[]{:S(2)}) %collective-permute-start.6) | collective-permute-done | bytes 12320 | tf_op jit(solution)/shard_map/ppermute | solution.py:448
  42.1 0.2 collective-permute-start.7
  42.3 0.7 %shard_map.142 = f32[8,8,512]{2,1,0:T(8,128)} custom-call(f32[64,640]{1,0:T(8,128)S(1)} %get-tuple-element.31.previous, f32[64,640]{1,0:T(8,128)S(1)} %get-tuple-element.32.change, f32[24,128]{1,0:T(8,128)S(1)} %add.15._), custom_call_target="tpu_custom_call" | custom-call | flops 1000000 | bytes 262144 | tf_op jit(solution)/shard_map/pallas_call | solution.py:541
  43.0 2.2 %collective-permute-done.7 = f32[24,128]{1,0:T(8,128)S(1)} collective-permute-done((f32[24,128]{1,0:T(8,128)S(1)}, f32[24,128]{1,0:T(8,128)S(1)}, u32[]{:S(2)}, u32[]{:S(2)}) %collective-permute-start.7) | collective-permute-done | bytes 12320 | tf_op jit(solution)/shard_map/ppermute | solution.py:448
  45.2 0.0 collective-permute-done.11.other_ref
  45.2 0.2 shard_map.143.base_ref
  45.4 1.5 %shard_map.144 = (f32[64,2048]{1,0:T(8,128)}, f32[64,68]{1,0:T(8,128)}, f32[64,64]{1,0:T(8,128)}, f32[1,1]{1,0:T(1,128)}) custom-call(f32[24,128]{1,0:T(8,128)S(1)} %add.19.pay_ref, f32[64,2048]{1,0:T(8,128)S(1)} %bitcast.7, f32[64,2048]{1,0:T(8,128)S(1)} %shard_map.143.base_ref, f32[64,68]{1,0:T(8,128)S(1)} %bitcast.9, ...), custom_call_target="tpu_custom_call" | custom-call | flops 1000000 | bytes 1116168 | tf_op jit(solution)/shard_map/pallas_call | solution.py:543
  (11 shorter events, 0.1 us)
Async XLA Ops:
  1.7 5.3 %collective-permute-start = (f32[128,128]{1,0:T(8,128)S(1)}, f32[128,128]{1,0:T(8,128)S(1)}, u32[]{:S(2)}, u32[]{:S(2)}) collective-permute-start(f32[128,128]{1,0:T(8,128)S(1)} %get-tuple-element.26.own_ref), channel_id=1, source_target_pairs={{0,16},{16,0},{1,17},{17,1},{2,18},{18,2},{3,19},{19,3},{4,20},{20... | collective-permute-start | bytes 196616 | tf_op jit(solution)/shard_map/ppermute | solution.py:487
  7.1 18.5 %copy-start = (f32[2048,64]{0,1:T(8,128)S(1)}, f32[2048,64]{0,1:T(8,128)}, u32[]{:S(2)}) copy-start(f32[2048,64]{0,1:T(8,128)} %param.16) | copy-start | bytes 1572868
  7.1 4.3 %collective-permute-start.8 = (f32[64,128]{1,0:T(8,128)S(1)}, f32[64,128]{1,0:T(8,128)S(1)}, u32[]{:S(2)}, u32[]{:S(2)}) collective-permute-start(f32[64,128]{1,0:T(8,128)S(1)} %get-tuple-element.34), channel_id=1, source_target_pairs={{0,9},{1,8},{2,11},{3,10},{4,13},{5,12},{6,15},{7,14},{8,1},{9,0},... | collective-permute-start | bytes 98312 | tf_op jit(solution)/shard_map/ppermute | solution.py:448
  11.4 4.1 %collective-permute-start.9 = (f32[128,128]{1,0:T(8,128)S(1)}, f32[128,128]{1,0:T(8,128)S(1)}, u32[]{:S(2)}, u32[]{:S(2)}) collective-permute-start(f32[128,128]{1,0:T(8,128)S(1)} %pad_maximum_fusion.1), channel_id=1, source_target_pairs={{0,5},{1,4},{2,7},{3,6},{4,1},{5,0},{6,3},{7,2},{8,13},{9,12},{10,... | collective-permute-start | bytes 196616 | tf_op jit(solution)/shard_map/ppermute | solution.py:448
  15.5 5.5 %collective-permute-start.10 = (f32[256,128]{1,0:T(8,128)S(1)}, f32[256,128]{1,0:T(8,128)S(1)}, u32[]{:S(2)}, u32[]{:S(2)}) collective-permute-start(f32[256,128]{1,0:T(8,128)S(1)} %pad_maximum_fusion), channel_id=1, source_target_pairs={{0,3},{1,2},{2,1},{3,0},{4,7},{5,6},{6,5},{7,4},{8,11},{9,10},{10,... | collective-permute-start | bytes 393224 | tf_op jit(solution)/shard_map/ppermute | solution.py:448
  17.4 8.2 %copy-start.1 = (f32[68,64]{0,1:T(8,128)S(1)}, f32[68,64]{0,1:T(8,128)}, u32[]{:S(2)}) copy-start(f32[68,64]{0,1:T(8,128)} %param.17) | copy-start | bytes 52228
  21.0 24.2 %collective-permute-start.11 = (f32[512,128]{1,0:T(8,128)S(1)}, f32[512,128]{1,0:T(8,128)S(1)}, u32[]{:S(2)}, u32[]{:S(2)}) collective-permute-start(f32[512,128]{1,0:T(8,128)S(1)} %constant_dynamic-update-slice_fusion.mine_ref), channel_id=1, source_target_pairs={{0,1},{1,0},{2,3},{3,2},{4,5},{5,4},{6,7},{7,6},{8,9},{9,8},{10,11... | collective-permute-start | bytes 786440 | tf_op jit(solution)/shard_map/ppermute | solution.py:448
  21.4 4.9 %collective-permute-start.1 = (f32[104,128]{1,0:T(8,128)S(1)}, f32[104,128]{1,0:T(8,128)S(1)}, u32[]{:S(2)}, u32[]{:S(2)}) collective-permute-start(f32[104,128]{1,0:T(8,128)S(1)} %get-tuple-element.27), channel_id=1, source_target_pairs={{0,1},{1,0},{2,3},{3,2},{4,5},{5,4},{6,7},{7,6},{8,9},{9,8},{10,11... | collective-permute-start | bytes 159752 | tf_op jit(solution)/shard_map/ppermute | solution.py:496
  21.6 6.3 %collective-permute-start.2 = (f32[104,128]{1,0:T(8,128)S(1)}, f32[104,128]{1,0:T(8,128)S(1)}, u32[]{:S(2)}, u32[]{:S(2)}) collective-permute-start(f32[104,128]{1,0:T(8,128)S(1)} %get-tuple-element.28), channel_id=1, source_target_pairs={{1,2},{3,4},{5,6},{7,8},{9,10},{11,12},{13,14},{15,0},{2,1},{4,3},... | collective-permute-start | bytes 159752 | tf_op jit(solution)/shard_map/ppermute | solution.py:495
  25.6 2.2 %copy-start.2 = (f32[64,128]{1,0:T(8,128)S(1)}, f32[64,128]{1,0:T(8,128)}, u32[]{:S(2)}) copy-start(f32[64,128]{1,0:T(8,128)} %constant.2.clone.table_ref) | copy-start | bytes 98308
  30.3 1.2 %collective-permute-start.3 = (f32[24,128]{1,0:T(8,128)S(1)}, f32[24,128]{1,0:T(8,128)S(1)}, u32[]{:S(2)}, u32[]{:S(2)}) collective-permute-start(f32[24,128]{1,0:T(8,128)S(1)} %get-tuple-element.33), channel_id=1, source_target_pairs={{0,1},{1,0},{2,3},{3,2},{4,5},{5,4},{6,7},{7,6},{8,9},{9,8},{10,11... | collective-permute-start | bytes 36872 | tf_op jit(solution)/shard_map/ppermute | solution.py:448
  31.5 3.4 %collective-permute-start.4 = (f32[24,128]{1,0:T(8,128)S(1)}, f32[24,128]{1,0:T(8,128)S(1)}, u32[]{:S(2)}, u32[]{:S(2)}) collective-permute-start(f32[24,128]{1,0:T(8,128)S(1)} %add.15._), channel_id=1, source_target_pairs={{0,17},{1,16},{2,19},{3,18},{4,21},{5,20},{6,23},{7,22},{8,25},{9,... | collective-permute-start | bytes 36872 | tf_op jit(solution)/shard_map/ppermute | solution.py:448
  34.9 3.1 %collective-permute-start.5 = (f32[24,128]{1,0:T(8,128)S(1)}, f32[24,128]{1,0:T(8,128)S(1)}, u32[]{:S(2)}, u32[]{:S(2)}) collective-permute-start(f32[24,128]{1,0:T(8,128)S(1)} %add.16), channel_id=1, source_target_pairs={{0,3},{1,2},{2,1},{3,0},{4,7},{5,6},{6,5},{7,4},{8,11},{9,10},{10,... | collective-permute-start | bytes 36872 | tf_op jit(solution)/shard_map/ppermute | solution.py:448
  38.0 4.0 %collective-permute-start.6 = (f32[24,128]{1,0:T(8,128)S(1)}, f32[24,128]{1,0:T(8,128)S(1)}, u32[]{:S(2)}, u32[]{:S(2)}) collective-permute-start(f32[24,128]{1,0:T(8,128)S(1)} %add.17), channel_id=1, source_target_pairs={{0,9},{1,8},{2,11},{3,10},{4,13},{5,12},{6,15},{7,14},{8,1},{9,0},... | collective-permute-start | bytes 36872 | tf_op jit(solution)/shard_map/ppermute | solution.py:448
  42.1 3.1 %collective-permute-start.7 = (f32[24,128]{1,0:T(8,128)S(1)}, f32[24,128]{1,0:T(8,128)S(1)}, u32[]{:S(2)}, u32[]{:S(2)}) collective-permute-start(f32[24,128]{1,0:T(8,128)S(1)} %add.18), channel_id=1, source_target_pairs={{0,5},{1,4},{2,7},{3,6},{4,1},{5,0},{6,3},{7,2},{8,13},{9,12},{10,... | collective-permute-start | bytes 36872 | tf_op jit(solution)/shard_map/ppermute | solution.py:448

commit v4 on v3

v4 whole, which is shorter than its diff:
```python
import functools
import math

import jax
import jax.numpy as jnp
import numpy as np
from jax import lax
from jax.experimental import pallas as pl
from jax.experimental.pallas import tpu as pltpu
from jax.sharding import PartitionSpec as P


SUB = 128
MODES = 16
LANES = 128
FEATURES = 2 * MODES + 8

decay_rate = 0.9
learn_rate = 0.5
dense_rate = 3.0

AXES = ("grp", "slab")
NT = (((1,), (1,)), ((), ()))
VMEM = pl.BlockSpec(memory_space=pltpu.VMEM)
HBM = pl.BlockSpec(memory_space=pltpu.HBM)


def call(kernel, outs, scratch=(), ins=(), places=None, flops=1000000):
    outs = [jax.ShapeDtypeStruct(shape, dtype) for shape, dtype in outs]
    size = sum(math.prod(o.shape) * o.dtype.itemsize for o in outs)
    return pl.pallas_call(
        kernel,
        out_shape=outs,
        in_specs=list(ins),
        out_specs=places or [VMEM] * len(outs),
        scratch_shapes=list(scratch),
        compiler_params=pltpu.CompilerParams(vmem_limit_bytes=16 << 20),
        cost_estimate=pl.CostEstimate(flops=flops, bytes_accessed=2 * size, transcendentals=0),
    )


def halves(array):
    coarse = array.astype(jnp.bfloat16).astype(jnp.float32)
    return coarse, array - coarse


def tables():
    counts = np.arange(SUB)
    waves = np.arange(MODES)
    angle = (waves[:, None] * counts[None, :] % SUB) * (2.0 * np.pi / SUB)
    weight = np.where(waves == 0, 1.0, 2.0)[:, None] / SUB
    plain = np.concatenate([np.cos(angle), np.sin(angle)]).astype(np.float32)
    parts = []
    rest = plain
    for _ in range(3):
        parts.append(rest.astype(jnp.bfloat16))
        rest = rest - parts[-1].astype(np.float32)
    high, middle, low = parts
    weighted = np.concatenate([weight * np.cos(angle), weight * np.sin(angle)]).astype(np.float32)
    return weighted, np.concatenate([high, high, middle, middle, high, low], axis=1)


def put_plane(ref, row, plane):
    for q in range(plane.shape[1] // LANES):
        ref[row + 8 * q : row + 8 * q + 8, :] = plane[:, q * LANES : (q + 1) * LANES]


def get_plane(ref, row, chunks):
    return jnp.concatenate([ref[row + 8 * q : row + 8 * q + 8, :] for q in range(chunks)], axis=1)


def pack_rows(block):
    half = block.shape[0] // 2
    return jnp.concatenate([block[:half], block[half:]], axis=1)


LAYERS = 3


def beside_in_z(plane):
    size = plane.shape[1]
    return pltpu.roll(plane, 1, 1) + pltpu.roll(plane, size - 1, 1)


def shifted(plane, before, after):
    sublane = lax.broadcasted_iota(jnp.int32, plane.shape, 0)
    last = plane.shape[0] - 1
    up = jnp.where(sublane == last, after, pltpu.roll(plane, last, 0))
    down = jnp.where(sublane == 0, before, pltpu.roll(plane, 1, 0))
    return up, down


def edge_kernel(with_momentum, sides, v_hbm, rate_hbm, forcing_hbm, momentum_hbm, *rest):
    v_ref, rate_ref, forcing_ref, momentum_ref, a_ref, b_ref = rest[:6]
    across = rest[6 : 6 + sides]
    corners_a = rest[6 + sides : 6 + 2 * sides]
    corners_b = rest[6 + 2 * sides : 6 + 3 * sides]
    sems = rest[-1]
    pairs = ((momentum_hbm, momentum_ref), (v_hbm, v_ref), (rate_hbm, rate_ref), (forcing_hbm, forcing_ref))
    moves = [pltpu.make_async_copy(*pair, sems.at[number]) for number, pair in enumerate(pairs)]
    for move in moves:
        move.start()
    last = v_ref.shape[0] - 1
    chunks = v_ref.shape[2] // LANES
    even = lax.rem(lax.axis_index("slab"), 2) == 0
    moves[0].wait()
    if with_momentum:
        packed = pack_rows(momentum_ref[...].T)
        start = LAYERS * 8 * chunks
        across[0][start : start + packed.shape[0], :] = packed
    for move in moves[1:]:
        move.wait()

    def message(edge, inside, rate, forcing):
        up, down = shifted(edge, 0.0, 0.0)
        partial = edge + (rate * (inside + up + down + beside_in_z(edge) - 6.0 * edge) + forcing)
        return edge, rate, partial

    highs = [lax.axis_index("grp") == 0] if sides == 1 else [True, False]
    for number, high in enumerate(highs):
        edge, inside = jnp.where(high, last, 0), jnp.where(high, last - 1, 1)
        planes = message(v_ref[edge], v_ref[inside], rate_ref[edge], forcing_ref[edge])
        for layer, plane in enumerate(planes):
            put_plane(across[number], layer * 8 * chunks, plane)
        left, right = planes[0][0:1], planes[0][planes[0].shape[0] - 1 :]
        for ref, line in (
            (corners_a[number], jnp.where(even, right, left)),
            (corners_b[number], jnp.where(even, left, right)),
        ):
            ref[...] = jnp.zeros_like(ref)
            for q in range(chunks):
                ref[q : q + 1, :] = line[:, q * LANES : (q + 1) * LANES]
    last = v_ref.shape[1] - 1
    lefts, rights = (
        message(v_ref[:, at, :], v_ref[:, inside, :], rate_ref[:, at, :], forcing_ref[:, at, :])
        for at, inside in ((0, 1), (last, last - 1))
    )
    for layer, (left, right) in enumerate(zip(lefts, rights)):
        put_plane(a_ref, layer * 8 * chunks, jnp.where(even, right, left))
        put_plane(b_ref, layer * 8 * chunks, jnp.where(even, left, right))


def grp_halo(two_sided, refs, layer, chunks):
    rows = 8 * chunks * layer
    if two_sided:
        return get_plane(refs[0], rows, chunks), get_plane(refs[1], rows, chunks)
    plane = get_plane(refs[0], rows, chunks)
    first = lax.axis_index("grp") == 0
    return jnp.where(first, 0.0, plane), jnp.where(first, plane, 0.0)


def as_row(column):
    size = column.shape[0]
    square = (size, size)
    same = lax.broadcasted_iota(jnp.int32, square, 0) == lax.broadcasted_iota(jnp.int32, square, 1)
    return jnp.sum(jnp.where(same, column, 0.0), axis=0, keepdims=True)


def feature_kernel(width, spectral_ref, dense_ref, map_ref, projection_ref, row_ref):
    gain = as_row(dense_ref[:, width : width + 1])
    bias = as_row(dense_ref[:, width + 1 : width + 2])
    projection_ref[...] = jnp.broadcast_to(dense_ref[:, width + 3 : width + 4], (width, LANES))
    row_ref[...] = jnp.zeros_like(row_ref)
    row_ref[0:1, :] = jnp.concatenate([gain, gain], axis=1)
    row_ref[1:2, :] = jnp.concatenate([bias, bias], axis=1)
    gains = row_ref[0:1, :]
    lane = lax.broadcasted_iota(jnp.int32, (width, LANES), 1)
    low = lane < width
    full = jnp.zeros((width, LANES), jnp.float32)
    for pair in range(MODES):
        product = spectral_ref[:, pair * LANES : (pair + 1) * LANES] * gains
        first = jnp.sum(jnp.where(low, product, 0.0), axis=1, keepdims=True)
        second = jnp.sum(jnp.where(low, 0.0, product), axis=1, keepdims=True)
        full = jnp.where(lane == 2 * pair, first, jnp.where(lane == 2 * pair + 1, second, full))
    mixing = dense_ref[:, 0:width]
    by_input = jnp.sum(gain * mixing, axis=1, keepdims=True)
    by_one = jnp.sum(bias * (mixing + spectral_ref[:, 0:width]), axis=1, keepdims=True)
    by_one = by_one + dense_ref[:, width + 2 : width + 3]
    full = jnp.where(lane == 2 * MODES, by_input, jnp.where(lane == 2 * MODES + 1, by_one, full))
    coarse = full.astype(jnp.bfloat16).astype(jnp.float32)
    fine = full - coarse
    joined = coarse + pltpu.roll(coarse, FEATURES, 1) + pltpu.roll(fine, 2 * FEATURES, 1)
    map_ref[...] = joined.astype(jnp.bfloat16)


def step_kernel(two_sided, width, scale, v_ref, rate_ref, forcing_ref, *refs):
    sides = 2 if two_sided else 1
    across, (a_ref, b_ref) = refs[:sides], refs[sides : sides + 2]
    corners_a, corners_b = refs[sides + 2 : 2 * sides + 2], refs[2 * sides + 2 : 3 * sides + 2]
    line_hbm, start_hbm, assign_hbm, map_ref, projection_ref, table_ref, wave_ref = refs[3 * sides + 2 : 3 * sides + 9]
    previous, change, pay_ref, line_ref, start_ref, assign_ref, sems = refs[3 * sides + 9 : 3 * sides + 16]
    inputs_ref, targets_ref, feature_ref, slope_ref = refs[3 * sides + 16 :]
    moves = [
        pltpu.make_async_copy(source, target, sems.at[number])
        for number, (source, target) in enumerate(
            ((line_hbm, line_ref), (start_hbm, start_ref), (assign_hbm, assign_ref))
        )
    ]
    for move in moves:
        move.start()
    cells_x, cells_y, cells_z = v_ref.shape
    chunks = cells_z // LANES
    slab = lax.axis_index("slab")
    even = lax.rem(slab, 2) == 0
    inner = jnp.logical_and(slab > 0, slab < lax.axis_size("slab") - 1)

    def slab_layer(layer):
        from_a = get_plane(a_ref, 8 * chunks * layer, chunks)
        from_b = jnp.where(inner, get_plane(b_ref, 8 * chunks * layer, chunks), 0.0)
        return jnp.where(even, from_b, from_a), jnp.where(even, from_a, from_b)

    def corner(side):
        here = True if two_sided else lax.axis_index("grp") == 1 - side

        def line(ref, valid):
            whole = jnp.concatenate([ref[q : q + 1, :] for q in range(chunks)], axis=1)
            return jnp.where(jnp.logical_and(here, valid), whole, 0.0)

        number = side if two_sided else 0
        from_a, from_b = line(corners_a[number], True), line(corners_b[number], inner)
        return jnp.where(even, from_b, from_a), jnp.where(even, from_a, from_b)

    def tendency(plane, above, below, up, down, rate, forcing):
        beside = above + below + up + down + beside_in_z(plane)
        return rate * (beside - 6.0 * plane) + forcing

    low, high = grp_halo(two_sided, across, 0, chunks)
    low_rate, high_rate = grp_halo(two_sided, across, 1, chunks)
    low_part, high_part = grp_halo(two_sided, across, 2, chunks)
    left, right = slab_layer(0)
    left_rate, right_rate = slab_layer(1)
    left_part, right_part = slab_layer(2)
    sublane = lax.broadcasted_iota(jnp.int32, (cells_y, cells_z), 0)

    def halo_step(part, rate, inner_plane, ends):
        last = part.shape[0] - 1
        at_ends = jnp.where(sublane == 0, ends[0], jnp.where(sublane == last, ends[1], 0.0))
        return part + rate * (inner_plane + at_ends)

    low_left, low_right = corner(0)
    high_left, high_right = corner(1)
    planes = [low] + [v_ref[i] for i in range(cells_x)] + [high]
    stepped = [halo_step(low_part, low_rate, planes[1], (low_left, low_right))]
    for i in range(cells_x):
        plane = planes[i + 1]
        up, down = shifted(plane, left[i : i + 1], right[i : i + 1])
        stepped.append(plane + tendency(plane, planes[i + 2], planes[i], up, down, rate_ref[i], forcing_ref[i]))
    stepped.append(halo_step(high_part, high_rate, planes[cells_x], (high_left, high_right)))
    left_new = halo_step(left_part, left_rate, v_ref[:, 0, :], (low_left, high_left))
    right_new = halo_step(right_part, right_rate, v_ref[:, cells_y - 1, :], (low_right, high_right))
    for i in range(cells_x):
        plane = stepped[i + 1]
        up, down = shifted(plane, left_new[i : i + 1], right_new[i : i + 1])
        moved = tendency(plane, stepped[i + 2], stepped[i], up, down, rate_ref[i], forcing_ref[i])
        previous[8 * i : 8 * i + 8, 0:cells_z] = plane
        change[8 * i : 8 * i + 8, 0:cells_z] = moved
    count = line_ref.shape[0]
    previous[:, cells_z : cells_z + LANES] = jnp.zeros((8 * cells_x, LANES), jnp.float32)
    change[:, cells_z : cells_z + LANES] = jnp.zeros((8 * cells_x, LANES), jnp.float32)
    for move in moves:
        move.wait()
    for t in range(count):
        line, start = line_ref[t], start_ref[t]
        inside = start & (LANES - 1)
        base = pl.multiple_of(start - inside, LANES)
        turn = (2 * LANES - inside) & (2 * LANES - 1)
        row = previous[pl.ds(line, 1), pl.ds(base, 2 * LANES)]
        inputs_ref[t : t + 1, :] = pltpu.roll(row, turn, 1)[:, :SUB]
        row = change[pl.ds(line, 1), pl.ds(base, 2 * LANES)]
        targets_ref[t : t + 1, :] = pltpu.roll(row, turn, 1)[:, :SUB]

    cos_w, sin_w = table_ref[0:MODES, :], table_ref[MODES:, :]
    coarse, rest = halves(inputs_ref[...])
    middle, fine = halves(rest)
    parts = jnp.concatenate([coarse, middle, coarse, middle, fine, coarse], axis=1).astype(jnp.bfloat16)
    waves = lax.dot_general(wave_ref[...], parts, NT, preferred_element_type=jnp.float32)
    tail = lax.broadcasted_iota(jnp.int32, (8, SUB), 0)
    half_projection = 0.5 * projection_ref[...]
    channel_map = map_ref[...]
    held = jnp.zeros((width, SUB), jnp.float32)
    lane = lax.broadcasted_iota(jnp.int32, (1, LANES), 1)
    losses = jnp.zeros((1, LANES), jnp.float32)
    root = math.sqrt(2.0 / math.pi)
    bend = 0.044715
    group = 4
    pairs = None
    for t in range(count):
        real, imag = waves[:MODES, t : t + 1], waves[MODES:, t : t + 1]
        line = inputs_ref[t : t + 1, :]
        rest = jnp.where(tail == 0, line, jnp.where(tail == 1, 1.0, 0.0))
        feature = jnp.concatenate([real * cos_w + imag * sin_w, imag * cos_w - real * sin_w, rest], axis=0)
        coarse, fine = halves(feature)
        zeros = jnp.zeros((LANES - 3 * FEATURES, SUB), jnp.float32)
        stack = jnp.concatenate([coarse, fine, coarse, zeros], axis=0).astype(jnp.bfloat16)
        at = slice(t % group * SUB, (t % group + 1) * SUB)
        feature_ref[t // group % 2, :, at] = stack
        before = jnp.dot(channel_map, stack, preferred_element_type=jnp.float32)
        square = before * before
        grown = 1.0 + jnp.tanh(before * (root + (root * bend) * square))
        after = before * grown
        slope = grown * (1.0 + (2.0 - grown) * (before * (root + (3.0 * root * bend) * square)))
        output = jnp.sum(after * half_projection, axis=0, keepdims=True)
        differ = output - targets_ref[t : t + 1, :]
        error = jnp.sum(differ * differ, axis=1, keepdims=True)
        losses = losses + jnp.where(lane == assign_ref[t], error, 0.0)
        pull = (2.0 * scale) * differ
        held = held + after * pull
        coarse, fine = halves(slope * (half_projection * pull))
        slope_ref[t // group % 2, 0:width, at] = coarse.astype(jnp.bfloat16)
        slope_ref[t // group % 2, width : 2 * width, at] = fine.astype(jnp.bfloat16)
        if (t + 1) % group == 0 or t + 1 == count:
            span = slice(0, (t % group + 1) * SUB)
            part = lax.dot_general(
                feature_ref[t // group % 2, :, span], slope_ref[t // group % 2, :, span], NT,
                preferred_element_type=jnp.float32,
            )[0 : 2 * FEATURES]
            pairs = part if pairs is None else pairs + part
    total = pairs[0:FEATURES, 0:width] + pairs[FEATURES : 2 * FEATURES, 0:width] + pairs[0:FEATURES, width:]
    pay_ref[...] = jnp.zeros_like(pay_ref)
    pay_ref[0:MODES, :] = jnp.concatenate([total[0:MODES], total[MODES : 2 * MODES]], axis=1)
    row = 2 * MODES
    pay_ref[MODES : MODES + 1, :] = jnp.concatenate([total[row : row + 1], total[row + 1 : row + 2]], axis=1)
    pay_ref[MODES + 1 : MODES + 2, 0:width] = as_row(0.5 * jnp.sum(held, axis=1, keepdims=True))
    pay_ref[pl.ds(MODES + 2 + lax.axis_index("grp"), 1), :] = losses


def field_kernel(previous, change, _, out_ref):
    cells_x, _, cells_z = out_ref.shape
    for i in range(cells_x):
        at = slice(8 * i, 8 * i + 8)
        out_ref[i] = previous[at, 0:cells_z] + change[at, 0:cells_z]


def base_kernel(masks, width, spectral_ref, mine_ref, other_ref, out_ref):
    here = lax.axis_index("grp") * lax.axis_size("slab") + lax.axis_index("slab")
    rows = width // 2
    low = lax.broadcasted_iota(jnp.int32, (rows, LANES), 1) < width
    for number in range(mine_ref.shape[0] // rows):
        source = here
        for bit, mask in enumerate(masks):
            if number >> bit & 1:
                source = source ^ mask
        even = lax.rem(source, 2) == 0
        columns = pl.ds(pl.multiple_of((source // 2) * LANES, LANES), LANES)
        mine = mine_ref[number * rows : (number + 1) * rows, :]
        other = other_ref[number * rows : (number + 1) * rows, :]
        first, second = jnp.where(even, mine, other), jnp.where(even, other, mine)
        top = jnp.where(low, first, pltpu.roll(second, width, 1))
        bottom = jnp.where(low, pltpu.roll(first, width, 1), second)
        factor = learn_rate * decay_rate
        out_ref[0:rows, columns] = spectral_ref[0:rows, columns] - factor * top
        out_ref[rows : 2 * rows, columns] = spectral_ref[rows : 2 * rows, columns] - factor * bottom


def prepare_kernel(width, spectral_ref, dense_ref, row_ref, spread_ref, turned_ref):
    tall = 2 * 8
    lane = lax.broadcasted_iota(jnp.int32, (tall, LANES), 1)
    row = lax.broadcasted_iota(jnp.int32, (tall, LANES), 0)
    low = lane < width
    gain, gain_rest = halves(learn_rate * row_ref[0:1, :])
    bias, bias_rest = halves(learn_rate * row_ref[1:2, :])
    parts = ((gain, bias), (gain_rest, bias_rest), (gain, bias))
    half = MODES // 2
    for pair in range(MODES):
        first = 2 * pair if pair < half else 2 * pair + 2
        for group in range(LANES // tall):
            block = jnp.zeros((tall, LANES), jnp.float32)
            for part, (gains, biases) in enumerate(parts):
                at = part * FEATURES + first - group * tall
                if -1 <= at < tall:
                    block = jnp.where(row == jnp.where(low, at, at + 1), gains, block)
                at = part * FEATURES + 2 * MODES + 2 - group * tall
                if pair == 0 and 0 <= at < tall:
                    block = jnp.where(jnp.logical_and(row == at, low), biases, block)
            columns = slice(pair * LANES, (pair + 1) * LANES)
            spread_ref[group * tall : (group + 1) * tall, columns] = block.astype(jnp.bfloat16)
    for pair in range(half):
        real = spectral_ref[:, pair * LANES : (pair + 1) * LANES].T
        imag = spectral_ref[:, (half + pair) * LANES : (half + pair + 1) * LANES].T
        turned_ref[pair * LANES : (pair + 1) * LANES, :] = jnp.concatenate([real, imag], axis=1)
    mixing = dense_ref[:, 0:width]
    both = jnp.concatenate([mixing, mixing + spectral_ref[:, 0:width]], axis=1).T
    turned_ref[MODES * width :, :] = jnp.concatenate([both[0:width], both[width:]], axis=1)


def update_kernel(
    width, lines, groups, pay_ref, base_ref, dense_ref, momentum_ref, row_ref, spread_ref, turned_ref,
    spectral_hbm, dense_hbm, momentum_hbm, loss_hbm, square, result, dense_out, momentum_out, loss_out, sems,
):
    first, second = lax.axis_index("grp"), lax.axis_index("slab")
    here = first * lax.axis_size("slab") + second
    copies = []

    def send(source, target):
        copies.append(pltpu.make_async_copy(source, target, sems.at[len(copies)]))
        copies[-1].start()

    kept = pay_ref.shape[0]
    square[0:kept, :] = pay_ref[...]
    square[kept:, :] = jnp.zeros((LANES - kept, LANES), jnp.float32)
    turned = square[...].T
    lane = lax.broadcasted_iota(jnp.int32, (width, LANES), 1)
    real, imag = turned[0:width], turned[width : 2 * width]
    factors = jnp.where(lane < MODES + 2, real, 0.0) + pltpu.roll(jnp.where(lane <= MODES, imag, 0.0), MODES + 2, 1)
    coarse, fine = halves(factors)
    stack = coarse + pltpu.roll(coarse, FEATURES, 1) + pltpu.roll(fine, 2 * FEATURES, 1)
    stack = stack.astype(jnp.bfloat16)
    columns = 2 * MODES * width // groups
    for group in range(groups):
        span = slice(group * columns, (group + 1) * columns)
        gradient = jnp.dot(stack, spread_ref[:, span], preferred_element_type=jnp.float32)
        result[:, span] = base_ref[:, span] - gradient
        send(result.at[:, pl.ds(group * columns, columns)], spectral_hbm.at[:, pl.ds(group * columns, columns)])

    slopes = pay_ref[MODES : MODES + 1, :]
    gain, bias = dense_ref[:, width : width + 1], dense_ref[:, width + 1 : width + 2]
    piece = momentum_ref.shape[0]
    block = here * piece // width
    inside = here * piece - block * width
    square[0:width, :] = jnp.where(lane < width, gain, bias)
    at = pl.ds(0 if piece == width else pl.multiple_of(inside, piece), piece)
    half = block // MODES
    row = pay_ref[pl.ds(block - half * MODES, 1), :]
    row = jnp.where(half == 0, row[:, 0:width], row[:, width:])
    gradient = square[at, 0:width] * row
    gradient = gradient + jnp.where(block == 0, square[at, width : 2 * width] * slopes[:, width:], 0.0)
    momentum_out[...] = decay_rate * momentum_ref[...] + gradient
    send(momentum_out, momentum_hbm)
    sums = pay_ref[pl.ds(MODES + 2 + first, 1), :]
    lane1 = lax.broadcasted_iota(jnp.int32, (1, LANES), 1)
    own = jnp.sum(jnp.where(lane1 == second, sums, 0.0), axis=1, keepdims=True)
    loss_out[...] = own * (1.0 / (lines * SUB))
    send(loss_out, loss_hbm)

    last = turned_ref[MODES * width :, :] * slopes
    gathered = jnp.where(lane < width, last, 0.0)
    for mode in range(MODES):
        gathered = gathered + turned_ref[mode * width : (mode + 1) * width, :] * pay_ref[mode : mode + 1, :]
    by_gain = jnp.sum(gathered, axis=1, keepdims=True)
    by_bias = jnp.sum(jnp.where(lane < width, 0.0, last), axis=1, keepdims=True)
    by_input, by_output, by_one = real[:, MODES : MODES + 1], real[:, MODES + 1 : MODES + 2], imag[:, MODES : MODES + 1]
    mixing = row_ref[0:1, 0:width] * by_input + row_ref[1:2, 0:width] * by_one
    dense_out[:, 0:width] = dense_ref[:, 0:width] - dense_rate * mixing
    lane4 = lax.broadcasted_iota(jnp.int32, (width, 4), 1)
    change = jnp.where(
        lane4 == 0, by_gain, jnp.where(lane4 == 1, by_bias, jnp.where(lane4 == 2, by_one, by_output)))
    dense_out[:, width : width + 4] = dense_ref[:, width : width + 4] - dense_rate * change
    send(dense_out, dense_hbm)
    for copy in copies:
        copy.wait()


def hop_masks(n_grp, n_slab):
    slab_bits = [1 << bit for bit in range(n_slab.bit_length() - 1)]
    grp_bits = [n_slab << bit for bit in range(n_grp.bit_length() - 1)]
    return [1] + [mask + 1 for mask in grp_bits + slab_bits[1:2] + slab_bits[:1:-1]]


def far_map(n_grp, n_slab):
    targets = {}
    for i in range(n_grp * n_slab):
        grp, slab = i // n_slab, i % n_slab
        if 0 < slab < n_slab - 1:
            targets[i] = i + 1 if slab % 2 else i - 1
        elif n_grp % 2 == 0:
            targets[i] = (grp ^ 1) * n_slab + slab
    return targets


def hop(array, targets):
    return lax.ppermute(array, AXES, sorted(targets.items()))


def in_hbm(array):
    return pltpu.with_memory_space_constraint(array, pltpu.HBM)


def swap(array, mask, count):
    return lax.ppermute(array, AXES, [(i, i ^ mask) for i in range(count)])


def local(velocity, rate, forcing, anchor_line, anchor_z, assign, spectral, dense, momentum):
    n_grp, n_slab = lax.axis_size("grp"), lax.axis_size("slab")
    devices = n_grp * n_slab
    width = dense.shape[1]
    lines = anchor_line.shape[0]
    cells_x, _, cells_z = velocity.shape
    chunks = cells_z // LANES
    halo_rows = LAYERS * 8 * chunks
    piece = momentum.shape[0]
    packed = piece // 2
    f32 = jnp.float32
    joined = n_grp == 2 and piece == width and devices & (devices - 1) == 0
    two_sided = n_grp != 2
    table, wave_table = (jnp.asarray(array) for array in tables())
    spectral, dense = spectral.T, dense.T

    sides = 2 if two_sided else 1
    edge_rows = halo_rows + (packed if joined else 0)
    message = ((halo_rows, LANES), f32)
    corner_message = ((-(-chunks // 8) * 8, LANES), f32)
    velocity, rate, forcing, near_momentum, to_a, to_b, *edges = call(
        functools.partial(edge_kernel, joined, sides),
        [(velocity.shape, f32)] * 3 + [(momentum.shape, f32), message, message]
        + [((edge_rows, LANES), f32)] * sides + [corner_message] * (2 * sides),
        scratch=[pltpu.SemaphoreType.DMA((4,))],
        ins=[HBM] * 4,
    )(*(in_hbm(array) for array in (velocity, rate, forcing, momentum)))
    far = far_map(n_grp, n_slab)
    near = {i: i ^ 1 for i in range(devices)}
    if two_sided:
        moves = [{i: i + n_slab for i in range(devices - n_slab)}, {i: i - n_slab for i in range(n_slab, devices)}]
        inner = [i for i in range(devices) if 0 < i % n_slab < n_slab - 1]
        diagonal_far = [{i: far[move[i]] for i in inner if i in move} for move in moves]
    else:
        moves = [{i: i ^ n_slab for i in range(devices)}]
        ends = (0, n_slab - 1)
        diagonal_far = [{i: i ^ n_slab if i % n_slab in ends else far[i ^ n_slab] for i in range(devices)}]
    from_grp = [hop(array, move) for array, move in zip(edges, moves)]
    from_b = hop(to_b, far)
    corners_b = [hop(array, move) for array, move in zip(edges[2 * sides :], diagonal_far)]
    corners_a = [
        hop(array, {i: j ^ 1 for i, j in move.items()}) for array, move in zip(edges[sides : 2 * sides], moves)
    ]
    from_a = hop(to_a, near)
    channel_map, projection, rows = call(
        functools.partial(feature_kernel, width),
        [((width, LANES), jnp.bfloat16), ((width, LANES), f32), ((8, LANES), f32)],
        ins=[VMEM] * 2,
    )(spectral, dense)
    pay_rows = -(-(MODES + 2 + n_grp) // 8) * 8
    scale = 1.0 / (devices * lines * SUB)
    window = ((8 * cells_x, cells_z + LANES), f32)
    previous, change, payload = call(
        functools.partial(step_kernel, two_sided, width, scale),
        [window, window, ((pay_rows, LANES), f32)],
        scratch=[pltpu.SMEM((lines,), jnp.int32)] * 3 + [
            pltpu.SemaphoreType.DMA((3,)),
            pltpu.VMEM((lines, SUB), f32),
            pltpu.VMEM((lines, SUB), f32),
            pltpu.VMEM((2, LANES, 4 * SUB), jnp.bfloat16),
            pltpu.VMEM((2, 2 * width, 4 * SUB), jnp.bfloat16),
        ],
        ins=[VMEM] * (5 + 3 * sides) + [HBM] * 3 + [VMEM] * 4,
    )(velocity, rate, forcing, *from_grp, from_a, from_b, *corners_a, *corners_b,
      in_hbm(anchor_line), in_hbm(anchor_z), in_hbm(assign.reshape(-1)), channel_map, projection, table, wave_table)

    masks = hop_masks(n_grp, n_slab)
    if joined:
        mine = jnp.concatenate([edges[0][halo_rows:], from_grp[0][halo_rows:]], axis=0)
        order = [n_slab] + masks[3:] + masks[2:3] + [1]
        for mask in order[1:-1]:
            other = swap(mine, mask, devices)
            mine = jnp.concatenate([mine, other], axis=0)
        other = swap(mine, order[-1], devices)
        base = call(
            functools.partial(base_kernel, order[:-1], width), [(spectral.shape, f32)], ins=[VMEM] * 3
        )(spectral, mine, other)[0]
    else:
        whole = lax.all_gather(momentum, AXES, axis=0, tiled=True)
        base = spectral - (learn_rate * decay_rate) * whole.T
    anchor = payload
    if devices & (devices - 1) == 0:
        for number, mask in enumerate(masks):
            payload = payload + swap(payload, mask, devices)
            if number == 0:
                anchor = payload
    else:
        payload = lax.psum(payload, AXES)
    field_now = call(field_kernel, [(velocity.shape, f32)], ins=[VMEM, VMEM, HBM])(previous, change, anchor)[0]
    spread, turned = call(
        functools.partial(prepare_kernel, width),
        [((LANES, 2 * MODES * width), jnp.bfloat16), (((MODES + 1) * width, LANES), f32)],
        ins=[VMEM] * 3,
    )(spectral, dense, rows)
    groups = 4
    spectral_new, dense_new, momentum_new, trainer_loss = call(
        functools.partial(update_kernel, width, lines, groups),
        [(spectral.shape, f32), (dense.shape, f32), (momentum.shape, f32), ((1, 1), f32)],
        scratch=[
            pltpu.VMEM((LANES, LANES), f32), pltpu.VMEM(spectral.shape, f32), pltpu.VMEM(dense.shape, f32),
            pltpu.VMEM(momentum.shape, f32), pltpu.VMEM((1, 1), f32), pltpu.SemaphoreType.DMA((groups + 3,)),
        ],
        ins=[VMEM] * 7,
        places=[HBM] * 4,
    )(payload, base, dense, near_momentum, rows, spread, turned)
    return (field_now, trainer_loss, spectral_new.T, dense_new.T, momentum_new)


def solution(mesh):
    placed = (
        P("grp", "slab", None),
        P("grp", "slab", None),
        P("grp", "slab", None),
        P(("grp", "slab")),
        P(("grp", "slab")),
        P(("grp", "slab"), None),
        P(),
        P(),
        P(("grp", "slab"), None),
    )

    return jax.shard_map(
        local,
        mesh=mesh,
        in_specs=placed,
        out_specs=(P("grp", "slab", None), P("grp", "slab"), P(), P(), P(("grp", "slab"), None)),
        check_vma=False,
    )
```

time: 47.2 us -> 48.2 us (1.021)
  starting transfers between devices: 16 us -> 20.5 us
  waiting for transfers between devices: 22.5 us -> 19.6 us
  Pallas kernels: 7.68 us -> 7.02 us
    ppermute x9, waiting for transfers between devices: 19.7 us -> 14.9 us  [swap(): return lax.ppermute(array, AXES, [(i, i ^ mask) for i in range(count)])]
    ppermute x9, starting transfers between devices: 8.71 us -> 13.3 us  [swap(): return lax.ppermute(array, AXES, [(i, i ^ mask) for i in range(count)])]
    ppermute x3 -> x5, waiting for transfers between devices: 2.76 us -> 4.69 us  [hop(): return lax.ppermute(array, AXES, sorted(targets.items()))]
    pallas_call x3 -> x2, Pallas kernels: 2.2 us -> 1.95 us  [the longest x1 1.2 us: local(): call(functools.partial(edge_kernel, joined, sides), [(velocity.shape, f32...]
    ppermute x3 -> x5, starting transfers between devices: 7.31 us -> 7.21 us  [hop(): return lax.ppermute(array, AXES, sorted(targets.items()))]
  transfers between devices with their start and end apart: 12 -> 14, of which waited for: 10 -> 10; matrix products, arithmetic and copies ran while one was open for 0% -> 0% of each run, Pallas kernels for 10% -> 9%
where the time goes in v4:
time: 48.2 us; the launch traced here: 48 us
  starting transfers between devices  20.5 us (43%)
  waiting for transfers between devices  19.6 us (41%)
  Pallas kernels  7.02 us (15%)
  between operations  0.73 us (2%)
    ppermute x9, waiting for transfers between devices, swap(): return lax.ppermute(array, AXES, [(i, i ^ mask) for i in range(count)])  14.9 us
    ppermute x9, starting transfers between devices, swap(): return lax.ppermute(array, AXES, [(i, i ^ mask) for i in range(count)])  13.3 us
    ppermute x5, starting transfers between devices, hop(): return lax.ppermute(array, AXES, sorted(targets.items()))  7.21 us
    ppermute x5, waiting for transfers between devices, hop(): return lax.ppermute(array, AXES, sorted(targets.items()))  4.69 us
    pallas_call x1, Pallas kernels, local(): call(functools.partial(step_kernel, two_sided, width, scale), [window, wi...  2.26 us
    pallas_call x1, Pallas kernels, local(): call(functools.partial(update_kernel, width, lines, groups), [(spectral.s...  1.27 us
    pallas_call x1, Pallas kernels, local(): call(functools.partial(edge_kernel, joined, sides), [(velocity.shape, f32...  1.2 us
  transfers between devices with their start and end apart: 14, of which 10 were waited for; matrix products, arithmetic and copies ran while one was open for 0% of the time, Pallas kernels for 9%

profile of v4, /device:TPU:0, one launch (start us, length us, event | category | flops | bytes accessed | tf_op | source)
XLA Modules:
  0.0 48.0 jit_solution(18319707776262032749)
XLA Ops:
  0.6 1.2 %shard_map.146 = (f32[8,8,512]{2,1,0:T(8,128)S(1)}, f32[8,8,512]{2,1,0:T(8,128)S(1)}, f32[8,8,512]{2,1,0:T(8,128)S(1)}, f32[64,64]{1,0:T(8,128)S(1)}, f32[96,128...) custom-call(f32[8,8,512]{2,1,0:T(8,128)} %v_hbm.1, ...), custom_call_target="tpu_custom_call" | custom-call | flops 1000000 | bytes 1163264 | tf_op jit(solution)/shard_map/pallas_call | solution.py:502
  1.8 0.0 copy-start
  1.8 3.1 %collective-permute-start = (f32[128,128]{1,0:T(8,128)S(1)}, f32[128,128]{1,0:T(8,128)S(1)}, u32[]{:S(2)}, u32[]{:S(2)}) collective-permute-start(f32[128,128]{1,0:T(8,128)S(1)} %get-tuple-element.29), channel_id=1, source_target_pairs={{0,16},{1,17},{2,18},{3,19},{4,20},{5,21},{6,22},{7,23},{8,24},{9,... | collective-permute-start | bytes 196616 | tf_op jit(solution)/shard_map/ppermute | solution.py:471
  4.9 2.2 %collective-permute-done.refs_0_ = f32[128,128]{1,0:T(8,128)S(1)} collective-permute-done((f32[128,128]{1,0:T(8,128)S(1)}, f32[128,128]{1,0:T(8,128)S(1)}, u32[]{:S(2)}, u32[]{:S(2)}) %collective-permute-start) | collective-permute-done | bytes 65568 | tf_op jit(solution)/shard_map/ppermute | solution.py:471
  7.2 1.4 %collective-permute-start.10 = (f32[64,128]{1,0:T(8,128)S(1)}, f32[64,128]{1,0:T(8,128)S(1)}, u32[]{:S(2)}, u32[]{:S(2)}) collective-permute-start(f32[64,128]{1,0:T(8,128)S(1)} %pad_maximum_fusion.2), channel_id=1, source_target_pairs={{0,9},{1,8},{2,11},{3,10},{4,13},{5,12},{6,15},{7,14},{8,1},{9,0},... | collective-permute-start | bytes 98312 | tf_op jit(solution)/shard_map/ppermute | solution.py:479
  8.6 2.9 %collective-permute-done.10 = f32[64,128]{1,0:T(8,128)S(1)} collective-permute-done((f32[64,128]{1,0:T(8,128)S(1)}, f32[64,128]{1,0:T(8,128)S(1)}, u32[]{:S(2)}, u32[]{:S(2)}) %collective-permute-start.10) | collective-permute-done | bytes 32800 | tf_op jit(solution)/shard_map/ppermute | solution.py:479
  11.5 1.9 %collective-permute-start.11 = (f32[128,128]{1,0:T(8,128)S(1)}, f32[128,128]{1,0:T(8,128)S(1)}, u32[]{:S(2)}, u32[]{:S(2)}) collective-permute-start(f32[128,128]{1,0:T(8,128)S(1)} %pad_maximum_fusion.1), channel_id=1, source_target_pairs={{0,5},{1,4},{2,7},{3,6},{4,1},{5,0},{6,3},{7,2},{8,13},{9,12},{10,... | collective-permute-start | bytes 196616 | tf_op jit(solution)/shard_map/ppermute | solution.py:479
  13.4 2.2 %collective-permute-done.11 = f32[128,128]{1,0:T(8,128)S(1)} collective-permute-done((f32[128,128]{1,0:T(8,128)S(1)}, f32[128,128]{1,0:T(8,128)S(1)}, u32[]{:S(2)}, u32[]{:S(2)}) %collective-permute-start.11) | collective-permute-done | bytes 65568 | tf_op jit(solution)/shard_map/ppermute | solution.py:479
  15.6 1.9 %collective-permute-start.12 = (f32[256,128]{1,0:T(8,128)S(1)}, f32[256,128]{1,0:T(8,128)S(1)}, u32[]{:S(2)}, u32[]{:S(2)}) collective-permute-start(f32[256,128]{1,0:T(8,128)S(1)} %pad_maximum_fusion), channel_id=1, source_target_pairs={{0,3},{1,2},{2,1},{3,0},{4,7},{5,6},{6,5},{7,4},{8,11},{9,10},{10,... | collective-permute-start | bytes 393224 | tf_op jit(solution)/shard_map/ppermute | solution.py:479
  17.5 3.6 %collective-permute-done.12 = f32[256,128]{1,0:T(8,128)S(1)} collective-permute-done((f32[256,128]{1,0:T(8,128)S(1)}, f32[256,128]{1,0:T(8,128)S(1)}, u32[]{:S(2)}, u32[]{:S(2)}) %collective-permute-start.12) | collective-permute-done | bytes 131104 | tf_op jit(solution)/shard_map/ppermute | solution.py:479
  21.1 0.0 copy-start.1
  21.1 0.3 collective-permute-start.13
  21.4 0.2 collective-permute-start.1
  21.6 2.2 %collective-permute-start.2 = (f32[96,128]{1,0:T(8,128)S(1)}, f32[96,128]{1,0:T(8,128)S(1)}, u32[]{:S(2)}, u32[]{:S(2)}) collective-permute-start(f32[96,128]{1,0:T(8,128)S(1)} %get-tuple-element.31), channel_id=1, source_target_pairs={{0,16},{1,2},{2,1},{3,4},{4,3},{5,6},{6,5},{7,8},{8,7},{9,10},{10,... | collective-permute-start | bytes 147464 | tf_op jit(solution)/shard_map/ppermute | solution.py:471
  23.9 1.2 %collective-permute-start.3 = (f32[8,128]{1,0:T(8,128)S(1)}, f32[8,128]{1,0:T(8,128)S(1)}, u32[]{:S(2)}, u32[]{:S(2)}) collective-permute-start(f32[8,128]{1,0:T(8,128)S(1)} %get-tuple-element.32), channel_id=1, source_target_pairs={{0,17},{1,16},{2,19},{3,18},{4,21},{5,20},{6,23},{7,22},{8,25},{9,... | collective-permute-start | bytes 12296 | tf_op jit(solution)/shard_map/ppermute | solution.py:471
  25.1 0.5 %collective-permute-start.4 = (f32[8,128]{1,0:T(8,128)S(1)}, f32[8,128]{1,0:T(8,128)S(1)}, u32[]{:S(2)}, u32[]{:S(2)}) collective-permute-start(f32[8,128]{1,0:T(8,128)S(1)} %get-tuple-element.33), channel_id=1, source_target_pairs={{0,16},{1,18},{2,17},{3,20},{4,19},{5,22},{6,21},{7,24},{8,23},{9,... | collective-permute-start | bytes 12296 | tf_op jit(solution)/shard_map/ppermute | solution.py:471
  25.6 0.0 copy-done
  25.6 0.0 copy-done.1
  25.6 0.0 copy-start.2
  25.6 0.0 copy-start.3
  25.6 0.6 %shard_map.147 = (bf16[64,128]{1,0:T(8,128)(2,1)S(1)}, f32[64,128]{1,0:T(8,128)S(1)}, f32[8,128]{1,0:T(8,128)S(1)}) custom-call(f32[64,2048]{1,0:T(8,128)S(1)} %bitcast.5, f32[64,68]{1,0:T(8,128)S(1)} %bitcast.8), custom_call_target="tpu_custom_call" | custom-call | flops 1000000 | bytes 106496 | tf_op jit(solution)/shard_map/pallas_call | solution.py:526
  26.2 0.7 %collective-permute-done.3.refs_3_ = f32[8,128]{1,0:T(8,128)S(1)} collective-permute-done((f32[8,128]{1,0:T(8,128)S(1)}, f32[8,128]{1,0:T(8,128)S(1)}, u32[]{:S(2)}, u32[]{:S(2)}) %collective-permute-start.3) | collective-permute-done | bytes 4128 | tf_op jit(solution)/shard_map/ppermute | solution.py:471
  26.9 1.8 %collective-permute-done.4.refs_4_ = f32[8,128]{1,0:T(8,128)S(1)} collective-permute-done((f32[8,128]{1,0:T(8,128)S(1)}, f32[8,128]{1,0:T(8,128)S(1)}, u32[]{:S(2)}, u32[]{:S(2)}) %collective-permute-start.4) | collective-permute-done | bytes 4128 | tf_op jit(solution)/shard_map/ppermute | solution.py:471
  28.7 0.0 collective-permute-done.1.refs_1_
  28.7 0.0 collective-permute-done.2.refs_2_
  28.7 0.0 copy-done.2
  28.7 0.0 copy-done.3
  28.7 2.3 %shard_map.148 = (f32[64,640]{1,0:T(8,128)S(1)}, f32[64,640]{1,0:T(8,128)S(1)}, f32[24,128]{1,0:T(8,128)S(1)}) custom-call(f32[8,8,512]{2,1,0:T(8,128)S(1)} %get-tuple-element.26.v_ref, f32[8,8,512]{2,1,0:T(8,128)S(1)} %get-tuple-element.27.rate_ref, f32[8,8,512]{2,1,0:T(8,128)S(1)} %get-tuple-element.28.forcing_ref, ...), custom_call_target="tpu_custom_call" | custom-call | flops 1000000 | bytes 679936 | tf_op jit(solution)/shard_map/pallas_call | solution.py:534
  31.0 0.1 collective-permute-start.5
  31.0 1.2 %collective-permute-done.5 = f32[24,128]{1,0:T(8,128)S(1)} collective-permute-done((f32[24,128]{1,0:T(8,128)S(1)}, f32[24,128]{1,0:T(8,128)S(1)}, u32[]{:S(2)}, u32[]{:S(2)}) %collective-permute-start.5) | collective-permute-done | bytes 12320 | tf_op jit(solution)/shard_map/ppermute | solution.py:479
  32.2 0.9 %collective-permute-start.6 = (f32[24,128]{1,0:T(8,128)S(1)}, f32[24,128]{1,0:T(8,128)S(1)}, u32[]{:S(2)}, u32[]{:S(2)}) collective-permute-start(f32[24,128]{1,0:T(8,128)S(1)} %add.15._), channel_id=1, source_target_pairs={{0,17},{1,16},{2,19},{3,18},{4,21},{5,20},{6,23},{7,22},{8,25},{9,... | collective-permute-start | bytes 36872 | tf_op jit(solution)/shard_map/ppermute | solution.py:479
  33.1 2.3 %collective-permute-done.6 = f32[24,128]{1,0:T(8,128)S(1)} collective-permute-done((f32[24,128]{1,0:T(8,128)S(1)}, f32[24,128]{1,0:T(8,128)S(1)}, u32[]{:S(2)}, u32[]{:S(2)}) %collective-permute-start.6) | collective-permute-done | bytes 12320 | tf_op jit(solution)/shard_map/ppermute | solution.py:479
  35.3 1.6 %collective-permute-start.7 = (f32[24,128]{1,0:T(8,128)S(1)}, f32[24,128]{1,0:T(8,128)S(1)}, u32[]{:S(2)}, u32[]{:S(2)}) collective-permute-start(f32[24,128]{1,0:T(8,128)S(1)} %add.16), channel_id=1, source_target_pairs={{0,3},{1,2},{2,1},{3,0},{4,7},{5,6},{6,5},{7,4},{8,11},{9,10},{10,... | collective-permute-start | bytes 36872 | tf_op jit(solution)/shard_map/ppermute | solution.py:479
  37.0 1.5 %collective-permute-done.7 = f32[24,128]{1,0:T(8,128)S(1)} collective-permute-done((f32[24,128]{1,0:T(8,128)S(1)}, f32[24,128]{1,0:T(8,128)S(1)}, u32[]{:S(2)}, u32[]{:S(2)}) %collective-permute-start.7) | collective-permute-done | bytes 12320 | tf_op jit(solution)/shard_map/ppermute | solution.py:479
  38.5 3.4 %collective-permute-start.8 = (f32[24,128]{1,0:T(8,128)S(1)}, f32[24,128]{1,0:T(8,128)S(1)}, u32[]{:S(2)}, u32[]{:S(2)}) collective-permute-start(f32[24,128]{1,0:T(8,128)S(1)} %add.17), channel_id=1, source_target_pairs={{0,9},{1,8},{2,11},{3,10},{4,13},{5,12},{6,15},{7,14},{8,1},{9,0},... | collective-permute-start | bytes 36872 | tf_op jit(solution)/shard_map/ppermute | solution.py:479
  41.9 1.4 %collective-permute-done.8 = f32[24,128]{1,0:T(8,128)S(1)} collective-permute-done((f32[24,128]{1,0:T(8,128)S(1)}, f32[24,128]{1,0:T(8,128)S(1)}, u32[]{:S(2)}, u32[]{:S(2)}) %collective-permute-start.8) | collective-permute-done | bytes 12320 | tf_op jit(solution)/shard_map/ppermute | solution.py:479
  43.3 1.8 %collective-permute-start.9 = (f32[24,128]{1,0:T(8,128)S(1)}, f32[24,128]{1,0:T(8,128)S(1)}, u32[]{:S(2)}, u32[]{:S(2)}) collective-permute-start(f32[24,128]{1,0:T(8,128)S(1)} %add.18), channel_id=1, source_target_pairs={{0,5},{1,4},{2,7},{3,6},{4,1},{5,0},{6,3},{7,2},{8,13},{9,12},{10,... | collective-permute-start | bytes 36872 | tf_op jit(solution)/shard_map/ppermute | solution.py:479
  45.1 0.8 %shard_map.151 = (bf16[128,2048]{1,0:T(8,128)(2,1)S(1)}, f32[1088,128]{1,0:T(8,128)S(1)}) custom-call(f32[64,2048]{1,0:T(8,128)S(1)} %bitcast.6, f32[64,68]{1,0:T(8,128)S(1)} %bitcast.9, f32[8,128]{1,0:T(8,128)S(1)} %get-tuple-element.40.row_ref), custom_call_target="tpu_custom_call" | custom-call | flops 1000000 | bytes 2162688 | tf_op jit(solution)/shard_map/pallas_call | solution.py:571
  45.8 0.7 %shard_map.149 = f32[8,8,512]{2,1,0:T(8,128)} custom-call(f32[64,640]{1,0:T(8,128)S(1)} %get-tuple-element.36.previous, f32[64,640]{1,0:T(8,128)S(1)} %get-tuple-element.37.change, f32[24,128]{1,0:T(8,128)S(1)} %add.15._), custom_call_target="tpu_custom_call" | custom-call | flops 1000000 | bytes 262144 | tf_op jit(solution)/shard_map/pallas_call | solution.py:570
  46.5 0.0 collective-permute-done.9
  46.5 0.0 collective-permute-done.13.other_ref
  46.5 0.2 shard_map.150.base_ref
  46.7 1.3 %shard_map.152 = (f32[64,2048]{1,0:T(8,128)}, f32[64,68]{1,0:T(8,128)}, f32[64,64]{1,0:T(8,128)}, f32[1,1]{1,0:T(1,128)}) custom-call(f32[24,128]{1,0:T(8,128)S(1)} %add.19.pay_ref, f32[64,2048]{1,0:T(8,128)S(1)} %shard_map.150.base_ref, f32[64,68]{1,0:T(8,128)S(1)} %bitcast.10, f32[64,64]{1,0:T(8,128)S(1)} %get-tuple-element.39.momentum_ref, ...), custom_call_target="tpu_custom_call" | custom-call | flops 1000000 | bytes 1116168 | tf_op jit(solution)/shard_map/pallas_call | solution.py:577
  (13 shorter events, 0.1 us)
Async XLA Ops:
  1.8 23.7 %copy-start = (f32[2048,64]{0,1:T(8,128)S(1)}, f32[2048,64]{0,1:T(8,128)}, u32[]{:S(2)}) copy-start(f32[2048,64]{0,1:T(8,128)} %param.17) | copy-start | bytes 1572868
  1.8 5.3 %collective-permute-start = (f32[128,128]{1,0:T(8,128)S(1)}, f32[128,128]{1,0:T(8,128)S(1)}, u32[]{:S(2)}, u32[]{:S(2)}) collective-permute-start(f32[128,128]{1,0:T(8,128)S(1)} %get-tuple-element.29), channel_id=1, source_target_pairs={{0,16},{1,17},{2,18},{3,19},{4,20},{5,21},{6,22},{7,23},{8,24},{9,... | collective-permute-start | bytes 196616 | tf_op jit(solution)/shard_map/ppermute | solution.py:471
  7.2 4.3 %collective-permute-start.10 = (f32[64,128]{1,0:T(8,128)S(1)}, f32[64,128]{1,0:T(8,128)S(1)}, u32[]{:S(2)}, u32[]{:S(2)}) collective-permute-start(f32[64,128]{1,0:T(8,128)S(1)} %pad_maximum_fusion.2), channel_id=1, source_target_pairs={{0,9},{1,8},{2,11},{3,10},{4,13},{5,12},{6,15},{7,14},{8,1},{9,0},... | collective-permute-start | bytes 98312 | tf_op jit(solution)/shard_map/ppermute | solution.py:479
  11.5 4.1 %collective-permute-start.11 = (f32[128,128]{1,0:T(8,128)S(1)}, f32[128,128]{1,0:T(8,128)S(1)}, u32[]{:S(2)}, u32[]{:S(2)}) collective-permute-start(f32[128,128]{1,0:T(8,128)S(1)} %pad_maximum_fusion.1), channel_id=1, source_target_pairs={{0,5},{1,4},{2,7},{3,6},{4,1},{5,0},{6,3},{7,2},{8,13},{9,12},{10,... | collective-permute-start | bytes 196616 | tf_op jit(solution)/shard_map/ppermute | solution.py:479
  15.6 5.5 %collective-permute-start.12 = (f32[256,128]{1,0:T(8,128)S(1)}, f32[256,128]{1,0:T(8,128)S(1)}, u32[]{:S(2)}, u32[]{:S(2)}) collective-permute-start(f32[256,128]{1,0:T(8,128)S(1)} %pad_maximum_fusion), channel_id=1, source_target_pairs={{0,3},{1,2},{2,1},{3,0},{4,7},{5,6},{6,5},{7,4},{8,11},{9,10},{10,... | collective-permute-start | bytes 393224 | tf_op jit(solution)/shard_map/ppermute | solution.py:479
  21.1 4.5 %copy-start.1 = (f32[68,64]{0,1:T(8,128)S(1)}, f32[68,64]{0,1:T(8,128)}, u32[]{:S(2)}) copy-start(f32[68,64]{0,1:T(8,128)} %param.18) | copy-start | bytes 52228
  21.1 25.4 %collective-permute-start.13 = (f32[512,128]{1,0:T(8,128)S(1)}, f32[512,128]{1,0:T(8,128)S(1)}, u32[]{:S(2)}, u32[]{:S(2)}) collective-permute-start(f32[512,128]{1,0:T(8,128)S(1)} %constant_dynamic-update-slice_fusion.mine_ref), channel_id=1, source_target_pairs={{0,1},{1,0},{2,3},{3,2},{4,5},{5,4},{6,7},{7,6},{8,9},{9,8},{10,11... | collective-permute-start | bytes 786440 | tf_op jit(solution)/shard_map/ppermute | solution.py:479
  21.4 7.3 %collective-permute-start.1 = (f32[96,128]{1,0:T(8,128)S(1)}, f32[96,128]{1,0:T(8,128)S(1)}, u32[]{:S(2)}, u32[]{:S(2)}) collective-permute-start(f32[96,128]{1,0:T(8,128)S(1)} %get-tuple-element.30), channel_id=1, source_target_pairs={{0,1},{1,0},{2,3},{3,2},{4,5},{5,4},{6,7},{7,6},{8,9},{9,8},{10,11... | collective-permute-start | bytes 147464 | tf_op jit(solution)/shard_map/ppermute | solution.py:471
  21.6 7.0 %collective-permute-start.2 = (f32[96,128]{1,0:T(8,128)S(1)}, f32[96,128]{1,0:T(8,128)S(1)}, u32[]{:S(2)}, u32[]{:S(2)}) collective-permute-start(f32[96,128]{1,0:T(8,128)S(1)} %get-tuple-element.31), channel_id=1, source_target_pairs={{0,16},{1,2},{2,1},{3,4},{4,3},{5,6},{6,5},{7,8},{8,7},{9,10},{10,... | collective-permute-start | bytes 147464 | tf_op jit(solution)/shard_map/ppermute | solution.py:471
  23.9 3.0 %collective-permute-start.3 = (f32[8,128]{1,0:T(8,128)S(1)}, f32[8,128]{1,0:T(8,128)S(1)}, u32[]{:S(2)}, u32[]{:S(2)}) collective-permute-start(f32[8,128]{1,0:T(8,128)S(1)} %get-tuple-element.32), channel_id=1, source_target_pairs={{0,17},{1,16},{2,19},{3,18},{4,21},{5,20},{6,23},{7,22},{8,25},{9,... | collective-permute-start | bytes 12296 | tf_op jit(solution)/shard_map/ppermute | solution.py:471
  25.1 3.6 %collective-permute-start.4 = (f32[8,128]{1,0:T(8,128)S(1)}, f32[8,128]{1,0:T(8,128)S(1)}, u32[]{:S(2)}, u32[]{:S(2)}) collective-permute-start(f32[8,128]{1,0:T(8,128)S(1)} %get-tuple-element.33), channel_id=1, source_target_pairs={{0,16},{1,18},{2,17},{3,20},{4,19},{5,22},{6,21},{7,24},{8,23},{9,... | collective-permute-start | bytes 12296 | tf_op jit(solution)/shard_map/ppermute | solution.py:471
  25.6 3.1 %copy-start.2 = (bf16[32,768]{1,0:T(8,128)(2,1)S(1)}, bf16[32,768]{1,0:T(8,128)(2,1)}, u32[]{:S(2)}) copy-start(bf16[32,768]{1,0:T(8,128)(2,1)} %constant.5.clone.refs_11_) | copy-start | bytes 147460
  25.6 3.1 %copy-start.3 = (f32[32,128]{1,0:T(8,128)S(1)}, f32[32,128]{1,0:T(8,128)}, u32[]{:S(2)}) copy-start(f32[32,128]{1,0:T(8,128)} %constant.4.clone.refs_10_) | copy-start | bytes 49156
  31.0 1.2 %collective-permute-start.5 = (f32[24,128]{1,0:T(8,128)S(1)}, f32[24,128]{1,0:T(8,128)S(1)}, u32[]{:S(2)}, u32[]{:S(2)}) collective-permute-start(f32[24,128]{1,0:T(8,128)S(1)} %get-tuple-element.38), channel_id=1, source_target_pairs={{0,1},{1,0},{2,3},{3,2},{4,5},{5,4},{6,7},{7,6},{8,9},{9,8},{10,11... | collective-permute-start | bytes 36872 | tf_op jit(solution)/shard_map/ppermute | solution.py:479
  32.2 3.1 %collective-permute-start.6 = (f32[24,128]{1,0:T(8,128)S(1)}, f32[24,128]{1,0:T(8,128)S(1)}, u32[]{:S(2)}, u32[]{:S(2)}) collective-permute-start(f32[24,128]{1,0:T(8,128)S(1)} %add.15._), channel_id=1, source_target_pairs={{0,17},{1,16},{2,19},{3,18},{4,21},{5,20},{6,23},{7,22},{8,25},{9,... | collective-permute-start | bytes 36872 | tf_op jit(solution)/shard_map/ppermute | solution.py:479
  35.3 3.1 %collective-permute-start.7 = (f32[24,128]{1,0:T(8,128)S(1)}, f32[24,128]{1,0:T(8,128)S(1)}, u32[]{:S(2)}, u32[]{:S(2)}) collective-permute-start(f32[24,128]{1,0:T(8,128)S(1)} %add.16), channel_id=1, source_target_pairs={{0,3},{1,2},{2,1},{3,0},{4,7},{5,6},{6,5},{7,4},{8,11},{9,10},{10,... | collective-permute-start | bytes 36872 | tf_op jit(solution)/shard_map/ppermute | solution.py:479
  38.5 4.8 %collective-permute-start.8 = (f32[24,128]{1,0:T(8,128)S(1)}, f32[24,128]{1,0:T(8,128)S(1)}, u32[]{:S(2)}, u32[]{:S(2)}) collective-permute-start(f32[24,128]{1,0:T(8,128)S(1)} %add.17), channel_id=1, source_target_pairs={{0,9},{1,8},{2,11},{3,10},{4,13},{5,12},{6,15},{7,14},{8,1},{9,0},... | collective-permute-start | bytes 36872 | tf_op jit(solution)/shard_map/ppermute | solution.py:479
  43.3 3.2 %collective-permute-start.9 = (f32[24,128]{1,0:T(8,128)S(1)}, f32[24,128]{1,0:T(8,128)S(1)}, u32[]{:S(2)}, u32[]{:S(2)}) collective-permute-start(f32[24,128]{1,0:T(8,128)S(1)} %add.18), channel_id=1, source_target_pairs={{0,5},{1,4},{2,7},{3,6},{4,1},{5,0},{6,3},{7,2},{8,13},{9,12},{10,... | collective-permute-start | bytes 36872 | tf_op jit(solution)/shard_map/ppermute | solution.py:479

commit v5 on v4

--- a/solution.py
+++ b/solution.py
@@ -69,6 +69,15 @@
     return jnp.concatenate([ref[row + 8 * q : row + 8 * q + 8, :] for q in range(chunks)], axis=1)
 
 
+def put_line(ref, row, line):
+    for q in range(line.shape[1] // LANES):
+        ref[row + q : row + q + 1, :] = line[:, q * LANES : (q + 1) * LANES]
+
+
+def get_line(ref, row, chunks):
+    return jnp.concatenate([ref[row + q : row + q + 1, :] for q in range(chunks)], axis=1)
+
+
 def pack_rows(block):
     half = block.shape[0] // 2
     return jnp.concatenate([block[:half], block[half:]], axis=1)
@@ -90,13 +99,18 @@
     return up, down
 
 
-def edge_kernel(with_momentum, sides, v_hbm, rate_hbm, forcing_hbm, momentum_hbm, *rest):
-    v_ref, rate_ref, forcing_ref, momentum_ref, a_ref, b_ref = rest[:6]
+def edge_kernel(
+    with_momentum, sides, v_hbm, rate_hbm, forcing_hbm, momentum_hbm, dense_hbm, table_hbm, wave_hbm, *rest
+):
+    v_ref, rate_ref, forcing_ref, momentum_ref, dense_ref, table_ref, wave_ref, a_ref, b_ref = rest[:9]
+    rest = rest[3:]
     across = rest[6 : 6 + sides]
-    corners_a = rest[6 + sides : 6 + 2 * sides]
-    corners_b = rest[6 + 2 * sides : 6 + 3 * sides]
+    corners = rest[6 + sides : 6 + 2 * sides]
     sems = rest[-1]
-    pairs = ((momentum_hbm, momentum_ref), (v_hbm, v_ref), (rate_hbm, rate_ref), (forcing_hbm, forcing_ref))
+    pairs = (
+        (momentum_hbm, momentum_ref), (v_hbm, v_ref), (rate_hbm, rate_ref), (forcing_hbm, forcing_ref),
+        (dense_hbm, dense_ref), (table_hbm, table_ref), (wave_hbm, wave_ref),
+    )
     moves = [pltpu.make_async_copy(*pair, sems.at[number]) for number, pair in enumerate(pairs)]
     for move in moves:
         move.start()
@@ -123,13 +137,8 @@
         for layer, plane in enumerate(planes):
             put_plane(across[number], layer * 8 * chunks, plane)
         left, right = planes[0][0:1], planes[0][planes[0].shape[0] - 1 :]
-        for ref, line in (
-            (corners_a[number], jnp.where(even, right, left)),
-            (corners_b[number], jnp.where(even, left, right)),
-        ):
-            ref[...] = jnp.zeros_like(ref)
-            for q in range(chunks):
-                ref[q : q + 1, :] = line[:, q * LANES : (q + 1) * LANES]
+        corners[number][...] = jnp.zeros_like(corners[number])
+        put_line(corners[number], 0, jnp.where(even, left, right))
     last = v_ref.shape[1] - 1
     lefts, rights = (
         message(v_ref[:, at, :], v_ref[:, inside, :], rate_ref[:, at, :], forcing_ref[:, at, :])
@@ -149,6 +158,18 @@
     return jnp.where(first, 0.0, plane), jnp.where(first, plane, 0.0)
 
 
+def near_kernel(sides, chunks, message_ref, *refs):
+    across, out_ref = refs[:sides], refs[sides]
+    even = lax.rem(lax.axis_index("slab"), 2) == 0
+    rows = message_ref.shape[0]
+    out_ref[0:rows, :] = message_ref[...]
+    out_ref[rows:, :] = jnp.zeros((out_ref.shape[0] - rows, LANES), jnp.float32)
+    for number in range(sides):
+        plane = get_plane(across[number], 0, chunks)
+        last = plane.shape[0] - 1
+        put_line(out_ref, rows + number * chunks, jnp.where(even, plane[last:], plane[0:1]))
+
+
 def as_row(column):
     size = column.shape[0]
     square = (size, size)
@@ -156,14 +177,10 @@
     return jnp.sum(jnp.where(same, column, 0.0), axis=0, keepdims=True)
 
 
-def feature_kernel(width, spectral_ref, dense_ref, map_ref, projection_ref, row_ref):
+def feature_map(width, spectral_ref, dense_ref):
     gain = as_row(dense_ref[:, width : width + 1])
     bias = as_row(dense_ref[:, width + 1 : width + 2])
-    projection_ref[...] = jnp.broadcast_to(dense_ref[:, width + 3 : width + 4], (width, LANES))
-    row_ref[...] = jnp.zeros_like(row_ref)
-    row_ref[0:1, :] = jnp.concatenate([gain, gain], axis=1)
-    row_ref[1:2, :] = jnp.concatenate([bias, bias], axis=1)
-    gains = row_ref[0:1, :]
+    gains = jnp.concatenate([gain, gain], axis=1)
     lane = lax.broadcasted_iota(jnp.int32, (width, LANES), 1)
     low = lane < width
     full = jnp.zeros((width, LANES), jnp.float32)
@@ -177,19 +194,18 @@
     by_one = jnp.sum(bias * (mixing + spectral_ref[:, 0:width]), axis=1, keepdims=True)
     by_one = by_one + dense_ref[:, width + 2 : width + 3]
     full = jnp.where(lane == 2 * MODES, by_input, jnp.where(lane == 2 * MODES + 1, by_one, full))
-    coarse = full.astype(jnp.bfloat16).astype(jnp.float32)
-    fine = full - coarse
+    coarse, fine = halves(full)
     joined = coarse + pltpu.roll(coarse, FEATURES, 1) + pltpu.roll(fine, 2 * FEATURES, 1)
-    map_ref[...] = joined.astype(jnp.bfloat16)
+    return joined.astype(jnp.bfloat16)
 
 
 def step_kernel(two_sided, width, scale, v_ref, rate_ref, forcing_ref, *refs):
     sides = 2 if two_sided else 1
     across, (a_ref, b_ref) = refs[:sides], refs[sides : sides + 2]
-    corners_a, corners_b = refs[sides + 2 : 2 * sides + 2], refs[2 * sides + 2 : 3 * sides + 2]
-    line_hbm, start_hbm, assign_hbm, map_ref, projection_ref, table_ref, wave_ref = refs[3 * sides + 2 : 3 * sides + 9]
-    previous, change, pay_ref, line_ref, start_ref, assign_ref, sems = refs[3 * sides + 9 : 3 * sides + 16]
-    inputs_ref, targets_ref, feature_ref, slope_ref = refs[3 * sides + 16 :]
+    corners, refs = refs[sides + 2 : 2 * sides + 2], refs[2 * sides + 2 :]
+    line_hbm, start_hbm, assign_hbm, spectral_ref, dense_ref, table_ref, wave_ref = refs[:7]
+    previous, change, pay_ref, line_ref, start_ref, assign_ref, sems = refs[7:14]
+    inputs_ref, feature_ref, slope_ref = refs[14:]
     moves = [
         pltpu.make_async_copy(source, target, sems.at[number])
         for number, (source, target) in enumerate(
@@ -212,12 +228,11 @@
     def corner(side):
         here = True if two_sided else lax.axis_index("grp") == 1 - side
 
-        def line(ref, valid):
-            whole = jnp.concatenate([ref[q : q + 1, :] for q in range(chunks)], axis=1)
-            return jnp.where(jnp.logical_and(here, valid), whole, 0.0)
-
         number = side if two_sided else 0
-        from_a, from_b = line(corners_a[number], True), line(corners_b[number], inner)
+        from_a = get_line(a_ref, LAYERS * 8 * chunks + number * chunks, chunks)
+        from_b = get_line(corners[number], 0, chunks)
+        from_a = jnp.where(here, from_a, 0.0)
+        from_b = jnp.where(jnp.logical_and(here, inner), from_b, 0.0)
         return jnp.where(even, from_b, from_a), jnp.where(even, from_a, from_b)
 
     def tendency(plane, above, below, up, down, rate, forcing):
@@ -257,17 +272,19 @@
     count = line_ref.shape[0]
     previous[:, cells_z : cells_z + LANES] = jnp.zeros((8 * cells_x, LANES), jnp.float32)
     change[:, cells_z : cells_z + LANES] = jnp.zeros((8 * cells_x, LANES), jnp.float32)
+    channel_map = feature_map(width, spectral_ref, dense_ref)
     for move in moves:
         move.wait()
-    for t in range(count):
+
+    def window(ref, t):
         line, start = line_ref[t], start_ref[t]
         inside = start & (LANES - 1)
         base = pl.multiple_of(start - inside, LANES)
-        turn = (2 * LANES - inside) & (2 * LANES - 1)
-        row = previous[pl.ds(line, 1), pl.ds(base, 2 * LANES)]
-        inputs_ref[t : t + 1, :] = pltpu.roll(row, turn, 1)[:, :SUB]
-        row = change[pl.ds(line, 1), pl.ds(base, 2 * LANES)]
-        targets_ref[t : t + 1, :] = pltpu.roll(row, turn, 1)[:, :SUB]
+        row = ref[pl.ds(line, 1), pl.ds(base, 2 * LANES)]
+        return pltpu.roll(row, (2 * LANES - inside) & (2 * LANES - 1), 1)[:, :SUB]
+
+    for t in range(count):
+        inputs_ref[t : t + 1, :] = window(previous, t)
 
     cos_w, sin_w = table_ref[0:MODES, :], table_ref[MODES:, :]
     coarse, rest = halves(inputs_ref[...])
@@ -275,14 +292,13 @@
     parts = jnp.concatenate([coarse, middle, coarse, middle, fine, coarse], axis=1).astype(jnp.bfloat16)
     waves = lax.dot_general(wave_ref[...], parts, NT, preferred_element_type=jnp.float32)
     tail = lax.broadcasted_iota(jnp.int32, (8, SUB), 0)
-    half_projection = 0.5 * projection_ref[...]
-    channel_map = map_ref[...]
+    half_projection = jnp.broadcast_to(0.5 * dense_ref[:, width + 3 : width + 4], (width, SUB))
     held = jnp.zeros((width, SUB), jnp.float32)
     lane = lax.broadcasted_iota(jnp.int32, (1, LANES), 1)
     losses = jnp.zeros((1, LANES), jnp.float32)
     root = math.sqrt(2.0 / math.pi)
     bend = 0.044715
-    group = 4
+    group = 2
     pairs = None
     for t in range(count):
         real, imag = waves[:MODES, t : t + 1], waves[MODES:, t : t + 1]
@@ -300,7 +316,7 @@
         after = before * grown
         slope = grown * (1.0 + (2.0 - grown) * (before * (root + (3.0 * root * bend) * square)))
         output = jnp.sum(after * half_projection, axis=0, keepdims=True)
-        differ = output - targets_ref[t : t + 1, :]
+        differ = output - window(change, t)
         error = jnp.sum(differ * differ, axis=1, keepdims=True)
         losses = losses + jnp.where(lane == assign_ref[t], error, 0.0)
         pull = (2.0 * scale) * differ
@@ -353,6 +369,10 @@
 
 
 def prepare_kernel(width, spectral_ref, dense_ref, row_ref, spread_ref, turned_ref):
+    row_ref[...] = jnp.zeros_like(row_ref)
+    for number in range(2):
+        row = as_row(dense_ref[:, width + number : width + number + 1])
+        row_ref[number : number + 1, :] = jnp.concatenate([row, row], axis=1)
     tall = 2 * 8
     lane = lax.broadcasted_iota(jnp.int32, (tall, LANES), 1)
     row = lax.broadcasted_iota(jnp.int32, (tall, LANES), 0)
@@ -499,13 +519,15 @@
     edge_rows = halo_rows + (packed if joined else 0)
     message = ((halo_rows, LANES), f32)
     corner_message = ((-(-chunks // 8) * 8, LANES), f32)
-    velocity, rate, forcing, near_momentum, to_a, to_b, *edges = call(
+    velocity, rate, forcing, near_momentum, dense, table, wave_table, to_a, to_b, *edges = call(
         functools.partial(edge_kernel, joined, sides),
-        [(velocity.shape, f32)] * 3 + [(momentum.shape, f32), message, message]
-        + [((edge_rows, LANES), f32)] * sides + [corner_message] * (2 * sides),
-        scratch=[pltpu.SemaphoreType.DMA((4,))],
-        ins=[HBM] * 4,
-    )(*(in_hbm(array) for array in (velocity, rate, forcing, momentum)))
+        [(velocity.shape, f32)] * 3
+        + [(array.shape, array.dtype) for array in (momentum, dense, table, wave_table)]
+        + [message, message]
+        + [((edge_rows, LANES), f32)] * sides + [corner_message] * sides,
+        scratch=[pltpu.SemaphoreType.DMA((7,))],
+        ins=[HBM] * 7,
+    )(*(in_hbm(array) for array in (velocity, rate, forcing, momentum, dense, table, wave_table)))
     far = far_map(n_grp, n_slab)
     near = {i: i ^ 1 for i in range(devices)}
     if two_sided:
@@ -518,16 +540,12 @@
         diagonal_far = [{i: i ^ n_slab if i % n_slab in ends else far[i ^ n_slab] for i in range(devices)}]
     from_grp = [hop(array, move) for array, move in zip(edges, moves)]
     from_b = hop(to_b, far)
-    corners_b = [hop(array, move) for array, move in zip(edges[2 * sides :], diagonal_far)]
-    corners_a = [
-        hop(array, {i: j ^ 1 for i, j in move.items()}) for array, move in zip(edges[sides : 2 * sides], moves)
-    ]
+    corners = [hop(array, move) for array, move in zip(edges[sides:], diagonal_far)]
+    rows = halo_rows + -(-sides * chunks // 8) * 8
+    to_a = call(
+        functools.partial(near_kernel, sides, chunks), [((rows, LANES), f32)], ins=[VMEM] * (1 + sides)
+    )(to_a, *from_grp)[0]
     from_a = hop(to_a, near)
-    channel_map, projection, rows = call(
-        functools.partial(feature_kernel, width),
-        [((width, LANES), jnp.bfloat16), ((width, LANES), f32), ((8, LANES), f32)],
-        ins=[VMEM] * 2,
-    )(spectral, dense)
     pay_rows = -(-(MODES + 2 + n_grp) // 8) * 8
     scale = 1.0 / (devices * lines * SUB)
     window = ((8 * cells_x, cells_z + LANES), f32)
@@ -537,13 +555,12 @@
         scratch=[pltpu.SMEM((lines,), jnp.int32)] * 3 + [
             pltpu.SemaphoreType.DMA((3,)),
             pltpu.VMEM((lines, SUB), f32),
-            pltpu.VMEM((lines, SUB), f32),
-            pltpu.VMEM((2, LANES, 4 * SUB), jnp.bfloat16),
-            pltpu.VMEM((2, 2 * width, 4 * SUB), jnp.bfloat16),
+            pltpu.VMEM((2, LANES, 2 * SUB), jnp.bfloat16),
+            pltpu.VMEM((2, 2 * width, 2 * SUB), jnp.bfloat16),
         ],
-        ins=[VMEM] * (5 + 3 * sides) + [HBM] * 3 + [VMEM] * 4,
-    )(velocity, rate, forcing, *from_grp, from_a, from_b, *corners_a, *corners_b,
-      in_hbm(anchor_line), in_hbm(anchor_z), in_hbm(assign.reshape(-1)), channel_map, projection, table, wave_table)
+        ins=[VMEM] * (5 + 2 * sides) + [HBM] * 3 + [VMEM] * 4,
+    )(velocity, rate, forcing, *from_grp, from_a, from_b, *corners,
+      in_hbm(anchor_line), in_hbm(anchor_z), in_hbm(assign.reshape(-1)), spectral, dense, table, wave_table)
 
     masks = hop_masks(n_grp, n_slab)
     if joined:
@@ -568,11 +585,11 @@
     else:
         payload = lax.psum(payload, AXES)
     field_now = call(field_kernel, [(velocity.shape, f32)], ins=[VMEM, VMEM, HBM])(previous, change, anchor)[0]
-    spread, turned = call(
+    rows, spread, turned = call(
         functools.partial(prepare_kernel, width),
-        [((LANES, 2 * MODES * width), jnp.bfloat16), (((MODES + 1) * width, LANES), f32)],
-        ins=[VMEM] * 3,
-    )(spectral, dense, rows)
+        [((8, LANES), f32), ((LANES, 2 * MODES * width), jnp.bfloat16), (((MODES + 1) * width, LANES), f32)],
+        ins=[VMEM] * 2,
+    )(spectral, dense)
     groups = 4
     spectral_new, dense_new, momentum_new, trainer_loss = call(
         functools.partial(update_kernel, width, lines, groups),

time: 48.2 us -> 46.9 us (0.973)
  starting transfers between devices: 20.5 us -> 19.3 us
  waiting for transfers between devices: 19.6 us -> 20.1 us
    ppermute x5 -> x4, starting transfers between devices: 7.21 us -> 5.59 us  [hop(): return lax.ppermute(array, AXES, sorted(targets.items()))]
    ppermute x5 -> x4, waiting for transfers between devices: 4.69 us -> 5.83 us  [hop(): return lax.ppermute(array, AXES, sorted(targets.items()))]
    ppermute x9, waiting for transfers between devices: 14.9 us -> 14.2 us  [swap(): return lax.ppermute(array, AXES, [(i, i ^ mask) for i in range(count)])]
  transfers between devices with their start and end apart: 14 -> 13, of which waited for: 10 -> 10; matrix products, arithmetic and copies ran while one was open for 0% -> 0% of each run, Pallas kernels for 9% -> 8%
where the time goes in v5:
time: 46.9 us; the launch traced here: 46.7 us
  waiting for transfers between devices  20.1 us (43%)
  starting transfers between devices  19.3 us (41%)
  Pallas kernels  6.55 us (14%)
  between operations  0.69 us (1%)
    ppermute x9, waiting for transfers between devices, swap(): return lax.ppermute(array, AXES, [(i, i ^ mask) for i in range(count)])  14.2 us
    ppermute x9, starting transfers between devices, swap(): return lax.ppermute(array, AXES, [(i, i ^ mask) for i in range(count)])  13.7 us
    ppermute x4, waiting for transfers between devices, hop(): return lax.ppermute(array, AXES, sorted(targets.items()))  5.83 us
    ppermute x4, starting transfers between devices, hop(): return lax.ppermute(array, AXES, sorted(targets.items()))  5.59 us
    pallas_call x1, Pallas kernels, local(): call(functools.partial(step_kernel, two_sided, width, scale), [window, wi...  2.24 us
    pallas_call x1, Pallas kernels, local(): call(functools.partial(update_kernel, width, lines, groups), [(spectral.s...  1.26 us
    pallas_call x1, Pallas kernels, local(): call(functools.partial(edge_kernel, joined, sides), [(velocity.shape, f32...  1.24 us
  transfers between devices with their start and end apart: 13, of which 10 were waited for; matrix products, arithmetic and copies ran while one was open for 0% of the time, Pallas kernels for 8%

profile of v5, /device:TPU:0, one launch (start us, length us, event | category | flops | bytes accessed | tf_op | source)
XLA Modules:
  0.0 46.7 jit_solution(6901168927875466926)
XLA Ops:
  0.6 1.2 %shard_map.146 = (f32[8,8,512]{2,1,0:T(8,128)S(1)}, f32[8,8,512]{2,1,0:T(8,128)S(1)}, f32[8,8,512]{2,1,0:T(8,128)S(1)}, f32[64,64]{1,0:T(8,128)S(1)}, f32[64,68]...) custom-call(f32[8,8,512]{2,1,0:T(8,128)} %v_hbm.1, ...), custom_call_target="tpu_custom_call" | custom-call | flops 1000000 | bytes 1320960 | tf_op jit(solution)/shard_map/pallas_call | solution.py:522
  1.9 3.1 %collective-permute-start = (f32[128,128]{1,0:T(8,128)S(1)}, f32[128,128]{1,0:T(8,128)S(1)}, u32[]{:S(2)}, u32[]{:S(2)}) collective-permute-start(f32[128,128]{1,0:T(8,128)S(1)} %get-tuple-element.29), channel_id=1, source_target_pairs={{0,16},{1,17},{2,18},{3,19},{4,20},{5,21},{6,22},{7,23},{8,24},{9,... | collective-permute-start | bytes 196616 | tf_op jit(solution)/shard_map/ppermute | solution.py:491
  4.9 2.2 %collective-permute-done.refs_0_ = f32[128,128]{1,0:T(8,128)S(1)} collective-permute-done((f32[128,128]{1,0:T(8,128)S(1)}, f32[128,128]{1,0:T(8,128)S(1)}, u32[]{:S(2)}, u32[]{:S(2)}) %collective-permute-start) | collective-permute-done | bytes 65568 | tf_op jit(solution)/shard_map/ppermute | solution.py:491
  7.2 0.0 copy-start
  7.2 1.4 %collective-permute-start.9 = (f32[64,128]{1,0:T(8,128)S(1)}, f32[64,128]{1,0:T(8,128)S(1)}, u32[]{:S(2)}, u32[]{:S(2)}) collective-permute-start(f32[64,128]{1,0:T(8,128)S(1)} %pad_maximum_fusion.2), channel_id=1, source_target_pairs={{0,9},{1,8},{2,11},{3,10},{4,13},{5,12},{6,15},{7,14},{8,1},{9,0},... | collective-permute-start | bytes 98312 | tf_op jit(solution)/shard_map/ppermute | solution.py:499
  8.6 2.9 %collective-permute-done.9 = f32[64,128]{1,0:T(8,128)S(1)} collective-permute-done((f32[64,128]{1,0:T(8,128)S(1)}, f32[64,128]{1,0:T(8,128)S(1)}, u32[]{:S(2)}, u32[]{:S(2)}) %collective-permute-start.9) | collective-permute-done | bytes 32800 | tf_op jit(solution)/shard_map/ppermute | solution.py:499
  11.5 1.9 %collective-permute-start.10 = (f32[128,128]{1,0:T(8,128)S(1)}, f32[128,128]{1,0:T(8,128)S(1)}, u32[]{:S(2)}, u32[]{:S(2)}) collective-permute-start(f32[128,128]{1,0:T(8,128)S(1)} %pad_maximum_fusion.1), channel_id=1, source_target_pairs={{0,5},{1,4},{2,7},{3,6},{4,1},{5,0},{6,3},{7,2},{8,13},{9,12},{10,... | collective-permute-start | bytes 196616 | tf_op jit(solution)/shard_map/ppermute | solution.py:499
  13.4 2.2 %collective-permute-done.10 = f32[128,128]{1,0:T(8,128)S(1)} collective-permute-done((f32[128,128]{1,0:T(8,128)S(1)}, f32[128,128]{1,0:T(8,128)S(1)}, u32[]{:S(2)}, u32[]{:S(2)}) %collective-permute-start.10) | collective-permute-done | bytes 65568 | tf_op jit(solution)/shard_map/ppermute | solution.py:499
  15.6 1.9 %collective-permute-start.11 = (f32[256,128]{1,0:T(8,128)S(1)}, f32[256,128]{1,0:T(8,128)S(1)}, u32[]{:S(2)}, u32[]{:S(2)}) collective-permute-start(f32[256,128]{1,0:T(8,128)S(1)} %pad_maximum_fusion), channel_id=1, source_target_pairs={{0,3},{1,2},{2,1},{3,0},{4,7},{5,6},{6,5},{7,4},{8,11},{9,10},{10,... | collective-permute-start | bytes 393224 | tf_op jit(solution)/shard_map/ppermute | solution.py:499
  17.5 3.6 %collective-permute-done.11 = f32[256,128]{1,0:T(8,128)S(1)} collective-permute-done((f32[256,128]{1,0:T(8,128)S(1)}, f32[256,128]{1,0:T(8,128)S(1)}, u32[]{:S(2)}, u32[]{:S(2)}) %collective-permute-start.11) | collective-permute-done | bytes 131104 | tf_op jit(solution)/shard_map/ppermute | solution.py:499
  21.1 0.3 collective-permute-start.12
  21.5 0.3 collective-permute-start.1
  21.8 2.2 %collective-permute-start.2 = (f32[96,128]{1,0:T(8,128)S(1)}, f32[96,128]{1,0:T(8,128)S(1)}, u32[]{:S(2)}, u32[]{:S(2)}) collective-permute-start(f32[96,128]{1,0:T(8,128)S(1)} %get-tuple-element.31), channel_id=1, source_target_pairs={{0,16},{1,2},{2,1},{3,4},{4,3},{5,6},{6,5},{7,8},{8,7},{9,10},{10,... | collective-permute-start | bytes 147464 | tf_op jit(solution)/shard_map/ppermute | solution.py:491
  24.0 0.0 collective-permute-start.3
  24.0 3.6 %collective-permute-done.3.refs_3_ = f32[8,128]{1,0:T(8,128)S(1)} collective-permute-done((f32[8,128]{1,0:T(8,128)S(1)}, f32[8,128]{1,0:T(8,128)S(1)}, u32[]{:S(2)}, u32[]{:S(2)}) %collective-permute-start.3) | collective-permute-done | bytes 4128 | tf_op jit(solution)/shard_map/ppermute | solution.py:491
  27.6 0.0 collective-permute-done.2.refs_2_
  27.6 0.0 collective-permute-done.1.refs_1_
  27.6 0.0 copy-done
  27.6 2.2 %shard_map.148 = (f32[64,640]{1,0:T(8,128)S(1)}, f32[64,640]{1,0:T(8,128)S(1)}, f32[24,128]{1,0:T(8,128)S(1)}) custom-call(f32[8,8,512]{2,1,0:T(8,128)S(1)} %get-tuple-element.26.v_ref, f32[8,8,512]{2,1,0:T(8,128)S(1)} %get-tuple-element.27.rate_ref, f32[8,8,512]{2,1,0:T(8,128)S(1)} %get-tuple-element.28.forcing_ref, ...), custom_call_target="tpu_custom_call" | custom-call | flops 1000000 | bytes 679936 | tf_op jit(solution)/shard_map/pallas_call | solution.py:552
  29.8 0.5 %collective-permute-start.4 = (f32[24,128]{1,0:T(8,128)S(1)}, f32[24,128]{1,0:T(8,128)S(1)}, u32[]{:S(2)}, u32[]{:S(2)}) collective-permute-start(f32[24,128]{1,0:T(8,128)S(1)} %get-tuple-element.38), channel_id=1, source_target_pairs={{0,1},{1,0},{2,3},{3,2},{4,5},{5,4},{6,7},{7,6},{8,9},{9,8},{10,11... | collective-permute-start | bytes 36872 | tf_op jit(solution)/shard_map/ppermute | solution.py:499
  30.3 0.8 %collective-permute-done.4 = f32[24,128]{1,0:T(8,128)S(1)} collective-permute-done((f32[24,128]{1,0:T(8,128)S(1)}, f32[24,128]{1,0:T(8,128)S(1)}, u32[]{:S(2)}, u32[]{:S(2)}) %collective-permute-start.4) | collective-permute-done | bytes 12320 | tf_op jit(solution)/shard_map/ppermute | solution.py:499
  31.2 1.5 %collective-permute-start.5 = (f32[24,128]{1,0:T(8,128)S(1)}, f32[24,128]{1,0:T(8,128)S(1)}, u32[]{:S(2)}, u32[]{:S(2)}) collective-permute-start(f32[24,128]{1,0:T(8,128)S(1)} %add.15._), channel_id=1, source_target_pairs={{0,17},{1,16},{2,19},{3,18},{4,21},{5,20},{6,23},{7,22},{8,25},{9,... | collective-permute-start | bytes 36872 | tf_op jit(solution)/shard_map/ppermute | solution.py:499
  32.6 1.7 %collective-permute-done.5 = f32[24,128]{1,0:T(8,128)S(1)} collective-permute-done((f32[24,128]{1,0:T(8,128)S(1)}, f32[24,128]{1,0:T(8,128)S(1)}, u32[]{:S(2)}, u32[]{:S(2)}) %collective-permute-start.5) | collective-permute-done | bytes 12320 | tf_op jit(solution)/shard_map/ppermute | solution.py:499
  34.3 2.4 %collective-permute-start.6 = (f32[24,128]{1,0:T(8,128)S(1)}, f32[24,128]{1,0:T(8,128)S(1)}, u32[]{:S(2)}, u32[]{:S(2)}) collective-permute-start(f32[24,128]{1,0:T(8,128)S(1)} %add.16), channel_id=1, source_target_pairs={{0,3},{1,2},{2,1},{3,0},{4,7},{5,6},{6,5},{7,4},{8,11},{9,10},{10,... | collective-permute-start | bytes 36872 | tf_op jit(solution)/shard_map/ppermute | solution.py:499
  36.7 1.4 %collective-permute-done.6 = f32[24,128]{1,0:T(8,128)S(1)} collective-permute-done((f32[24,128]{1,0:T(8,128)S(1)}, f32[24,128]{1,0:T(8,128)S(1)}, u32[]{:S(2)}, u32[]{:S(2)}) %collective-permute-start.6) | collective-permute-done | bytes 12320 | tf_op jit(solution)/shard_map/ppermute | solution.py:499
  38.1 2.4 %collective-permute-start.7 = (f32[24,128]{1,0:T(8,128)S(1)}, f32[24,128]{1,0:T(8,128)S(1)}, u32[]{:S(2)}, u32[]{:S(2)}) collective-permute-start(f32[24,128]{1,0:T(8,128)S(1)} %add.17), channel_id=1, source_target_pairs={{0,9},{1,8},{2,11},{3,10},{4,13},{5,12},{6,15},{7,14},{8,1},{9,0},... | collective-permute-start | bytes 36872 | tf_op jit(solution)/shard_map/ppermute | solution.py:499
  40.5 1.6 %collective-permute-done.7 = f32[24,128]{1,0:T(8,128)S(1)} collective-permute-done((f32[24,128]{1,0:T(8,128)S(1)}, f32[24,128]{1,0:T(8,128)S(1)}, u32[]{:S(2)}, u32[]{:S(2)}) %collective-permute-start.7) | collective-permute-done | bytes 12320 | tf_op jit(solution)/shard_map/ppermute | solution.py:499
  42.1 1.4 %collective-permute-start.8 = (f32[24,128]{1,0:T(8,128)S(1)}, f32[24,128]{1,0:T(8,128)S(1)}, u32[]{:S(2)}, u32[]{:S(2)}) collective-permute-start(f32[24,128]{1,0:T(8,128)S(1)} %add.18), channel_id=1, source_target_pairs={{0,5},{1,4},{2,7},{3,6},{4,1},{5,0},{6,3},{7,2},{8,13},{9,12},{10,... | collective-permute-start | bytes 36872 | tf_op jit(solution)/shard_map/ppermute | solution.py:499
  43.5 0.9 %shard_map.151 = (f32[8,128]{1,0:T(8,128)S(1)}, bf16[128,2048]{1,0:T(8,128)(2,1)S(1)}, f32[1088,128]{1,0:T(8,128)S(1)}) custom-call(f32[64,2048]{1,0:T(8,128)S(1)} %bitcast.6, f32[64,68]{1,0:T(8,128)S(1)} %get-tuple-element.33.refs_8_.dense_ref), custom_call_target="tpu_custom_call" | custom-call | flops 1000000 | bytes 2170880 | tf_op jit(solution)/shard_map/pallas_call | solution.py:588
  44.4 0.7 %shard_map.149 = f32[8,8,512]{2,1,0:T(8,128)} custom-call(f32[64,640]{1,0:T(8,128)S(1)} %get-tuple-element.36.previous, f32[64,640]{1,0:T(8,128)S(1)} %get-tuple-element.37.change, f32[24,128]{1,0:T(8,128)S(1)} %add.15._), custom_call_target="tpu_custom_call" | custom-call | flops 1000000 | bytes 262144 | tf_op jit(solution)/shard_map/pallas_call | solution.py:587
  45.1 0.1 collective-permute-done.8
  45.2 0.0 collective-permute-done.12.other_ref
  45.2 0.2 shard_map.150.base_ref
  45.5 1.3 %shard_map.152 = (f32[64,2048]{1,0:T(8,128)}, f32[64,68]{1,0:T(8,128)}, f32[64,64]{1,0:T(8,128)}, f32[1,1]{1,0:T(1,128)}) custom-call(f32[24,128]{1,0:T(8,128)S(1)} %add.19.pay_ref, f32[64,2048]{1,0:T(8,128)S(1)} %shard_map.150.base_ref, f32[64,68]{1,0:T(8,128)S(1)} %get-tuple-element.33.refs_8_.dense_ref, f32[64,64]{1,0:T(8,128)S(1)} %get-tuple-element.39.momentum_ref, ...), custom_call_target="tpu_custom_call" | custom-call | flops 1000000 | bytes 1116168 | tf_op jit(solution)/shard_map/pallas_call | solution.py:594
  (14 shorter events, 0.1 us)
Async XLA Ops:
  1.9 5.3 %collective-permute-start = (f32[128,128]{1,0:T(8,128)S(1)}, f32[128,128]{1,0:T(8,128)S(1)}, u32[]{:S(2)}, u32[]{:S(2)}) collective-permute-start(f32[128,128]{1,0:T(8,128)S(1)} %get-tuple-element.29), channel_id=1, source_target_pairs={{0,16},{1,17},{2,18},{3,19},{4,20},{5,21},{6,22},{7,23},{8,24},{9,... | collective-permute-start | bytes 196616 | tf_op jit(solution)/shard_map/ppermute | solution.py:491
  7.2 20.4 %copy-start = (f32[2048,64]{0,1:T(8,128)S(1)}, f32[2048,64]{0,1:T(8,128)}, u32[]{:S(2)}) copy-start(f32[2048,64]{0,1:T(8,128)} %param.17) | copy-start | bytes 1572868
  7.2 4.3 %collective-permute-start.9 = (f32[64,128]{1,0:T(8,128)S(1)}, f32[64,128]{1,0:T(8,128)S(1)}, u32[]{:S(2)}, u32[]{:S(2)}) collective-permute-start(f32[64,128]{1,0:T(8,128)S(1)} %pad_maximum_fusion.2), channel_id=1, source_target_pairs={{0,9},{1,8},{2,11},{3,10},{4,13},{5,12},{6,15},{7,14},{8,1},{9,0},... | collective-permute-start | bytes 98312 | tf_op jit(solution)/shard_map/ppermute | solution.py:499
  11.5 4.1 %collective-permute-start.10 = (f32[128,128]{1,0:T(8,128)S(1)}, f32[128,128]{1,0:T(8,128)S(1)}, u32[]{:S(2)}, u32[]{:S(2)}) collective-permute-start(f32[128,128]{1,0:T(8,128)S(1)} %pad_maximum_fusion.1), channel_id=1, source_target_pairs={{0,5},{1,4},{2,7},{3,6},{4,1},{5,0},{6,3},{7,2},{8,13},{9,12},{10,... | collective-permute-start | bytes 196616 | tf_op jit(solution)/shard_map/ppermute | solution.py:499
  15.6 5.5 %collective-permute-start.11 = (f32[256,128]{1,0:T(8,128)S(1)}, f32[256,128]{1,0:T(8,128)S(1)}, u32[]{:S(2)}, u32[]{:S(2)}) collective-permute-start(f32[256,128]{1,0:T(8,128)S(1)} %pad_maximum_fusion), channel_id=1, source_target_pairs={{0,3},{1,2},{2,1},{3,0},{4,7},{5,6},{6,5},{7,4},{8,11},{9,10},{10,... | collective-permute-start | bytes 393224 | tf_op jit(solution)/shard_map/ppermute | solution.py:499
  21.1 24.1 %collective-permute-start.12 = (f32[512,128]{1,0:T(8,128)S(1)}, f32[512,128]{1,0:T(8,128)S(1)}, u32[]{:S(2)}, u32[]{:S(2)}) collective-permute-start(f32[512,128]{1,0:T(8,128)S(1)} %constant_dynamic-update-slice_fusion.mine_ref), channel_id=1, source_target_pairs={{0,1},{1,0},{2,3},{3,2},{4,5},{5,4},{6,7},{7,6},{8,9},{9,8},{10,11... | collective-permute-start | bytes 786440 | tf_op jit(solution)/shard_map/ppermute | solution.py:499
  21.5 6.1 %collective-permute-start.1 = (f32[104,128]{1,0:T(8,128)S(1)}, f32[104,128]{1,0:T(8,128)S(1)}, u32[]{:S(2)}, u32[]{:S(2)}) collective-permute-start(f32[104,128]{1,0:T(8,128)S(1)} %shard_map.147), channel_id=1, source_target_pairs={{0,1},{1,0},{2,3},{3,2},{4,5},{5,4},{6,7},{7,6},{8,9},{9,8},{10,11... | collective-permute-start | bytes 159752 | tf_op jit(solution)/shard_map/ppermute | solution.py:491
  21.8 5.8 %collective-permute-start.2 = (f32[96,128]{1,0:T(8,128)S(1)}, f32[96,128]{1,0:T(8,128)S(1)}, u32[]{:S(2)}, u32[]{:S(2)}) collective-permute-start(f32[96,128]{1,0:T(8,128)S(1)} %get-tuple-element.31), channel_id=1, source_target_pairs={{0,16},{1,2},{2,1},{3,4},{4,3},{5,6},{6,5},{7,8},{8,7},{9,10},{10,... | collective-permute-start | bytes 147464 | tf_op jit(solution)/shard_map/ppermute | solution.py:491
  24.0 3.6 %collective-permute-start.3 = (f32[8,128]{1,0:T(8,128)S(1)}, f32[8,128]{1,0:T(8,128)S(1)}, u32[]{:S(2)}, u32[]{:S(2)}) collective-permute-start(f32[8,128]{1,0:T(8,128)S(1)} %get-tuple-element.32), channel_id=1, source_target_pairs={{0,16},{1,18},{2,17},{3,20},{4,19},{5,22},{6,21},{7,24},{8,23},{9,... | collective-permute-start | bytes 12296 | tf_op jit(solution)/shard_map/ppermute | solution.py:491
  29.8 1.3 %collective-permute-start.4 = (f32[24,128]{1,0:T(8,128)S(1)}, f32[24,128]{1,0:T(8,128)S(1)}, u32[]{:S(2)}, u32[]{:S(2)}) collective-permute-start(f32[24,128]{1,0:T(8,128)S(1)} %get-tuple-element.38), channel_id=1, source_target_pairs={{0,1},{1,0},{2,3},{3,2},{4,5},{5,4},{6,7},{7,6},{8,9},{9,8},{10,11... | collective-permute-start | bytes 36872 | tf_op jit(solution)/shard_map/ppermute | solution.py:499
  31.2 3.1 %collective-permute-start.5 = (f32[24,128]{1,0:T(8,128)S(1)}, f32[24,128]{1,0:T(8,128)S(1)}, u32[]{:S(2)}, u32[]{:S(2)}) collective-permute-start(f32[24,128]{1,0:T(8,128)S(1)} %add.15._), channel_id=1, source_target_pairs={{0,17},{1,16},{2,19},{3,18},{4,21},{5,20},{6,23},{7,22},{8,25},{9,... | collective-permute-start | bytes 36872 | tf_op jit(solution)/shard_map/ppermute | solution.py:499
  34.3 3.8 %collective-permute-start.6 = (f32[24,128]{1,0:T(8,128)S(1)}, f32[24,128]{1,0:T(8,128)S(1)}, u32[]{:S(2)}, u32[]{:S(2)}) collective-permute-start(f32[24,128]{1,0:T(8,128)S(1)} %add.16), channel_id=1, source_target_pairs={{0,3},{1,2},{2,1},{3,0},{4,7},{5,6},{6,5},{7,4},{8,11},{9,10},{10,... | collective-permute-start | bytes 36872 | tf_op jit(solution)/shard_map/ppermute | solution.py:499
  38.1 4.0 %collective-permute-start.7 = (f32[24,128]{1,0:T(8,128)S(1)}, f32[24,128]{1,0:T(8,128)S(1)}, u32[]{:S(2)}, u32[]{:S(2)}) collective-permute-start(f32[24,128]{1,0:T(8,128)S(1)} %add.17), channel_id=1, source_target_pairs={{0,9},{1,8},{2,11},{3,10},{4,13},{5,12},{6,15},{7,14},{8,1},{9,0},... | collective-permute-start | bytes 36872 | tf_op jit(solution)/shard_map/ppermute | solution.py:499
  42.1 3.1 %collective-permute-start.8 = (f32[24,128]{1,0:T(8,128)S(1)}, f32[24,128]{1,0:T(8,128)S(1)}, u32[]{:S(2)}, u32[]{:S(2)}) collective-permute-start(f32[24,128]{1,0:T(8,128)S(1)} %add.18), channel_id=1, source_target_pairs={{0,5},{1,4},{2,7},{3,6},{4,1},{5,0},{6,3},{7,2},{8,13},{9,12},{10,... | collective-permute-start | bytes 36872 | tf_op jit(solution)/shard_map/ppermute | solution.py:499

commit v6 on v5

--- a/solution.py
+++ b/solution.py
@@ -283,8 +283,10 @@
         row = ref[pl.ds(line, 1), pl.ds(base, 2 * LANES)]
         return pltpu.roll(row, (2 * LANES - inside) & (2 * LANES - 1), 1)[:, :SUB]
 
+    targets = []
     for t in range(count):
         inputs_ref[t : t + 1, :] = window(previous, t)
+        targets.append(window(change, t))
 
     cos_w, sin_w = table_ref[0:MODES, :], table_ref[MODES:, :]
     coarse, rest = halves(inputs_ref[...])
@@ -316,7 +318,7 @@
         after = before * grown
         slope = grown * (1.0 + (2.0 - grown) * (before * (root + (3.0 * root * bend) * square)))
         output = jnp.sum(after * half_projection, axis=0, keepdims=True)
-        differ = output - window(change, t)
+        differ = output - targets[t]
         error = jnp.sum(differ * differ, axis=1, keepdims=True)
         losses = losses + jnp.where(lane == assign_ref[t], error, 0.0)
         pull = (2.0 * scale) * differ
@@ -351,15 +353,19 @@
     here = lax.axis_index("grp") * lax.axis_size("slab") + lax.axis_index("slab")
     rows = width // 2
     low = lax.broadcasted_iota(jnp.int32, (rows, LANES), 1) < width
+    even = lax.rem(here, 2) == 0
     for number in range(mine_ref.shape[0] // rows):
         source = here
-        for bit, mask in enumerate(masks):
+        twin_even = twin_odd = 0
+        for bit, (at_even, at_odd) in enumerate(masks):
             if number >> bit & 1:
-                source = source ^ mask
-        even = lax.rem(source, 2) == 0
+                source = source ^ jnp.where(even, at_even, at_odd)
+                twin_even |= 1 << [odd for _, odd in masks].index(at_even)
+                twin_odd |= 1 << [ev for ev, _ in masks].index(at_odd)
+        twin = jnp.where(even, twin_even, twin_odd)
         columns = pl.ds(pl.multiple_of((source // 2) * LANES, LANES), LANES)
         mine = mine_ref[number * rows : (number + 1) * rows, :]
-        other = other_ref[number * rows : (number + 1) * rows, :]
+        other = other_ref[pl.ds(pl.multiple_of(twin * rows, rows), rows), :]
         first, second = jnp.where(even, mine, other), jnp.where(even, other, mine)
         top = jnp.where(low, first, pltpu.roll(second, width, 1))
         bottom = jnp.where(low, pltpu.roll(first, width, 1), second)
@@ -565,13 +571,15 @@
     masks = hop_masks(n_grp, n_slab)
     if joined:
         mine = jnp.concatenate([edges[0][halo_rows:], from_grp[0][halo_rows:]], axis=0)
-        order = [n_slab] + masks[3:] + masks[2:3] + [1]
-        for mask in order[1:-1]:
-            other = swap(mine, mask, devices)
+        bits = [1 << bit for bit in range(n_slab.bit_length() - 2, 0, -1)]
+        order = list(zip(bits, bits[:-2] + bits[-2:][::-1]))
+        for at_even, at_odd in order:
+            other = hop(mine, {i: i ^ (at_odd if i & 1 else at_even) for i in range(devices)})
             mine = jnp.concatenate([mine, other], axis=0)
-        other = swap(mine, order[-1], devices)
+        other = hop(mine, near)
+        order = [(n_slab, n_slab)] + order
         base = call(
-            functools.partial(base_kernel, order[:-1], width), [(spectral.shape, f32)], ins=[VMEM] * 3
+            functools.partial(base_kernel, order, width), [(spectral.shape, f32)], ins=[VMEM] * 3
         )(spectral, mine, other)[0]
     else:
         whole = lax.all_gather(momentum, AXES, axis=0, tiled=True)

time: 46.9 us -> 47.7 us (1.017)
  starting transfers between devices: 19.3 us -> 21 us
  waiting for transfers between devices: 20.1 us -> 19.2 us
    ppermute x9 -> x5, waiting for transfers between devices: 14.2 us -> 5.51 us  [swap(): return lax.ppermute(array, AXES, [(i, i ^ mask) for i in range(count)])]
    ppermute x4 -> x8, waiting for transfers between devices: 5.83 us -> 13.7 us  [hop(): return lax.ppermute(array, AXES, sorted(targets.items()))]
    ppermute x4 -> x8, starting transfers between devices: 5.59 us -> 12.7 us  [hop(): return lax.ppermute(array, AXES, sorted(targets.items()))]
    ppermute x9 -> x5, starting transfers between devices: 13.7 us -> 8.27 us  [swap(): return lax.ppermute(array, AXES, [(i, i ^ mask) for i in range(count)])]
where the time goes in v6:
time: 47.7 us; the launch traced here: 47.5 us
  starting transfers between devices  21 us (44%)
  waiting for transfers between devices  19.2 us (40%)
  Pallas kernels  6.56 us (14%)
  between operations  0.71 us (1%)
    ppermute x8, waiting for transfers between devices, hop(): return lax.ppermute(array, AXES, sorted(targets.items()))  13.7 us
    ppermute x8, starting transfers between devices, hop(): return lax.ppermute(array, AXES, sorted(targets.items()))  12.7 us
    ppermute x5, starting transfers between devices, swap(): return lax.ppermute(array, AXES, [(i, i ^ mask) for i in range(count)])  8.27 us
    ppermute x5, waiting for transfers between devices, swap(): return lax.ppermute(array, AXES, [(i, i ^ mask) for i in range(count)])  5.51 us
    pallas_call x1, Pallas kernels, local(): call(functools.partial(step_kernel, two_sided, width, scale), [window, wi...  2.24 us
    pallas_call x1, Pallas kernels, local(): call(functools.partial(update_kernel, width, lines, groups), [(spectral.s...  1.26 us
    pallas_call x1, Pallas kernels, local(): call(functools.partial(edge_kernel, joined, sides), [(velocity.shape, f32...  1.24 us
  transfers between devices with their start and end apart: 13, of which 10 were waited for; matrix products, arithmetic and copies ran while one was open for 0% of the time, Pallas kernels for 8%

profile of v6, /device:TPU:0, one launch (start us, length us, event | category | flops | bytes accessed | tf_op | source)
XLA Modules:
  0.0 47.5 jit_solution(7582822778034267344)
XLA Ops:
  0.6 1.2 %shard_map.146 = (f32[8,8,512]{2,1,0:T(8,128)S(1)}, f32[8,8,512]{2,1,0:T(8,128)S(1)}, f32[8,8,512]{2,1,0:T(8,128)S(1)}, f32[64,64]{1,0:T(8,128)S(1)}, f32[64,68]...) custom-call(f32[8,8,512]{2,1,0:T(8,128)} %v_hbm.1, ...), custom_call_target="tpu_custom_call" | custom-call | flops 1000000 | bytes 1320960 | tf_op jit(solution)/shard_map/pallas_call | solution.py:528
  1.9 3.1 %collective-permute-start = (f32[128,128]{1,0:T(8,128)S(1)}, f32[128,128]{1,0:T(8,128)S(1)}, u32[]{:S(2)}, u32[]{:S(2)}) collective-permute-start(f32[128,128]{1,0:T(8,128)S(1)} %get-tuple-element.29), channel_id=1, source_target_pairs={{0,16},{1,17},{2,18},{3,19},{4,20},{5,21},{6,22},{7,23},{8,24},{9,... | collective-permute-start | bytes 196616 | tf_op jit(solution)/shard_map/ppermute | solution.py:497
  4.9 2.2 %collective-permute-done.refs_0_ = f32[128,128]{1,0:T(8,128)S(1)} collective-permute-done((f32[128,128]{1,0:T(8,128)S(1)}, f32[128,128]{1,0:T(8,128)S(1)}, u32[]{:S(2)}, u32[]{:S(2)}) %collective-permute-start) | collective-permute-done | bytes 65568 | tf_op jit(solution)/shard_map/ppermute | solution.py:497
  7.2 0.0 copy-start
  7.2 3.2 %collective-permute-start.9 = (f32[64,128]{1,0:T(8,128)S(1)}, f32[64,128]{1,0:T(8,128)S(1)}, u32[]{:S(2)}, u32[]{:S(2)}) collective-permute-start(f32[64,128]{1,0:T(8,128)S(1)} %pad_maximum_fusion.2), channel_id=1, source_target_pairs={{0,8},{1,9},{2,10},{3,11},{4,12},{5,13},{6,14},{7,15},{8,0},{9,1},... | collective-permute-start | bytes 98312 | tf_op jit(solution)/shard_map/ppermute | solution.py:497
  10.4 1.9 %collective-permute-done.9 = f32[64,128]{1,0:T(8,128)S(1)} collective-permute-done((f32[64,128]{1,0:T(8,128)S(1)}, f32[64,128]{1,0:T(8,128)S(1)}, u32[]{:S(2)}, u32[]{:S(2)}) %collective-permute-start.9) | collective-permute-done | bytes 32800 | tf_op jit(solution)/shard_map/ppermute | solution.py:497
  12.3 1.9 %collective-permute-start.10 = (f32[128,128]{1,0:T(8,128)S(1)}, f32[128,128]{1,0:T(8,128)S(1)}, u32[]{:S(2)}, u32[]{:S(2)}) collective-permute-start(f32[128,128]{1,0:T(8,128)S(1)} %pad_maximum_fusion.1), channel_id=1, source_target_pairs={{0,4},{1,3},{2,6},{3,1},{4,0},{5,7},{6,2},{7,5},{8,12},{9,11},{10,... | collective-permute-start | bytes 196616 | tf_op jit(solution)/shard_map/ppermute | solution.py:497
  14.2 3.0 %collective-permute-done.10 = f32[128,128]{1,0:T(8,128)S(1)} collective-permute-done((f32[128,128]{1,0:T(8,128)S(1)}, f32[128,128]{1,0:T(8,128)S(1)}, u32[]{:S(2)}, u32[]{:S(2)}) %collective-permute-start.10) | collective-permute-done | bytes 65568 | tf_op jit(solution)/shard_map/ppermute | solution.py:497
  17.2 1.9 %collective-permute-start.11 = (f32[256,128]{1,0:T(8,128)S(1)}, f32[256,128]{1,0:T(8,128)S(1)}, u32[]{:S(2)}, u32[]{:S(2)}) collective-permute-start(f32[256,128]{1,0:T(8,128)S(1)} %pad_maximum_fusion), channel_id=1, source_target_pairs={{0,2},{1,5},{2,0},{3,7},{4,6},{5,1},{6,4},{7,3},{8,10},{9,13},{10,... | collective-permute-start | bytes 393224 | tf_op jit(solution)/shard_map/ppermute | solution.py:497
  19.1 3.1 %collective-permute-done.11 = f32[256,128]{1,0:T(8,128)S(1)} collective-permute-done((f32[256,128]{1,0:T(8,128)S(1)}, f32[256,128]{1,0:T(8,128)S(1)}, u32[]{:S(2)}, u32[]{:S(2)}) %collective-permute-start.11) | collective-permute-done | bytes 131104 | tf_op jit(solution)/shard_map/ppermute | solution.py:497
  22.2 0.1 collective-permute-start.12
  22.3 0.6 %collective-permute-start.1 = (f32[104,128]{1,0:T(8,128)S(1)}, f32[104,128]{1,0:T(8,128)S(1)}, u32[]{:S(2)}, u32[]{:S(2)}) collective-permute-start(f32[104,128]{1,0:T(8,128)S(1)} %shard_map.147), channel_id=1, source_target_pairs={{0,1},{1,0},{2,3},{3,2},{4,5},{5,4},{6,7},{7,6},{8,9},{9,8},{10,11... | collective-permute-start | bytes 159752 | tf_op jit(solution)/shard_map/ppermute | solution.py:497
  22.9 1.9 %collective-permute-start.2 = (f32[96,128]{1,0:T(8,128)S(1)}, f32[96,128]{1,0:T(8,128)S(1)}, u32[]{:S(2)}, u32[]{:S(2)}) collective-permute-start(f32[96,128]{1,0:T(8,128)S(1)} %get-tuple-element.31), channel_id=1, source_target_pairs={{0,16},{1,2},{2,1},{3,4},{4,3},{5,6},{6,5},{7,8},{8,7},{9,10},{10,... | collective-permute-start | bytes 147464 | tf_op jit(solution)/shard_map/ppermute | solution.py:497
  24.8 0.1 collective-permute-start.3
  24.9 3.5 %collective-permute-done.3.refs_3_ = f32[8,128]{1,0:T(8,128)S(1)} collective-permute-done((f32[8,128]{1,0:T(8,128)S(1)}, f32[8,128]{1,0:T(8,128)S(1)}, u32[]{:S(2)}, u32[]{:S(2)}) %collective-permute-start.3) | collective-permute-done | bytes 4128 | tf_op jit(solution)/shard_map/ppermute | solution.py:497
  28.4 0.0 collective-permute-done.2.refs_2_
  28.4 0.0 collective-permute-done.1.refs_1_
  28.4 0.0 copy-done
  28.4 2.2 %shard_map.148 = (f32[64,640]{1,0:T(8,128)S(1)}, f32[64,640]{1,0:T(8,128)S(1)}, f32[24,128]{1,0:T(8,128)S(1)}) custom-call(f32[8,8,512]{2,1,0:T(8,128)S(1)} %get-tuple-element.26.v_ref, f32[8,8,512]{2,1,0:T(8,128)S(1)} %get-tuple-element.27.rate_ref, f32[8,8,512]{2,1,0:T(8,128)S(1)} %get-tuple-element.28.forcing_ref, ...), custom_call_target="tpu_custom_call" | custom-call | flops 1000000 | bytes 679936 | tf_op jit(solution)/shard_map/pallas_call | solution.py:558
  30.7 0.5 %collective-permute-start.4 = (f32[24,128]{1,0:T(8,128)S(1)}, f32[24,128]{1,0:T(8,128)S(1)}, u32[]{:S(2)}, u32[]{:S(2)}) collective-permute-start(f32[24,128]{1,0:T(8,128)S(1)} %get-tuple-element.38), channel_id=1, source_target_pairs={{0,1},{1,0},{2,3},{3,2},{4,5},{5,4},{6,7},{7,6},{8,9},{9,8},{10,11... | collective-permute-start | bytes 36872 | tf_op jit(solution)/shard_map/ppermute | solution.py:505
  31.1 0.8 %collective-permute-done.4 = f32[24,128]{1,0:T(8,128)S(1)} collective-permute-done((f32[24,128]{1,0:T(8,128)S(1)}, f32[24,128]{1,0:T(8,128)S(1)}, u32[]{:S(2)}, u32[]{:S(2)}) %collective-permute-start.4) | collective-permute-done | bytes 12320 | tf_op jit(solution)/shard_map/ppermute | solution.py:505
  32.0 1.5 %collective-permute-start.5 = (f32[24,128]{1,0:T(8,128)S(1)}, f32[24,128]{1,0:T(8,128)S(1)}, u32[]{:S(2)}, u32[]{:S(2)}) collective-permute-start(f32[24,128]{1,0:T(8,128)S(1)} %add.15._), channel_id=1, source_target_pairs={{0,17},{1,16},{2,19},{3,18},{4,21},{5,20},{6,23},{7,22},{8,25},{9,... | collective-permute-start | bytes 36872 | tf_op jit(solution)/shard_map/ppermute | solution.py:505
  33.4 1.7 %collective-permute-done.5 = f32[24,128]{1,0:T(8,128)S(1)} collective-permute-done((f32[24,128]{1,0:T(8,128)S(1)}, f32[24,128]{1,0:T(8,128)S(1)}, u32[]{:S(2)}, u32[]{:S(2)}) %collective-permute-start.5) | collective-permute-done | bytes 12320 | tf_op jit(solution)/shard_map/ppermute | solution.py:505
  35.1 2.4 %collective-permute-start.6 = (f32[24,128]{1,0:T(8,128)S(1)}, f32[24,128]{1,0:T(8,128)S(1)}, u32[]{:S(2)}, u32[]{:S(2)}) collective-permute-start(f32[24,128]{1,0:T(8,128)S(1)} %add.16), channel_id=1, source_target_pairs={{0,3},{1,2},{2,1},{3,0},{4,7},{5,6},{6,5},{7,4},{8,11},{9,10},{10,... | collective-permute-start | bytes 36872 | tf_op jit(solution)/shard_map/ppermute | solution.py:505
  37.5 1.4 %collective-permute-done.6 = f32[24,128]{1,0:T(8,128)S(1)} collective-permute-done((f32[24,128]{1,0:T(8,128)S(1)}, f32[24,128]{1,0:T(8,128)S(1)}, u32[]{:S(2)}, u32[]{:S(2)}) %collective-permute-start.6) | collective-permute-done | bytes 12320 | tf_op jit(solution)/shard_map/ppermute | solution.py:505
  38.9 2.6 %collective-permute-start.7 = (f32[24,128]{1,0:T(8,128)S(1)}, f32[24,128]{1,0:T(8,128)S(1)}, u32[]{:S(2)}, u32[]{:S(2)}) collective-permute-start(f32[24,128]{1,0:T(8,128)S(1)} %add.17), channel_id=1, source_target_pairs={{0,9},{1,8},{2,11},{3,10},{4,13},{5,12},{6,15},{7,14},{8,1},{9,0},... | collective-permute-start | bytes 36872 | tf_op jit(solution)/shard_map/ppermute | solution.py:505
  41.5 1.4 %collective-permute-done.7 = f32[24,128]{1,0:T(8,128)S(1)} collective-permute-done((f32[24,128]{1,0:T(8,128)S(1)}, f32[24,128]{1,0:T(8,128)S(1)}, u32[]{:S(2)}, u32[]{:S(2)}) %collective-permute-start.7) | collective-permute-done | bytes 12320 | tf_op jit(solution)/shard_map/ppermute | solution.py:505
  42.9 1.4 %collective-permute-start.8 = (f32[24,128]{1,0:T(8,128)S(1)}, f32[24,128]{1,0:T(8,128)S(1)}, u32[]{:S(2)}, u32[]{:S(2)}) collective-permute-start(f32[24,128]{1,0:T(8,128)S(1)} %add.18), channel_id=1, source_target_pairs={{0,5},{1,4},{2,7},{3,6},{4,1},{5,0},{6,3},{7,2},{8,13},{9,12},{10,... | collective-permute-start | bytes 36872 | tf_op jit(solution)/shard_map/ppermute | solution.py:505
  44.3 0.9 %shard_map.151 = (f32[8,128]{1,0:T(8,128)S(1)}, bf16[128,2048]{1,0:T(8,128)(2,1)S(1)}, f32[1088,128]{1,0:T(8,128)S(1)}) custom-call(f32[64,2048]{1,0:T(8,128)S(1)} %bitcast.6, f32[64,68]{1,0:T(8,128)S(1)} %get-tuple-element.33.refs_8_.dense_ref), custom_call_target="tpu_custom_call" | custom-call | flops 1000000 | bytes 2170880 | tf_op jit(solution)/shard_map/pallas_call | solution.py:596
  45.2 0.7 %shard_map.149 = f32[8,8,512]{2,1,0:T(8,128)} custom-call(f32[64,640]{1,0:T(8,128)S(1)} %get-tuple-element.36.previous, f32[64,640]{1,0:T(8,128)S(1)} %get-tuple-element.37.change, f32[24,128]{1,0:T(8,128)S(1)} %add.15._), custom_call_target="tpu_custom_call" | custom-call | flops 1000000 | bytes 262144 | tf_op jit(solution)/shard_map/pallas_call | solution.py:595
  45.9 0.2 collective-permute-done.8
  46.0 0.0 collective-permute-done.12.other_ref
  46.1 0.2 shard_map.150.base_ref
  46.3 1.3 %shard_map.152 = (f32[64,2048]{1,0:T(8,128)}, f32[64,68]{1,0:T(8,128)}, f32[64,64]{1,0:T(8,128)}, f32[1,1]{1,0:T(1,128)}) custom-call(f32[24,128]{1,0:T(8,128)S(1)} %add.19.pay_ref, f32[64,2048]{1,0:T(8,128)S(1)} %shard_map.150.base_ref, f32[64,68]{1,0:T(8,128)S(1)} %get-tuple-element.33.refs_8_.dense_ref, f32[64,64]{1,0:T(8,128)S(1)} %get-tuple-element.39.momentum_ref, ...), custom_call_target="tpu_custom_call" | custom-call | flops 1000000 | bytes 1116168 | tf_op jit(solution)/shard_map/pallas_call | solution.py:602
  (14 shorter events, 0.1 us)
Async XLA Ops:
  1.9 5.3 %collective-permute-start = (f32[128,128]{1,0:T(8,128)S(1)}, f32[128,128]{1,0:T(8,128)S(1)}, u32[]{:S(2)}, u32[]{:S(2)}) collective-permute-start(f32[128,128]{1,0:T(8,128)S(1)} %get-tuple-element.29), channel_id=1, source_target_pairs={{0,16},{1,17},{2,18},{3,19},{4,20},{5,21},{6,22},{7,23},{8,24},{9,... | collective-permute-start | bytes 196616 | tf_op jit(solution)/shard_map/ppermute | solution.py:497
  7.2 21.2 %copy-start = (f32[2048,64]{0,1:T(8,128)S(1)}, f32[2048,64]{0,1:T(8,128)}, u32[]{:S(2)}) copy-start(f32[2048,64]{0,1:T(8,128)} %param.17) | copy-start | bytes 1572868
  7.2 5.0 %collective-permute-start.9 = (f32[64,128]{1,0:T(8,128)S(1)}, f32[64,128]{1,0:T(8,128)S(1)}, u32[]{:S(2)}, u32[]{:S(2)}) collective-permute-start(f32[64,128]{1,0:T(8,128)S(1)} %pad_maximum_fusion.2), channel_id=1, source_target_pairs={{0,8},{1,9},{2,10},{3,11},{4,12},{5,13},{6,14},{7,15},{8,0},{9,1},... | collective-permute-start | bytes 98312 | tf_op jit(solution)/shard_map/ppermute | solution.py:497
  12.3 4.9 %collective-permute-start.10 = (f32[128,128]{1,0:T(8,128)S(1)}, f32[128,128]{1,0:T(8,128)S(1)}, u32[]{:S(2)}, u32[]{:S(2)}) collective-permute-start(f32[128,128]{1,0:T(8,128)S(1)} %pad_maximum_fusion.1), channel_id=1, source_target_pairs={{0,4},{1,3},{2,6},{3,1},{4,0},{5,7},{6,2},{7,5},{8,12},{9,11},{10,... | collective-permute-start | bytes 196616 | tf_op jit(solution)/shard_map/ppermute | solution.py:497
  17.2 5.0 %collective-permute-start.11 = (f32[256,128]{1,0:T(8,128)S(1)}, f32[256,128]{1,0:T(8,128)S(1)}, u32[]{:S(2)}, u32[]{:S(2)}) collective-permute-start(f32[256,128]{1,0:T(8,128)S(1)} %pad_maximum_fusion), channel_id=1, source_target_pairs={{0,2},{1,5},{2,0},{3,7},{4,6},{5,1},{6,4},{7,3},{8,10},{9,13},{10,... | collective-permute-start | bytes 393224 | tf_op jit(solution)/shard_map/ppermute | solution.py:497
  22.2 23.8 %collective-permute-start.12 = (f32[512,128]{1,0:T(8,128)S(1)}, f32[512,128]{1,0:T(8,128)S(1)}, u32[]{:S(2)}, u32[]{:S(2)}) collective-permute-start(f32[512,128]{1,0:T(8,128)S(1)} %constant_dynamic-update-slice_fusion.mine_ref), channel_id=1, source_target_pairs={{0,1},{1,0},{2,3},{3,2},{4,5},{5,4},{6,7},{7,6},{8,9},{9,8},{10,11... | collective-permute-start | bytes 786440 | tf_op jit(solution)/shard_map/ppermute | solution.py:497
  22.3 6.1 %collective-permute-start.1 = (f32[104,128]{1,0:T(8,128)S(1)}, f32[104,128]{1,0:T(8,128)S(1)}, u32[]{:S(2)}, u32[]{:S(2)}) collective-permute-start(f32[104,128]{1,0:T(8,128)S(1)} %shard_map.147), channel_id=1, source_target_pairs={{0,1},{1,0},{2,3},{3,2},{4,5},{5,4},{6,7},{7,6},{8,9},{9,8},{10,11... | collective-permute-start | bytes 159752 | tf_op jit(solution)/shard_map/ppermute | solution.py:497
  22.9 5.5 %collective-permute-start.2 = (f32[96,128]{1,0:T(8,128)S(1)}, f32[96,128]{1,0:T(8,128)S(1)}, u32[]{:S(2)}, u32[]{:S(2)}) collective-permute-start(f32[96,128]{1,0:T(8,128)S(1)} %get-tuple-element.31), channel_id=1, source_target_pairs={{0,16},{1,2},{2,1},{3,4},{4,3},{5,6},{6,5},{7,8},{8,7},{9,10},{10,... | collective-permute-start | bytes 147464 | tf_op jit(solution)/shard_map/ppermute | solution.py:497
  24.8 3.6 %collective-permute-start.3 = (f32[8,128]{1,0:T(8,128)S(1)}, f32[8,128]{1,0:T(8,128)S(1)}, u32[]{:S(2)}, u32[]{:S(2)}) collective-permute-start(f32[8,128]{1,0:T(8,128)S(1)} %get-tuple-element.32), channel_id=1, source_target_pairs={{0,16},{1,18},{2,17},{3,20},{4,19},{5,22},{6,21},{7,24},{8,23},{9,... | collective-permute-start | bytes 12296 | tf_op jit(solution)/shard_map/ppermute | solution.py:497
  30.7 1.3 %collective-permute-start.4 = (f32[24,128]{1,0:T(8,128)S(1)}, f32[24,128]{1,0:T(8,128)S(1)}, u32[]{:S(2)}, u32[]{:S(2)}) collective-permute-start(f32[24,128]{1,0:T(8,128)S(1)} %get-tuple-element.38), channel_id=1, source_target_pairs={{0,1},{1,0},{2,3},{3,2},{4,5},{5,4},{6,7},{7,6},{8,9},{9,8},{10,11... | collective-permute-start | bytes 36872 | tf_op jit(solution)/shard_map/ppermute | solution.py:505
  32.0 3.1 %collective-permute-start.5 = (f32[24,128]{1,0:T(8,128)S(1)}, f32[24,128]{1,0:T(8,128)S(1)}, u32[]{:S(2)}, u32[]{:S(2)}) collective-permute-start(f32[24,128]{1,0:T(8,128)S(1)} %add.15._), channel_id=1, source_target_pairs={{0,17},{1,16},{2,19},{3,18},{4,21},{5,20},{6,23},{7,22},{8,25},{9,... | collective-permute-start | bytes 36872 | tf_op jit(solution)/shard_map/ppermute | solution.py:505
  35.1 3.8 %collective-permute-start.6 = (f32[24,128]{1,0:T(8,128)S(1)}, f32[24,128]{1,0:T(8,128)S(1)}, u32[]{:S(2)}, u32[]{:S(2)}) collective-permute-start(f32[24,128]{1,0:T(8,128)S(1)} %add.16), channel_id=1, source_target_pairs={{0,3},{1,2},{2,1},{3,0},{4,7},{5,6},{6,5},{7,4},{8,11},{9,10},{10,... | collective-permute-start | bytes 36872 | tf_op jit(solution)/shard_map/ppermute | solution.py:505
  38.9 4.0 %collective-permute-start.7 = (f32[24,128]{1,0:T(8,128)S(1)}, f32[24,128]{1,0:T(8,128)S(1)}, u32[]{:S(2)}, u32[]{:S(2)}) collective-permute-start(f32[24,128]{1,0:T(8,128)S(1)} %add.17), channel_id=1, source_target_pairs={{0,9},{1,8},{2,11},{3,10},{4,13},{5,12},{6,15},{7,14},{8,1},{9,0},... | collective-permute-start | bytes 36872 | tf_op jit(solution)/shard_map/ppermute | solution.py:505
  42.9 3.1 %collective-permute-start.8 = (f32[24,128]{1,0:T(8,128)S(1)}, f32[24,128]{1,0:T(8,128)S(1)}, u32[]{:S(2)}, u32[]{:S(2)}) collective-permute-start(f32[24,128]{1,0:T(8,128)S(1)} %add.18), channel_id=1, source_target_pairs={{0,5},{1,4},{2,7},{3,6},{4,1},{5,0},{6,3},{7,2},{8,13},{9,12},{10,... | collective-permute-start | bytes 36872 | tf_op jit(solution)/shard_map/ppermute | solution.py:505
